TPU v7x, 32 devices: a whole 2x2x4 slice. The times are simulated.
32 devices in a mesh: grp: 2 (over x), seq: 16 (over z, y, core).
Axes of the slice: x: 2, y: 2, z: 4, core: 2. Of those that a mesh axis runs over, the one named last changes fastest.
Arguments:
- item_features: bfloat16 [4096, 1024], P(('grp', 'seq')), parts along dimension 0, may hold values from -6 to 6
- tower_in: bfloat16 [1024, 2048], replicated, may hold values from -0.1875 to 0.1875
- tower_out: bfloat16 [2048, 512], replicated, may hold values from -0.125 to 0.125
- proj_weight: bfloat16 [512, 2048], replicated, may hold values from -0.25 to 0.25
- out_weight: bfloat16 [512, 512], replicated, may hold values from -0.25 to 0.25
- hist_keys: bfloat16 [4, 16384, 512], P('grp', 'seq'), parts along dimension 0, may hold values from -6 to 6
- hist_values: bfloat16 [4, 16384, 512], P('grp', 'seq'), parts along dimension 0, may hold values from -6 to 6
- owner_of: int32 [512, 2, 1], P(('grp', 'seq')), parts along dimension 0, may hold values from 0 to 15; in each aligned block of 32 rows (0 to 31, 32 to 63, ..., all dimensions but the last counted through in order) at most 4 rows name the same one
- row_in: int32 [512, 2], P(('grp', 'seq')), parts along dimension 0, may hold values from 0 to 127
- hist_lengths: int32 [4], P('grp'), parts along dimension 0, may hold values from 4096 to 16384
- causal_offsets: int32 [512, 2], P('grp'), parts along dimension 0, may hold values from 0 to 1023
Outputs:
- item_embed: bfloat16 [4096, 512], P(('grp', 'seq')), parts along dimension 0
- cand_out: bfloat16 [512, 2, 512], P(('grp', 'seq')), parts along dimension 0
There are 2 independent parts, one for each index of `grp`. A program takes and returns all parts, laid end to end along the dimension named above; an argument that names none is the same for every part. Nothing has to cross between parts.
Inputs may be any that keep to these rules, and one draw needn't show every extreme that they name: `owner_of`: within the 32 slots of one device (candidate-major), no device number appears more than 4 times.
All inputs are finite; a program needn't handle non-finite values.
Results may differ from a plain program's by a relative error of at most 0.011.
Values may be sent and summed in bfloat16 or wider, within the bound.
No kernel may reach another device: no remote copies, remote signals or barrier semaphores. Data moves between devices by JAX's collectives and lax.ppermute only.
A program may use at most 128 MiB of HBM per device.

v0:
```python
import jax
import jax.numpy as jnp
from jax import lax
from jax.sharding import PartitionSpec as P

HEADS = 8


def layer_norm(values):
    centre = values - jnp.mean(values, axis=-1, keepdims=True)
    return centre * lax.rsqrt(jnp.mean(centre * centre, axis=-1, keepdims=True) + 1e-05)


def self_term(query, key, value):
    rows, width = query.shape
    size = width // HEADS
    q_heads = query.astype(jnp.float32).reshape(rows, HEADS, size)
    k_heads = key.astype(jnp.float32).reshape(rows, HEADS, size)
    v_heads = value.astype(jnp.float32).reshape(rows, HEADS, size)
    score = jnp.sum(q_heads * k_heads, axis=-1) * size ** (-0.5)
    return (jax.nn.silu(score)[:, :, None] * v_heads).reshape(rows, width)


def attend_block(query, keys, values, visible):
    rows, width = query.shape
    size = width // HEADS
    q_heads = query.reshape(rows, HEADS, size)
    k_heads = keys.reshape(keys.shape[0], HEADS, size)
    v_heads = values.reshape(values.shape[0], HEADS, size)
    scores = jnp.einsum(
        "chd,jhd->hcj", q_heads, k_heads, preferred_element_type=jnp.float32
    ) * size ** (-0.5)
    weights = jnp.where(visible[None], jax.nn.silu(scores), 0.0).astype(jnp.bfloat16)
    mixed = jnp.einsum("hcj,jhd->chd", weights, v_heads, preferred_element_type=jnp.float32)
    return mixed.reshape(rows, width)


def slot_ranks(owners, devices):
    onehot = (owners[:, None] == jnp.arange(devices, dtype=jnp.int32)[None, :]).astype(jnp.int32)
    before = jnp.cumsum(onehot, axis=0) - onehot
    return jnp.sum(before * onehot, axis=1)


def per_device(
    item_features,
    tower_in,
    tower_out,
    proj_weight,
    out_weight,
    hist_keys,
    hist_values,
    owner_of,
    row_in,
    hist_lengths,
    causal_offsets,
):
    width = tower_out.shape[1]
    hidden = jax.nn.silu(
        jnp.dot(item_features, tower_in, preferred_element_type=jnp.float32)
    ).astype(jnp.bfloat16)
    item_embed = jnp.dot(hidden, tower_out, preferred_element_type=jnp.float32).astype(jnp.bfloat16)
    devices = lax.axis_size("seq")
    rank_me = lax.axis_index("seq")
    slot_count, users = row_in.shape
    slots = slot_count * users
    depth = max(2, 2 * slots // devices)
    owners = owner_of.reshape(slots)
    rows_local = row_in.reshape(slots)
    peers = jnp.arange(devices, dtype=jnp.int32)
    levels = jnp.arange(depth, dtype=jnp.int32)
    ranks = slot_ranks(owners, devices)
    select = (owners[None, None, :] == peers[:, None, None]) & (
        ranks[None, None, :] == levels[None, :, None]
    )
    requests = jnp.sum(jnp.where(select, rows_local[None, None, :], 0), axis=2)
    returned_rows = lax.all_to_all(
        jnp.take(
            item_embed,
            lax.all_to_all(requests, "seq", split_axis=0, concat_axis=0, tiled=True),
            axis=0,
        ),
        "seq",
        split_axis=0,
        concat_axis=0,
        tiled=True,
    )
    routed = jnp.einsum(
        "nks,nkd->sd",
        select.astype(jnp.bfloat16),
        returned_rows,
        preferred_element_type=jnp.float32,
    ).astype(jnp.bfloat16)
    proj = jax.nn.silu(jnp.dot(routed, proj_weight, preferred_element_type=jnp.float32))
    gate = proj[:, :width]
    value = proj[:, width : 2 * width].astype(jnp.bfloat16)
    query = proj[:, 2 * width : 3 * width].astype(jnp.bfloat16)
    key = proj[:, 3 * width :].astype(jnp.bfloat16)
    query_grid = query.reshape(slot_count, users, width)
    hist_dev = hist_keys.shape[1]
    group = devices // users
    share = hist_dev * users // devices
    user_me = rank_me // group
    member = rank_me % group
    moved_keys, moved_values = (
        lax.all_to_all(
            hist_keys.reshape(devices, share, width), "seq", split_axis=0, concat_axis=0, tiled=True
        ),
        lax.all_to_all(
            hist_values.reshape(devices, share, width),
            "seq",
            split_axis=0,
            concat_axis=0,
            tiled=True,
        ),
    )
    copies = jnp.broadcast_to(
        query_grid.transpose(1, 0, 2)[:, None], (users, group, slot_count, width)
    ).reshape(devices, slot_count, width)
    user_queries = lax.all_to_all(copies, "seq", split_axis=0, concat_axis=0, tiled=True).reshape(
        devices * slot_count, width
    )
    limit = (
        lax.dynamic_slice_in_dim(hist_lengths, user_me, 1, 0)
        - lax.dynamic_slice_in_dim(causal_offsets, user_me, 1, 1)[:, 0]
    )
    event_pos = (
        peers[:, None] * hist_dev + member * share + jnp.arange(share, dtype=jnp.int32)[None, :]
    ).reshape(-1)
    visible = event_pos[None, :] < limit[:, None]
    user_part = attend_block(
        user_queries, moved_keys.reshape(-1, width), moved_values.reshape(-1, width), visible
    )
    backs = lax.all_to_all(
        user_part.reshape(devices, slot_count, width).astype(jnp.bfloat16),
        "seq",
        split_axis=0,
        concat_axis=0,
        tiled=True,
    ).astype(jnp.float32)
    attended = jnp.sum(backs.reshape(users, group, slot_count, width), axis=1).transpose(1, 0, 2)
    own = self_term(query, key, value)
    total = attended.reshape(slots, width) + own
    mixed = (layer_norm(total) * gate).astype(jnp.bfloat16)
    result = routed.astype(jnp.float32) + jnp.dot(
        mixed, out_weight, preferred_element_type=jnp.float32
    )
    return (item_embed, result.astype(jnp.bfloat16).reshape(slot_count, users, width))


def solution(mesh):
    return jax.shard_map(
        per_device,
        mesh=mesh,
        in_specs=(
            P(("grp", "seq"), None),
            P(),
            P(),
            P(),
            P(),
            P("grp", "seq", None),
            P("grp", "seq", None),
            P(("grp", "seq"), None, None),
            P(("grp", "seq"), None),
            P("grp"),
            P("grp", None),
        ),
        out_specs=(P(("grp", "seq"), None), P(("grp", "seq"), None, None)),
        check_vma=False,
    )
```

profile of v0, /device:TPU:0, one launch (start us, length us, event | category | flops | bytes accessed | tf_op | source)
XLA Modules:
  0.0 187.0 jit_solution(17393624436280311442)
XLA Ops:
  0.6 0.9 copy.75
  1.7 0.8 copy.76
  3.0 0.7 copy.77
  3.7 7.4 %all-to-all-start = ((s32[16,1,4]{2,1,0:T(1,128)}), s32[16,1,4]{2,1,0:T(1,128)S(1)}, u32[]{:S(2)}, u32[]{:S(2)}) async-start(s32[16,1,4]{2,1,0:T(1,128)} %copy.77), calls=%async_computation | async-start | bytes 16384 | tf_op jit(solution)/shard_map/all_to_all | solution.py:79
  11.1 4.0 %convolution_convert_fusion = bf16[128,512]{1,0:T(8,128)(2,1)S(1)} fusion(bf16[2048,512]{1,0:T(8,128)(2,1)} %param.13, bf16[128,1024]{1,0:T(8,128)(2,1)} %param.11, bf16[1024,2048]{1,0:T(8,128)(2,1)} %param.12), kind=kOutput, calls=%fused_computation.6 | convolution fusion | flops 806682624 | bytes 6684672 | tf_op jit(solution)/shard_map/dot_general | solution.py:61
  15.1 2.4 %all-to-all-done = s32[16,1,4]{2,1,0:T(1,128)S(1)} async-done(((s32[16,1,4]{2,1,0:T(1,128)}), s32[16,1,4]{2,1,0:T(1,128)S(1)}, u32[]{:S(2)}, u32[]{:S(2)}) %all-to-all-start) | async-done | bytes 288 | tf_op jit(solution)/shard_map/all_to_all | solution.py:79
  17.7 0.7 gather_fusion
  18.7 10.3 %all_to_all.40 = bf16[16,4,512]{2,1,0:T(4,128)(2,1)S(1)} all-to-all(bf16[16,4,512]{2,1,0:T(4,128)(2,1)S(1)} %broadcast_select_fusion), channel_id=1, replica_groups=mesh['grp'=2,'seq'=16] {'seq'}, dimensions={0} | all-to-all | bytes 131072 | tf_op jit(solution)/shard_map/all_to_all | solution.py:76
  29.2 1.2 fusion.25
  30.5 0.7 broadcast_in_dim.59
  31.2 3.5 %all-to-all-start.2 = ((bf16[16,16,512]{2,1,0:T(8,128)(2,1)}), bf16[16,16,512]{2,1,0:T(8,128)(2,1)S(1)}, u32[]{:S(2)}, u32[]{:S(2)}) async-start(bf16[16,16,512]{2,1,0:T(8,128)(2,1)} %bitcast.8), calls=%async_computation.2 | async-start | bytes 524288 | tf_op jit(solution)/shard_map/all_to_all | solution.py:119
  34.7 3.9 %copy.87 = bf16[16,128,512]{1,2,0:T(8,128)(2,1)} copy(bf16[16,128,512]{2,1,0:T(8,128)(2,1)} %bitcast.41) | data formatting | bytes 4194304 | tf_op jit(solution)/shard_map/reshape | solution.py:109
  38.7 6.0 %all-to-all-done.2 = bf16[16,16,512]{2,1,0:T(8,128)(2,1)S(1)} async-done(((bf16[16,16,512]{2,1,0:T(8,128)(2,1)}), bf16[16,16,512]{2,1,0:T(8,128)(2,1)S(1)}, u32[]{:S(2)}, u32[]{:S(2)}) %all-to-all-start.2) | async-done | bytes 262176 | tf_op jit(solution)/shard_map/all_to_all | solution.py:119
  44.7 4.4 %all-to-all-start.4 = ((bf16[16,128,512]{1,2,0:T(8,128)(2,1)}), bf16[16,128,512]{1,2,0:T(8,128)(2,1)}, u32[]{:S(2)}, u32[]{:S(2)}) async-start(bf16[16,128,512]{1,2,0:T(8,128)(2,1)} %copy.87), calls=%async_computation.4 | async-start | bytes 4194304 | tf_op jit(solution)/shard_map/all_to_all | solution.py:108
  49.1 3.9 %copy.84 = bf16[16,128,512]{1,2,0:T(8,128)(2,1)} copy(bf16[16,128,512]{2,1,0:T(8,128)(2,1)} %bitcast.42) | data formatting | bytes 4194304 | tf_op jit(solution)/shard_map/reshape | solution.py:106
  53.1 37.0 %all-to-all-done.4 = bf16[16,128,512]{1,2,0:T(8,128)(2,1)} async-done(((bf16[16,128,512]{1,2,0:T(8,128)(2,1)}), bf16[16,128,512]{1,2,0:T(8,128)(2,1)}, u32[]{:S(2)}, u32[]{:S(2)}) %all-to-all-start.4) | async-done | bytes 2097184 | tf_op jit(solution)/shard_map/all_to_all | solution.py:108
  90.1 11.3 %all-to-all-start.3 = ((bf16[16,128,512]{1,2,0:T(8,128)(2,1)}), bf16[16,128,512]{1,2,0:T(8,128)(2,1)}, u32[]{:S(2)}, u32[]{:S(2)}) async-start(bf16[16,128,512]{1,2,0:T(8,128)(2,1)} %copy.84), calls=%async_computation.3 | async-start | bytes 4194304 | tf_op jit(solution)/shard_map/all_to_all | solution.py:105
  101.4 0.6 dynamic_slice.6
  102.0 0.7 dynamic-slice_subtract_fusion
  102.7 1.2 broadcast_compare_fusion
  104.2 4.3 %copy.88 = bf16[16,128,512]{1,0,2:T(8,128)(2,1)} copy(bf16[16,128,512]{1,2,0:T(8,128)(2,1)} %all-to-all-done.4) | data formatting | bytes 4194304 | tf_op jit(solution)/shard_map/all_to_all | solution.py:108
  108.5 4.2 %reshape_reshape.12 = bf16[2048,8,64]{0,2,1:T(8,128)(2,1)} reshape(bf16[16,128,512]{1,0,2:T(8,128)(2,1)} %copy.88) | data formatting | bytes 4194304 | tf_op jit(solution)/shard_map/reshape;reshape | solution.py:29
  112.7 29.7 %all-to-all-done.3 = bf16[16,128,512]{1,2,0:T(8,128)(2,1)} async-done(((bf16[16,128,512]{1,2,0:T(8,128)(2,1)}), bf16[16,128,512]{1,2,0:T(8,128)(2,1)}, u32[]{:S(2)}, u32[]{:S(2)}) %all-to-all-start.3) | async-done | bytes 2097184 | tf_op jit(solution)/shard_map/all_to_all | solution.py:105
  142.4 4.3 %copy.85 = bf16[16,128,512]{1,0,2:T(8,128)(2,1)} copy(bf16[16,128,512]{1,2,0:T(8,128)(2,1)} %all-to-all-done.3) | data formatting | bytes 4194304 | tf_op jit(solution)/shard_map/all_to_all | solution.py:105
  146.7 4.2 %reshape_reshape.11 = bf16[2048,8,64]{0,2,1:T(8,128)(2,1)} reshape(bf16[16,128,512]{1,0,2:T(8,128)(2,1)} %copy.85) | data formatting | bytes 4194304 | tf_op jit(solution)/shard_map/reshape;reshape | solution.py:28
  150.9 10.4 %fusion.4 = bf16[256,8,64]{0,2,1:T(8,128)(2,1)} fusion(bf16[2048,8,64]{0,2,1:T(8,128)(2,1)} %reshape_reshape.12, pred[256,2048]{1,0:T(8,128)(4,1)S(1)} %copy-done.3, bf16[2048,8,64]{0,2,1:T(8,128)(2,1)} %reshape_reshape.11, bf16[256,8,64]{2,1,0:T(8,128)(2,1)S(1)} %reshape_reshape.10), kind=kOutput, calls=%fused_computation.5 | convolution fusion | flops 1103233024 | bytes 5242880 | tf_op jit(solution)/shard_map/hcj,jhd->chd/dot_general | solution.py:34
  161.2 1.3 copy.89
  162.6 1.0 convert_element_type.55
  163.6 11.2 %all-to-all-start.5 = ((bf16[16,16,512]{2,1,0:T(8,128)(2,1)}), bf16[16,16,512]{2,1,0:T(8,128)(2,1)S(1)}, u32[]{:S(2)}, u32[]{:S(2)}) async-start(bf16[16,16,512]{2,1,0:T(8,128)(2,1)} %convert_element_type.55), calls=%async_computation.5 | async-start | bytes 524288 | tf_op jit(solution)/shard_map/all_to_all | solution.py:133
  175.4 9.4 %all-to-all-done.5 = bf16[16,16,512]{2,1,0:T(8,128)(2,1)S(1)} async-done(((bf16[16,16,512]{2,1,0:T(8,128)(2,1)}), bf16[16,16,512]{2,1,0:T(8,128)(2,1)S(1)}, u32[]{:S(2)}, u32[]{:S(2)}) %all-to-all-start.5) | async-done | bytes 262176 | tf_op jit(solution)/shard_map/all_to_all | solution.py:133
  185.3 1.1 fusion.6
  186.4 0.7 reshape.199
  (51 shorter events, 2.8 us)
Async XLA Ops:
  0.6 28.6 %copy-start = (bf16[512,2048]{1,0:T(8,128)(2,1)S(1)}, bf16[512,2048]{1,0:T(8,128)(2,1)}, u32[]{:S(2)}) copy-start(bf16[512,2048]{1,0:T(8,128)(2,1)} %param.14) | copy-start | bytes 6291460
  3.7 13.8 %all-to-all-start = ((s32[16,1,4]{2,1,0:T(1,128)}), s32[16,1,4]{2,1,0:T(1,128)S(1)}, u32[]{:S(2)}, u32[]{:S(2)}) async-start(s32[16,1,4]{2,1,0:T(1,128)} %copy.77), calls=%async_computation | async-start | bytes 16384 | tf_op jit(solution)/shard_map/all_to_all | solution.py:79
  15.1 16.1 %copy-start.1 = (bf16[128,512]{1,0:T(8,128)(2,1)}, bf16[128,512]{1,0:T(8,128)(2,1)S(1)}, u32[]{:S(2)}) copy-start(bf16[128,512]{1,0:T(8,128)(2,1)S(1)} %convolution_convert_fusion) | copy-start | bytes 393220
  31.2 13.5 %all-to-all-start.2 = ((bf16[16,16,512]{2,1,0:T(8,128)(2,1)}), bf16[16,16,512]{2,1,0:T(8,128)(2,1)S(1)}, u32[]{:S(2)}, u32[]{:S(2)}) async-start(bf16[16,16,512]{2,1,0:T(8,128)(2,1)} %bitcast.8), calls=%async_computation.2 | async-start | bytes 524288 | tf_op jit(solution)/shard_map/all_to_all | solution.py:119
  44.7 45.4 %all-to-all-start.4 = ((bf16[16,128,512]{1,2,0:T(8,128)(2,1)}), bf16[16,128,512]{1,2,0:T(8,128)(2,1)}, u32[]{:S(2)}, u32[]{:S(2)}) async-start(bf16[16,128,512]{1,2,0:T(8,128)(2,1)} %copy.87), calls=%async_computation.4 | async-start | bytes 4194304 | tf_op jit(solution)/shard_map/all_to_all | solution.py:108
  53.1 48.3 %copy-start.5 = (s32[2]{0:T(128)S(1)}, s32[2]{0:T(128)}, u32[]{:S(2)}) copy-start(s32[2]{0:T(128)} %param.20) | copy-start | bytes 28
  53.1 48.9 %copy-start.4 = (s32[256,2]{0,1:T(2,128)S(1)}, s32[256,2]{0,1:T(2,128)}, u32[]{:S(2)}) copy-start(s32[256,2]{0,1:T(2,128)} %param.21) | copy-start | bytes 6148
  90.1 52.3 %all-to-all-start.3 = ((bf16[16,128,512]{1,2,0:T(8,128)(2,1)}), bf16[16,128,512]{1,2,0:T(8,128)(2,1)}, u32[]{:S(2)}, u32[]{:S(2)}) async-start(bf16[16,128,512]{1,2,0:T(8,128)(2,1)} %copy.84), calls=%async_computation.3 | async-start | bytes 4194304 | tf_op jit(solution)/shard_map/all_to_all | solution.py:105
  146.6 4.2 %copy-start.3 = (pred[256,2048]{1,0:T(8,128)(4,1)S(1)}, pred[256,2048]{1,0:T(8,128)(4,1)}, u32[]{:S(2)}) copy-start(pred[256,2048]{1,0:T(8,128)(4,1)} %broadcast_compare_fusion) | copy-start | bytes 1572868
  161.2 24.1 %copy-start.2 = (bf16[512,512]{1,0:T(8,128)(2,1)S(1)}, bf16[512,512]{1,0:T(8,128)(2,1)}, u32[]{:S(2)}) copy-start(bf16[512,512]{1,0:T(8,128)(2,1)} %param.15) | copy-start | bytes 1572868
  163.6 21.2 %all-to-all-start.5 = ((bf16[16,16,512]{2,1,0:T(8,128)(2,1)}), bf16[16,16,512]{2,1,0:T(8,128)(2,1)S(1)}, u32[]{:S(2)}, u32[]{:S(2)}) async-start(bf16[16,16,512]{2,1,0:T(8,128)(2,1)} %convert_element_type.55), calls=%async_computation.5 | async-start | bytes 524288 | tf_op jit(solution)/shard_map/all_to_all | solution.py:133
where the time goes:
time: 188 us; the launch traced here: 187 us
  waiting for transfers between devices  84.6 us (45%)
  starting transfers between devices  37.8 us (20%)
  local copies, waits for them, and re-layouts  33.6 us (18%)
  matrix products  16.8 us (9%)
  blocking collectives  10.3 us (5%)
  other arithmetic  3.03 us (2%)
    all_to_all x1, waiting for transfers between devices, per_device(): lax.all_to_all(hist_values.reshape(devices, share, width), 'seq', split_a...  37 us
    all_to_all x1, waiting for transfers between devices, per_device(): lax.all_to_all(hist_keys.reshape(devices, share, width), 'seq', split_axi...  29.7 us
    all_to_all x1, starting transfers between devices, per_device(): lax.all_to_all(hist_keys.reshape(devices, share, width), 'seq', split_axi...  11.3 us
    all_to_all x1, starting transfers between devices, per_device(): lax.all_to_all(user_part.reshape(devices, slot_count, width).astype(jnp.b...  11.2 us
    dot_general x1, matrix products, attend_block(): jnp.einsum('hcj,jhd->chd', weights, v_heads, preferred_element_type=jnp.f...  10.4 us
    all_to_all x1, blocking collectives, per_device(): lax.all_to_all(jnp.take(item_embed, lax.all_to_all(requests, 'seq', split...  10.3 us
    all_to_all x1, waiting for transfers between devices, per_device(): lax.all_to_all(user_part.reshape(devices, slot_count, width).astype(jnp.b...  9.43 us
    all_to_all x1, starting transfers between devices, per_device(): lax.all_to_all(requests, 'seq', split_axis=0, concat_axis=0, tiled=True)  7.41 us
  transfers between devices with their start and end apart: 5, of which 5 were waited for; matrix products, arithmetic and copies ran while one was open for 13% of the time, Pallas kernels for 0%

commit v1 on v0

v1 whole, which is shorter than its diff:
```python
import functools

import jax
import jax.numpy as jnp
from jax import lax
from jax.experimental import pallas as pl
from jax.experimental.pallas import tpu as pltpu
from jax.sharding import PartitionSpec as P

HEADS = 8
LANES = 128


def layer_norm(values):
    centre = values - jnp.mean(values, axis=-1, keepdims=True)
    return centre * lax.rsqrt(jnp.mean(centre * centre, axis=-1, keepdims=True) + 1e-05)


def self_term(query, key, value):
    rows, width = query.shape
    size = width // HEADS
    q_heads = query.astype(jnp.float32).reshape(rows, HEADS, size)
    k_heads = key.astype(jnp.float32).reshape(rows, HEADS, size)
    v_heads = value.astype(jnp.float32).reshape(rows, HEADS, size)
    score = jnp.sum(q_heads * k_heads, axis=-1) * size ** (-0.5)
    return (jax.nn.silu(score)[:, :, None] * v_heads).reshape(rows, width)


def attend_kernel(routed_ref, weight_ref, first_ref, second_ref, keys_a, values_a, keys_b, values_b, out_ref):
    rows, width = routed_ref.shape
    size = width // HEADS
    query = jax.nn.silu(
        jnp.dot(routed_ref[...], weight_ref[...], preferred_element_type=jnp.float32)
    ).astype(jnp.bfloat16)
    query = query * jnp.bfloat16(0.5 * size ** (-0.5))
    lane = lax.broadcasted_iota(jnp.int32, (rows, LANES), 1)
    per_tile = LANES // size
    for tile in range(width // LANES):
        span = slice(tile * LANES, (tile + 1) * LANES)
        whole = query[:, span]
        joined = None
        for head in range(per_tile):
            mine = (lane >= head * size) & (lane < (head + 1) * size)
            part = jnp.where(mine, whole, jnp.zeros_like(whole))
            total = None
            for keys, values, seen in ((keys_a, values_a, first_ref), (keys_b, values_b, second_ref)):
                half = lax.dot_general(
                    part, keys[:, span], (((1,), (1,)), ((), ())), preferred_element_type=jnp.float32
                ).astype(jnp.bfloat16)
                weight = half + half * jnp.tanh(half)
                event = lax.broadcasted_iota(jnp.int32, weight.shape, 1)
                weight = jnp.where(event < seen[...], weight, jnp.zeros_like(weight))
                mixed = jnp.dot(weight, values[:, span], preferred_element_type=jnp.float32)
                total = mixed if total is None else total + mixed
            joined = total if joined is None else jnp.where(mine, total, joined)
        out_ref[:, span] = joined.astype(out_ref.dtype)


def attend(routed, weight, first, second, keys_a, values_a, keys_b, values_b):
    rows, width = routed.shape
    in_vmem = pl.BlockSpec(memory_space=pltpu.VMEM)
    return pl.pallas_call(
        attend_kernel,
        out_shape=jax.ShapeDtypeStruct((rows, width), jnp.bfloat16),
        in_specs=[in_vmem] * 8,
        out_specs=in_vmem,
        compiler_params=pltpu.CompilerParams(vmem_limit_bytes=40 * 2**20),
        name="attend",
    )(routed, weight, first, second, keys_a, values_a, keys_b, values_b)


def per_device(
    item_features,
    tower_in,
    tower_out,
    proj_weight,
    out_weight,
    hist_keys,
    hist_values,
    owner_of,
    row_in,
    hist_lengths,
    causal_offsets,
):
    width = tower_out.shape[1]
    devices = lax.axis_size("seq")
    me = lax.axis_index("seq")
    slot_count, users = row_in.shape
    assert users == 2 and devices % users == 0
    slots = slot_count * users
    rows = item_features.shape[0]
    hist_dev = hist_keys.shape[1]
    depth = max(2, 2 * slots // devices)
    room = devices * depth
    core = me % users
    partner = me + 1 - 2 * core
    swap = [(i, i ^ 1) for i in range(devices)]
    alike = [[b + users * k for k in range(devices // users)] for b in range(users)]

    owners = owner_of.reshape(slots)
    order = jnp.arange(slots, dtype=jnp.int32)
    earlier = (owners[:, None] == owners[None, :]) & (order[None, :] < order[:, None])
    ranks = jnp.sum(earlier.astype(jnp.int32), axis=1)
    code = (owners * depth + ranks) * rows + row_in.reshape(slots)
    codes = lax.all_to_all(
        jnp.broadcast_to(code[None], (devices, slots)), "seq", split_axis=0, concat_axis=0, tiled=True
    )

    def of_user(array, user, axis=0):
        return lax.dynamic_index_in_dim(array, user, axis, keepdims=False)

    keys_b = lax.ppermute(of_user(hist_keys, 1 - core), "seq", swap)
    values_b = lax.ppermute(of_user(hist_values, 1 - core), "seq", swap)
    keys_a = of_user(hist_keys, core)
    values_a = of_user(hist_values, core)

    hidden = jax.nn.silu(
        jnp.dot(item_features, tower_in, preferred_element_type=jnp.float32)
    ).astype(jnp.bfloat16)
    item_embed = jnp.dot(hidden, tower_out, preferred_element_type=jnp.float32).astype(jnp.bfloat16)

    places = codes // rows
    want = me * depth + jnp.arange(depth, dtype=jnp.int32)
    hit = places[:, None, :] == want[None, :, None]
    asked = jnp.sum(jnp.where(hit, (codes % rows)[:, None, :], 0), axis=2).reshape(room)
    picked = jnp.dot(
        (asked[:, None] == jnp.arange(rows, dtype=jnp.int32)[None, :]).astype(jnp.bfloat16),
        item_embed,
        preferred_element_type=jnp.float32,
    ).astype(jnp.bfloat16)
    gathered = lax.all_to_all(
        jnp.broadcast_to(picked[None], (devices // users, room, width)),
        "seq",
        split_axis=0,
        concat_axis=0,
        tiled=True,
        axis_index_groups=alike,
    ).reshape(devices // users * room, width)

    asker = jnp.arange(devices, dtype=jnp.int32)[:, None]
    owner = places // depth
    spot = jnp.where(
        owner % users == core, (owner // users) * room + asker * depth + places % depth, -1
    ).reshape(devices, slot_count, users)
    spot_mine = of_user(spot, core, 2)
    spot_other = of_user(spot, 1 - core, 2)

    def pick(spots):
        chosen = (
            spots[:, None] == jnp.arange(devices // users * room, dtype=jnp.int32)[None, :]
        ).astype(jnp.bfloat16)
        return jnp.dot(chosen, gathered, preferred_element_type=jnp.float32).astype(jnp.bfloat16)

    cands = devices * slot_count
    sent = pick(jnp.concatenate([spot_other.reshape(cands), of_user(spot_mine, partner)]))
    kept = pick(jnp.concatenate([spot_mine.reshape(cands), of_user(spot_other, me)]))
    routed = kept + lax.ppermute(sent, "seq", swap)
    routed_user = routed[:cands]
    own_mine = lax.dynamic_slice_in_dim(routed_user, me * slot_count, slot_count, 0)
    own_other = routed[cands:]
    routed_own = jnp.where(
        core == 0,
        jnp.concatenate([own_mine, own_other]),
        jnp.concatenate([own_other, own_mine]),
    )

    limit = (of_user(hist_lengths, core) - of_user(causal_offsets, core, 1))[:, None]
    user_part = attend(
        routed_user,
        proj_weight[:, 2 * width : 3 * width],
        limit - me * hist_dev,
        limit - partner * hist_dev,
        keys_a,
        values_a,
        keys_b,
        values_b,
    )
    routed_own, user_part = lax.optimization_barrier((routed_own, user_part))
    backs = lax.all_to_all(
        user_part.reshape(devices, slot_count, width), "seq", split_axis=0, concat_axis=0, tiled=True
    )

    proj = jax.nn.silu(jnp.dot(routed_own, proj_weight, preferred_element_type=jnp.float32))
    gate = proj[:, :width]
    value = proj[:, width : 2 * width].astype(jnp.bfloat16)
    query = proj[:, 2 * width : 3 * width].astype(jnp.bfloat16)
    key = proj[:, 3 * width :].astype(jnp.bfloat16)
    own = self_term(query, key, value)

    attended = jnp.sum(
        backs.astype(jnp.float32).reshape(devices // users, slots, width), axis=0
    )
    mixed = (layer_norm(attended + own) * gate).astype(jnp.bfloat16)
    result = routed_own.astype(jnp.float32) + jnp.dot(
        mixed, out_weight, preferred_element_type=jnp.float32
    )
    cand_out = result.astype(jnp.bfloat16).reshape(users, slot_count, width).transpose(1, 0, 2)
    return (item_embed, cand_out)


def solution(mesh):
    return jax.shard_map(
        per_device,
        mesh=mesh,
        in_specs=(
            P(("grp", "seq"), None),
            P(),
            P(),
            P(),
            P(),
            P("grp", "seq", None),
            P("grp", "seq", None),
            P(("grp", "seq"), None, None),
            P(("grp", "seq"), None),
            P("grp"),
            P("grp", None),
        ),
        out_specs=(P(("grp", "seq"), None), P(("grp", "seq"), None, None)),
        check_vma=False,
    )
```

time: 188 us -> 66.4 us (0.35)
  waiting for transfers between devices: 84.6 us -> 17.4 us
  starting transfers between devices: 37.8 us -> 15.8 us
  local copies, waits for them, and re-layouts: 33.6 us -> 12.7 us
  blocking collectives: 10.3 us -> 0 us
  Pallas kernels: 0 us -> 7.7 us
  matrix products: 16.8 us -> 9.45 us
    all_to_all x5 -> x3, waiting for transfers between devices: 84.6 us -> 16.3 us  [the longest x1 7.27 us: per_device(): lax.all_to_all(user_part.reshape(devices, slot_count, width), 'seq', spli...]
    all_to_all x5 -> x3, starting transfers between devices: 37.8 us -> 15.3 us  [the longest x1 7.41 us: per_device(): lax.all_to_all(jnp.broadcast_to(code[None], (devices, slots)), 'seq', spl...]
    all_to_all x1 -> x0, blocking collectives: 10.3 us -> none  [per_device(): lax.all_to_all(jnp.take(item_embed, lax.all_to_all(requests, 'seq', split...]
    all_to_all x4 -> x1, local copies, waits for them, and re-layouts: 9.33 us -> 0.07 us  [per_device(): lax.all_to_all(jnp.broadcast_to(code[None], (devices, slots)), 'seq', spl...]
    another operation x3 -> x0, local copies, waits for them, and re-layouts: 8.67 us -> none  [the longest x1 4.23 us: attend_block(): k_heads = keys.reshape(keys.shape[0], HEADS, size)]
    pallas_call x0 -> x1, Pallas kernels: none -> 7.7 us  [attend(): pl.pallas_call(attend_kernel, out_shape=jax.ShapeDtypeStruct((rows, width...]
    reshape x5, local copies, waits for them, and re-layouts: 8.58 us -> 1 us  [the longest x1 0.67 us: per_device(): result.astype(jnp.bfloat16).reshape(users, slot_count, width)]
    dot_general x3 -> x4, matrix products: 11.8 us -> 5.93 us  [the longest x2 3.58 us: pick(): jnp.dot(chosen, gathered, preferred_element_type=jnp.float32)]
  transfers between devices with their start and end apart: 5 -> 6, of which waited for: 5 -> 4; matrix products, arithmetic and copies ran while one was open for 13% -> 28% of each run, Pallas kernels for 0% -> 0%
where the time goes in v1:
time: 66.4 us; the launch traced here: 65.8 us
  waiting for transfers between devices  17.4 us (26%)
  starting transfers between devices  15.8 us (24%)
  local copies, waits for them, and re-layouts  12.7 us (19%)
  matrix products  9.45 us (14%)
  Pallas kernels  7.7 us (12%)
  other arithmetic  1.81 us (3%)
  between operations  0.96 us (1%)
    pallas_call x1, Pallas kernels, attend(): pl.pallas_call(attend_kernel, out_shape=jax.ShapeDtypeStruct((rows, width...  7.7 us
    all_to_all x1, starting transfers between devices, per_device(): lax.all_to_all(jnp.broadcast_to(code[None], (devices, slots)), 'seq', spl...  7.41 us
    all_to_all x1, waiting for transfers between devices, per_device(): lax.all_to_all(user_part.reshape(devices, slot_count, width), 'seq', spli...  7.27 us
    all_to_all x1, waiting for transfers between devices, per_device(): lax.all_to_all(jnp.broadcast_to(picked[None], (devices // users, room, wi...  6.06 us
    squeeze x2, local copies, waits for them, and re-layouts, of_user(): return lax.dynamic_index_in_dim(array, user, axis, keepdims=False)  4.32 us
    all_to_all x1, starting transfers between devices, per_device(): lax.all_to_all(jnp.broadcast_to(picked[None], (devices // users, room, wi...  4.15 us
    all_to_all x1, starting transfers between devices, per_device(): lax.all_to_all(user_part.reshape(devices, slot_count, width), 'seq', spli...  3.72 us
    dot_general x2, matrix products, pick(): jnp.dot(chosen, gathered, preferred_element_type=jnp.float32)  3.58 us
  transfers between devices with their start and end apart: 6, of which 4 were waited for; matrix products, arithmetic and copies ran while one was open for 28% of the time, Pallas kernels for 0%

profile of v1, /device:TPU:0, one launch (start us, length us, event | category | flops | bytes accessed | tf_op | source)
XLA Modules:
  0.0 65.8 jit_solution(7655958740034254393)
XLA Ops:
  0.6 0.9 %copy.56 = s32[16,2,1]{1,0,2:T(8,128)S(1)} copy(s32[16,2,1]{0,2,1:T(1,128)} %param.18) | data formatting | bytes 256 | tf_op args[7]
  1.6 0.2 convert_reduce_fusion.1
  1.8 0.8 %copy.57 = s32[16,2]{1,0:T(8,128)S(1)} copy(s32[16,2]{0,1:T(2,128)} %param.19) | data formatting | bytes 256 | tf_op args[8]
  2.7 0.6 broadcast_in_dim.19
  3.3 7.4 %all-to-all-start = ((s32[16,1,32]{2,1,0:T(1,128)}), s32[16,1,32]{2,1,0:T(1,128)S(1)}, u32[]{:S(2)}, u32[]{:S(2)}) async-start(s32[16,1,32]{2,1,0:T(1,128)} %broadcast_in_dim.19), calls=%async_computation | async-start | bytes 16384 | tf_op jit(solution)/shard_map/all_to_all | solution.py:105
  10.7 3.3 %convolution_convert_fusion.2 = bf16[128,512]{1,0:T(8,128)(2,1)S(1)} fusion(bf16[2048,512]{1,0:T(8,128)(2,1)S(1)} %copy-done, bf16[128,1024]{1,0:T(8,128)(2,1)} %param.11, bf16[1024,2048]{1,0:T(8,128)(2,1)} %param.12), kind=kOutput, calls=%fused_computation.3 | convolution fusion | flops 806682624 | bytes 6684672 | tf_op jit(solution)/shard_map/dot_general | solution.py:120
  14.1 3.0 %all-to-all-done = s32[16,1,32]{2,1,0:T(1,128)S(1)} async-done(((s32[16,1,32]{2,1,0:T(1,128)}), s32[16,1,32]{2,1,0:T(1,128)S(1)}, u32[]{:S(2)}, u32[]{:S(2)}) %all-to-all-start) | async-done | bytes 2080 | tf_op jit(solution)/shard_map/all_to_all | solution.py:105
  17.1 0.2 select_reduce_fusion
  17.5 0.2 convolution_convert_fusion.3
  17.7 0.9 %broadcast_in_dim.23 = bf16[8,64,512]{2,1,0:T(8,128)(2,1)} broadcast(bf16[64,512]{1,0:T(8,128)(2,1)S(1)} %convolution_convert_fusion.3), dimensions={1,2} | broadcast | bytes 589824 | tf_op jit(solution)/shard_map/broadcast_in_dim | solution.py:132
  18.6 4.1 %all-to-all-start.1 = ((bf16[8,64,512]{2,1,0:T(8,128)(2,1)}), bf16[8,64,512]{2,1,0:T(8,128)(2,1)}, u32[]{:S(2)}, u32[]{:S(2)}) async-start(bf16[8,64,512]{2,1,0:T(8,128)(2,1)} %broadcast_in_dim.23), calls=%async_computation.1 | async-start | bytes 1048576 | tf_op jit(solution)/shard_map/all_to_all | solution.py:131
  22.8 2.8 %dynamic-slice_bitcast_fusion.1 = (bf16[1024,512]{1,0:T(8,128)(2,1)}, bf16[1024,512]{1,0:T(8,128)(2,1)S(1)}) fusion(bf16[2,1024,512]{2,1,0:T(8,128)(2,1)} %param.16, s32[]{:T(128)S(6)} %select_n.103, s32[]{:T(128)S(6)} %select_n.100), kind=kLoop, calls=%fused_computation.6 | loop fusion | bytes 4194312 | tf_op jit(solution)/shard_map/jit(dynamic_index_in_dim)/squeeze | solution.py:110
  25.6 1.5 %dynamic-slice_bitcast_fusion = (bf16[1024,512]{1,0:T(8,128)(2,1)}, bf16[1024,512]{1,0:T(8,128)(2,1)}) fusion(bf16[2,1024,512]{2,1,0:T(8,128)(2,1)S(1)} %copy-done.3, s32[]{:T(128)S(6)} %select_n.103, s32[]{:T(128)S(6)} %select_n.100), kind=kLoop, calls=%fused_computation.5 | loop fusion | bytes 4194312 | tf_op jit(solution)/shard_map/jit(dynamic_index_in_dim)/squeeze | solution.py:110
  27.1 0.5 collective-permute-start.2
  27.6 0.1 copy.67
  27.8 0.6 dynamic_slice.43
  28.4 1.9 %slice.26.weight_ref = bf16[512,512]{1,0:T(8,128)(2,1)} slice(bf16[512,2048]{1,0:T(8,128)(2,1)} %param.14), slice={[0:512], [1024:1536]} | slice | bytes 1048576 | tf_op jit(solution)/shard_map/slice | solution.py:170
  30.3 0.2 compare_select_fusion
  30.7 0.7 %dynamic-slice_reduce_fusion.1 = (s32[16]{0:T(128)S(1)}, s32[16]{0:T(128)S(1)}) fusion(s32[16,16,2]{0,2,1:T(2,128)S(1)} %compare_select_fusion, s32[]{:T(128)S(6)} %select_n.102, s32[]{:T(128)S(6)} %select_n.104, s32[]{:T(128)S(6)} %select_n.109, s32[]{:T(128)S(6)} %select_n.110), kind=kLoop, calls=%fused_computation.58 | loop fusion | bytes 272 | tf_op jit(solution)/shard_map/jit(dynamic_index_in_dim)/dynamic_slice | solution.py:110
  31.4 6.1 %all-to-all-done.1 = bf16[8,64,512]{2,1,0:T(8,128)(2,1)} async-done(((bf16[8,64,512]{2,1,0:T(8,128)(2,1)}), bf16[8,64,512]{2,1,0:T(8,128)(2,1)}, u32[]{:S(2)}, u32[]{:S(2)}) %all-to-all-start.1) | async-done | bytes 524320 | tf_op jit(solution)/shard_map/all_to_all | solution.py:131
  37.5 2.1 %convolution_convert_fusion = bf16[272,512]{1,0:T(8,128)(2,1)} fusion(bf16[512,512]{1,0:T(8,128)(2,1)} %bitcast.3, s32[272]{0:T(512)S(1)} %pad_add_fusion.1), kind=kOutput, calls=%fused_computation | convolution fusion | flops 142884864 | bytes 803904 | tf_op jit(solution)/shard_map/dot_general | solution.py:152
  39.6 0.7 %subtract_subtract_fusion = (s32[256,1]{1,0:T(8,128)S(1)}, s32[256,1]{1,0:T(8,128)S(1)}) fusion(s32[256,1]{1,0:T(8,128)S(1)} %copy.67, s32[]{:T(128)} %bitcast.4, s32[]{:T(128)S(6)} %mul.119, s32[]{:T(128)S(6)} %mul.118), kind=kLoop, calls=%fused_computation.17 | loop fusion | flops 768 | bytes 3084 | tf_op jit(solution)/shard_map/sub | solution.py:172
  40.4 1.0 %collective-permute-done = bf16[272,512]{1,0:T(8,128)(2,1)} collective-permute-done((bf16[272,512]{1,0:T(8,128)(2,1)}, bf16[272,512]{1,0:T(8,128)(2,1)}, u32[]{:S(2)}, u32[]{:S(2)}) %collective-permute-start) | collective-permute-done | bytes 278560 | tf_op jit(solution)/shard_map/ppermute | solution.py:157
  41.5 1.5 %fusion = bf16[272,512]{1,0:T(8,128)(2,1)S(1)} fusion(bf16[272,512]{1,0:T(8,128)(2,1)} %collective-permute-done, bf16[512,512]{1,0:T(8,128)(2,1)} %bitcast.3, s32[272]{0:T(512)S(1)} %pad_add_fusion), kind=kOutput, calls=%fused_computation.2 | convolution fusion | flops 143024128 | bytes 1082432 | tf_op jit(solution)/shard_map/dot_general | solution.py:152
  43.1 7.7 %attend.1 = bf16[256,512]{1,0:T(8,128)(2,1)} custom-call(bf16[256,512]{1,0:T(8,128)(2,1)S(1)} %slice.31.routed_ref, bf16[512,512]{1,0:T(8,128)(2,1)S(1)} %copy-done.2, s32[256,1]{1,0:T(8,128)S(1)} %get-tuple-element.19.first_ref, s32[256,1]{1,0:T(8,128)S(1)} %get-tuple-element.18.second_ref, bf16[1024,512]{1,0:T(8,128)(2,1)S(1)} %get-tuple-element.17.keys_a, ...), custom_call_target="tpu_custom_call" | custom-call | tf_op jit(solution)/shard_map/attend/pallas_call | solution.py:62
  50.8 3.7 %all-to-all-start.2 = ((bf16[16,16,512]{2,1,0:T(8,128)(2,1)}), bf16[16,16,512]{2,1,0:T(8,128)(2,1)S(1)}, u32[]{:S(2)}, u32[]{:S(2)}) async-start(bf16[16,16,512]{2,1,0:T(8,128)(2,1)} %bitcast.9), calls=%async_computation.2 | async-start | bytes 524288 | tf_op jit(solution)/shard_map/all_to_all | solution.py:179
  54.5 2.1 %fusion.16 = (bf16[32,2048]{1,0:T(8,128)(2,1)S(1)}, f32[32,2048]{1,0:T(8,128)S(1)}) fusion(bf16[32,512]{1,0:T(8,128)(2,1)S(1)} %maximum_select_fusion, bf16[512,2048]{1,0:T(8,128)(2,1)} %param.14), kind=kOutput, calls=%fused_computation.73 | convolution fusion | flops 67436544 | bytes 2523136 | tf_op jit(solution)/shard_map/dot_general | solution.py:183
  57.2 7.3 %all-to-all-done.2 = bf16[16,16,512]{2,1,0:T(8,128)(2,1)S(1)} async-done(((bf16[16,16,512]{2,1,0:T(8,128)(2,1)}), bf16[16,16,512]{2,1,0:T(8,128)(2,1)S(1)}, u32[]{:S(2)}, u32[]{:S(2)}) %all-to-all-start.2) | async-done | bytes 262176 | tf_op jit(solution)/shard_map/all_to_all | solution.py:179
  64.6 0.1 fusion.15
  64.7 0.2 multiply_reduce_fusion
  64.9 0.2 add_convert_fusion
  65.1 0.7 %copy.69 = bf16[2,16,512]{2,0,1:T(2,128)(2,1)} copy(bf16[2,16,512]{2,1,0:T(8,128)(2,1)S(1)} %bitcast.38) | data formatting | bytes 65536 | tf_op jit(solution)/shard_map/reshape | solution.py:197
  (53 shorter events, 1.6 us)
Async XLA Ops:
  0.6 10.1 %copy-start = (bf16[2048,512]{1,0:T(8,128)(2,1)S(1)}, bf16[2048,512]{1,0:T(8,128)(2,1)}, u32[]{:S(2)}) copy-start(bf16[2048,512]{1,0:T(8,128)(2,1)} %param.13) | copy-start | bytes 6291460
  3.3 13.8 %all-to-all-start = ((s32[16,1,32]{2,1,0:T(1,128)}), s32[16,1,32]{2,1,0:T(1,128)S(1)}, u32[]{:S(2)}, u32[]{:S(2)}) async-start(s32[16,1,32]{2,1,0:T(1,128)} %broadcast_in_dim.19), calls=%async_computation | async-start | bytes 16384 | tf_op jit(solution)/shard_map/all_to_all | solution.py:105
  14.0 4.6 %copy-start.5 = (bf16[128,512]{1,0:T(8,128)(2,1)}, bf16[128,512]{1,0:T(8,128)(2,1)S(1)}, u32[]{:S(2)}) copy-start(bf16[128,512]{1,0:T(8,128)(2,1)S(1)} %convolution_convert_fusion.2) | copy-start | bytes 393220
  18.6 18.9 %all-to-all-start.1 = ((bf16[8,64,512]{2,1,0:T(8,128)(2,1)}), bf16[8,64,512]{2,1,0:T(8,128)(2,1)}, u32[]{:S(2)}, u32[]{:S(2)}) async-start(bf16[8,64,512]{2,1,0:T(8,128)(2,1)} %broadcast_in_dim.23), calls=%async_computation.1 | async-start | bytes 1048576 | tf_op jit(solution)/shard_map/all_to_all | solution.py:131
  22.8 2.8 %copy-start.3 = (bf16[2,1024,512]{2,1,0:T(8,128)(2,1)S(1)}, bf16[2,1024,512]{2,1,0:T(8,128)(2,1)}, u32[]{:S(2)}) copy-start(bf16[2,1024,512]{2,1,0:T(8,128)(2,1)} %param.17) | copy-start | bytes 6291460
  25.6 2.0 %copy-start.6 = (s32[256,2]{0,1:T(2,128)S(1)}, s32[256,2]{0,1:T(2,128)}, u32[]{:S(2)}) copy-start(s32[256,2]{0,1:T(2,128)} %param.21) | copy-start | bytes 6148
  25.6 2.2 %copy-start.7 = (s32[2]{0:T(128)S(1)}, s32[2]{0:T(128)}, u32[]{:S(2)}) copy-start(s32[2]{0:T(128)} %param.20) | copy-start | bytes 28
  25.6 17.4 %collective-permute-start.1 = (bf16[1024,512]{1,0:T(8,128)(2,1)}, bf16[1024,512]{1,0:T(8,128)(2,1)}, u32[]{:S(2)}, u32[]{:S(2)}) collective-permute-start(bf16[1024,512]{1,0:T(8,128)(2,1)} %get-tuple-element.16), channel_id=1, source_target_pairs={{0,1},{1,0},{2,3},{3,2},{4,5},{5,4},{6,7},{7,6},{8,9},{9,8},{10,11... | collective-permute-start | bytes 3145736 | tf_op jit(solution)/shard_map/ppermute | solution.py:112
  27.1 15.9 %collective-permute-start.2 = (bf16[1024,512]{1,0:T(8,128)(2,1)}, bf16[1024,512]{1,0:T(8,128)(2,1)}, u32[]{:S(2)}, u32[]{:S(2)}) collective-permute-start(bf16[1024,512]{1,0:T(8,128)(2,1)} %get-tuple-element.14), channel_id=1, source_target_pairs={{0,1},{1,0},{2,3},{3,2},{4,5},{5,4},{6,7},{7,6},{8,9},{9,8},{10,11... | collective-permute-start | bytes 3145736 | tf_op jit(solution)/shard_map/ppermute | solution.py:113
  39.6 1.9 %collective-permute-start = (bf16[272,512]{1,0:T(8,128)(2,1)}, bf16[272,512]{1,0:T(8,128)(2,1)}, u32[]{:S(2)}, u32[]{:S(2)}) collective-permute-start(bf16[272,512]{1,0:T(8,128)(2,1)} %convolution_convert_fusion), channel_id=1, source_target_pairs={{0,1},{1,0},{2,3},{3,2},{4,5},{5,4},{6,7},{7,6},{8,9},{9,8},{10,11... | collective-permute-start | bytes 835592 | tf_op jit(solution)/shard_map/ppermute | solution.py:157
  40.4 2.6 %copy-start.1 = (bf16[1024,512]{1,0:T(8,128)(2,1)S(1)}, bf16[1024,512]{1,0:T(8,128)(2,1)}, u32[]{:S(2)}) copy-start(bf16[1024,512]{1,0:T(8,128)(2,1)} %get-tuple-element.15.values_a) | copy-start | bytes 3145732
  40.4 2.7 %copy-start.2 = (bf16[512,512]{1,0:T(8,128)(2,1)S(1)}, bf16[512,512]{1,0:T(8,128)(2,1)}, u32[]{:S(2)}) copy-start(bf16[512,512]{1,0:T(8,128)(2,1)} %slice.26.weight_ref) | copy-start | bytes 1572868
  50.8 13.7 %all-to-all-start.2 = ((bf16[16,16,512]{2,1,0:T(8,128)(2,1)}), bf16[16,16,512]{2,1,0:T(8,128)(2,1)S(1)}, u32[]{:S(2)}, u32[]{:S(2)}) async-start(bf16[16,16,512]{2,1,0:T(8,128)(2,1)} %bitcast.9), calls=%async_computation.2 | async-start | bytes 524288 | tf_op jit(solution)/shard_map/all_to_all | solution.py:179
  54.5 10.4 %copy-start.4 = (bf16[512,512]{1,0:T(8,128)(2,1)S(1)}, bf16[512,512]{1,0:T(8,128)(2,1)}, u32[]{:S(2)}) copy-start(bf16[512,512]{1,0:T(8,128)(2,1)} %param.15) | copy-start | bytes 1572868

commit v2 on v1

v2 whole, which is shorter than its diff:
```python
import functools

import jax
import jax.numpy as jnp
from jax import lax
from jax.experimental import pallas as pl
from jax.experimental.pallas import tpu as pltpu
from jax.sharding import PartitionSpec as P

HEADS = 8
LANES = 128


def layer_norm(values):
    centre = values - jnp.mean(values, axis=-1, keepdims=True)
    return centre * lax.rsqrt(jnp.mean(centre * centre, axis=-1, keepdims=True) + 1e-05)


def self_term(query, key, value):
    rows, width = query.shape
    size = width // HEADS
    q_heads = query.astype(jnp.float32).reshape(rows, HEADS, size)
    k_heads = key.astype(jnp.float32).reshape(rows, HEADS, size)
    v_heads = value.astype(jnp.float32).reshape(rows, HEADS, size)
    score = jnp.sum(q_heads * k_heads, axis=-1) * size ** (-0.5)
    return (jax.nn.silu(score)[:, :, None] * v_heads).reshape(rows, width)


def code_kernel(depth, rows, owner_ref, row_ref, out_ref):
    users = owner_ref.shape[0]
    owners = jnp.concatenate([owner_ref[user] for user in range(users)], axis=1)
    wanted = jnp.concatenate([row_ref[user : user + 1, :] for user in range(users)], axis=1)
    slot = lax.broadcasted_iota(jnp.int32, owners.shape, 1)
    ranks = jnp.zeros_like(owners)
    for other in range(owners.shape[1] - 1):
        same = (owners == owners[:, other : other + 1]) & (slot > other)
        ranks = ranks + same.astype(jnp.int32)
    code = (owners * depth + ranks) * rows + wanted
    out_ref[...] = jnp.broadcast_to(code[None], out_ref.shape)


def asked_kernel(depth, codes_ref, embed_ref, out_ref):
    room = codes_ref.shape[0]
    rows = embed_ref.shape[0]
    codes = codes_ref[...]
    rank = lax.rem(lax.broadcasted_iota(jnp.int32, codes.shape, 0), depth)
    hit = lax.div(codes, rows) == lax.axis_index("seq") * depth + rank
    asked = jnp.sum(jnp.where(hit, lax.rem(codes, rows), 0), axis=1, keepdims=True)
    chosen = (lax.broadcasted_iota(jnp.int32, (room, rows), 1) == asked).astype(jnp.bfloat16)
    picked = jnp.dot(chosen, embed_ref[...], preferred_element_type=jnp.float32).astype(jnp.bfloat16)
    for receiver in range(out_ref.shape[0]):
        out_ref[receiver] = picked


def dot_kernel(left_ref, right_ref, out_ref):
    out_ref[...] = jnp.dot(
        left_ref[...], right_ref[...], preferred_element_type=jnp.float32
    ).astype(out_ref.dtype)


def attend_kernel(
    kept_ref, came_ref, weight_ref, seen_ref, keys_a, values_a, keys_b, values_b, out_ref, routed_ref, keys, values, sems
):
    rows, width = out_ref.shape
    size = width // HEADS
    block = keys_b.shape[0]
    core = lax.rem(lax.axis_index("seq"), 2)
    copies = []
    for tile in range(width // LANES):
        span = pl.ds(tile * LANES, LANES)
        for number, (mine, other, target) in enumerate(
            ((keys_a, keys_b, keys), (values_a, values_b, values))
        ):
            here = pl.ds(pl.multiple_of(core * block, block), block)
            there = pl.ds(pl.multiple_of((1 - core) * block, block), block)
            pair = (
                pltpu.make_async_copy(
                    mine.at[core, :, span], target.at[here, span], sems.at[tile, 2 * number]
                ),
                pltpu.make_async_copy(
                    other.at[:, span], target.at[there, span], sems.at[tile, 2 * number + 1]
                ),
            )
            for copy in pair:
                copy.start()
            copies.append(pair)

    routed = kept_ref[...] + came_ref[...]
    routed_ref[...] = routed
    query = jax.nn.silu(
        jnp.dot(routed[:rows], weight_ref[...], preferred_element_type=jnp.float32)
    ).astype(jnp.bfloat16)
    query = query * jnp.bfloat16(0.5 * size ** (-0.5))
    lane = lax.broadcasted_iota(jnp.int32, (rows, LANES), 1)
    per_tile = LANES // size
    for tile in range(width // LANES):
        span = slice(tile * LANES, (tile + 1) * LANES)
        whole = query[:, span]
        joined = None
        for copy in copies[2 * tile]:
            copy.wait()
        for head in range(per_tile):
            mine = (lane >= head * size) & (lane < (head + 1) * size)
            part = jnp.where(mine, whole, jnp.zeros_like(whole))
            half = lax.dot_general(
                part, keys[:, span], (((1,), (1,)), ((), ())), preferred_element_type=jnp.float32
            ).astype(jnp.bfloat16)
            weight = half + half * jnp.tanh(half)
            event = lax.broadcasted_iota(jnp.int32, weight.shape, 1)
            weight = jnp.where(event < seen_ref[...], weight, jnp.zeros_like(weight))
            if head == 0:
                for copy in copies[2 * tile + 1]:
                    copy.wait()
            total = jnp.dot(weight, values[:, span], preferred_element_type=jnp.float32)
            joined = total if joined is None else jnp.where(mine, total, joined)
        out_ref[:, span] = joined.astype(out_ref.dtype)


IN_VMEM = pl.BlockSpec(memory_space=pltpu.VMEM)
ANYWHERE = pl.BlockSpec(memory_space=pl.ANY)


def small_call(kernel, shape, dtype, name, operands):
    return pl.pallas_call(
        kernel,
        out_shape=jax.ShapeDtypeStruct(shape, dtype),
        in_specs=[IN_VMEM] * operands,
        out_specs=IN_VMEM,
        compiler_params=pltpu.CompilerParams(vmem_limit_bytes=24 * 2**20),
        name=name,
    )


def attend(rows, kept, came, weight, seen, keys_a, values_a, keys_b, values_b):
    width = kept.shape[1]
    events = 2 * keys_b.shape[0]
    return pl.pallas_call(
        attend_kernel,
        out_shape=(
            jax.ShapeDtypeStruct((rows, width), jnp.bfloat16),
            jax.ShapeDtypeStruct(kept.shape, jnp.bfloat16),
        ),
        in_specs=[IN_VMEM] * 4 + [ANYWHERE] * 4,
        out_specs=(IN_VMEM, IN_VMEM),
        scratch_shapes=[
            pltpu.VMEM((events, width), jnp.bfloat16),
            pltpu.VMEM((events, width), jnp.bfloat16),
            pltpu.SemaphoreType.DMA((width // LANES, 4)),
        ],
        compiler_params=pltpu.CompilerParams(vmem_limit_bytes=40 * 2**20),
        name="attend",
    )(kept, came, weight, seen, keys_a, values_a, keys_b, values_b)


def per_device(
    item_features,
    tower_in,
    tower_out,
    proj_weight,
    out_weight,
    hist_keys,
    hist_values,
    owner_of,
    row_in,
    hist_lengths,
    causal_offsets,
):
    width = tower_out.shape[1]
    devices = lax.axis_size("seq")
    me = lax.axis_index("seq")
    slot_count, users = row_in.shape
    assert users == 2 and devices % users == 0
    slots = slot_count * users
    rows = item_features.shape[0]
    hist_dev = hist_keys.shape[1]
    depth = max(2, 2 * slots // devices)
    room = devices * depth
    core = me % users
    partner = me + 1 - 2 * core
    swap = [(i, i ^ 1) for i in range(devices)]
    alike = [[b + users * k for k in range(devices // users)] for b in range(users)]

    codes = lax.all_to_all(
        small_call(
            functools.partial(code_kernel, depth, rows), (devices, depth, slots), jnp.int32, "codes", 2
        )(owner_of.transpose(1, 2, 0), row_in.T),
        "seq",
        split_axis=0,
        concat_axis=0,
        tiled=True,
    )

    hidden = jax.nn.silu(
        jnp.dot(item_features, tower_in, preferred_element_type=jnp.float32)
    ).astype(jnp.bfloat16)
    item_embed = jnp.dot(hidden, tower_out, preferred_element_type=jnp.float32).astype(jnp.bfloat16)

    handed = small_call(
        functools.partial(asked_kernel, depth), (devices // users, room, width), jnp.bfloat16, "asked", 2
    )(codes.reshape(room, slots), item_embed)
    gathered = lax.all_to_all(
        handed, "seq", split_axis=0, concat_axis=0, tiled=True, axis_index_groups=alike
    ).reshape(devices // users * room, width)

    def of_user(array, user, axis=0):
        return lax.dynamic_index_in_dim(array, user, axis, keepdims=False)

    handed, give_keys, give_values = lax.optimization_barrier((handed, hist_keys, hist_values))
    keys_b = lax.ppermute(of_user(give_keys, 1 - core), "seq", swap)
    values_b = lax.ppermute(of_user(give_values, 1 - core), "seq", swap)

    places = codes[:, 0] // rows
    asker = jnp.arange(devices, dtype=jnp.int32)[:, None]
    owner = places // depth
    spot = jnp.where(
        owner % users == core, (owner // users) * room + asker * depth + places % depth, -1
    ).reshape(devices, users, slot_count)
    spot_mine = of_user(spot, core, 1)
    spot_other = of_user(spot, 1 - core, 1)

    def choice(spots):
        return (
            spots[:, None] == jnp.arange(devices // users * room, dtype=jnp.int32)[None, :]
        ).astype(jnp.bfloat16)

    cands = devices * slot_count
    choose_sent = choice(jnp.concatenate([spot_other.reshape(cands), of_user(spot_mine, partner)]))
    choose_kept = choice(jnp.concatenate([spot_mine.reshape(cands), of_user(spot_other, me)]))
    choose_sent, choose_kept = lax.optimization_barrier((choose_sent, choose_kept))
    pick = small_call(dot_kernel, (cands + slot_count, width), jnp.bfloat16, "pick", 2)
    sent = pick(choose_sent, gathered)
    kept = pick(choose_kept, gathered)
    came = lax.ppermute(sent, "seq", swap)

    limit = (of_user(hist_lengths, core) - of_user(causal_offsets, core, 1))[:, None]
    user_part, routed = attend(
        cands,
        kept,
        came,
        proj_weight[:, 2 * width : 3 * width],
        limit - (me - core) * hist_dev,
        hist_keys,
        hist_values,
        keys_b,
        values_b,
    )
    backs = lax.all_to_all(
        user_part.reshape(devices, slot_count, width), "seq", split_axis=0, concat_axis=0, tiled=True
    )

    own_mine = lax.dynamic_slice_in_dim(routed, me * slot_count, slot_count, 0)
    own_other = routed[cands:]
    routed_own = jnp.where(
        core == 0,
        jnp.concatenate([own_mine, own_other]),
        jnp.concatenate([own_other, own_mine]),
    )
    proj = jax.nn.silu(jnp.dot(routed_own, proj_weight, preferred_element_type=jnp.float32))
    gate = proj[:, :width]
    value = proj[:, width : 2 * width].astype(jnp.bfloat16)
    query = proj[:, 2 * width : 3 * width].astype(jnp.bfloat16)
    key = proj[:, 3 * width :].astype(jnp.bfloat16)
    own = self_term(query, key, value)

    attended = jnp.sum(
        backs.astype(jnp.float32).reshape(devices // users, slots, width), axis=0
    )
    mixed = (layer_norm(attended + own) * gate).astype(jnp.bfloat16)
    result = routed_own.astype(jnp.float32) + jnp.dot(
        mixed, out_weight, preferred_element_type=jnp.float32
    )
    cand_out = result.astype(jnp.bfloat16).reshape(users, slot_count, width).transpose(1, 0, 2)
    return (item_embed, cand_out)


def solution(mesh):
    return jax.shard_map(
        per_device,
        mesh=mesh,
        in_specs=(
            P(("grp", "seq"), None),
            P(),
            P(),
            P(),
            P(),
            P("grp", "seq", None),
            P("grp", "seq", None),
            P(("grp", "seq"), None, None),
            P(("grp", "seq"), None),
            P("grp"),
            P("grp", None),
        ),
        out_specs=(P(("grp", "seq"), None), P(("grp", "seq"), None, None)),
        check_vma=False,
    )
```

time: 66.4 us -> 68.9 us (1.038)
  matrix products: 9.45 us -> 5.66 us
  Pallas kernels: 7.7 us -> 11.4 us
  waiting for transfers between devices: 17.4 us -> 20.1 us
    all_to_all x2, waiting for transfers between devices: 9.06 us -> 12.9 us  [the longest x1 9.87 us: per_device(): lax.all_to_all(handed, 'seq', split_axis=0, concat_axis=0, tiled=True, ax...]
    dot_general x3 -> x0, matrix products: 3.79 us -> none  [the longest x2 3.58 us: pick(): jnp.dot(chosen, gathered, preferred_element_type=jnp.float32)]
    unnamed x19 -> x23, local copies, waits for them, and re-layouts: 1.85 us -> 5.62 us
    pallas_call x1 -> x5, Pallas kernels: 7.7 us -> 11.4 us  [the longest x1 8.8 us: attend(): pl.pallas_call(attend_kernel, out_shape=(jax.ShapeDtypeStruct((rows, widt...]
    broadcast_in_dim x2 -> x0, local copies, waits for them, and re-layouts: 1.46 us -> none  [the longest x1 0.85 us: per_device(): jnp.broadcast_to(picked[None], (devices // users, room, width))]
    ppermute x3, waiting for transfers between devices: 1.05 us -> 0.01 us  [the longest x1 0.01 us: per_device(): keys_b = lax.ppermute(of_user(give_keys, 1 - core), 'seq', swap)]
    dynamic_slice x6 -> x3, local copies, waits for them, and re-layouts: 1.49 us -> 0.65 us  [of_user(): return lax.dynamic_index_in_dim(array, user, axis, keepdims=False)]
    squeeze x2 -> x3, local copies, waits for them, and re-layouts: 4.32 us -> 3.5 us  [of_user(): return lax.dynamic_index_in_dim(array, user, axis, keepdims=False)]
  transfers between devices with their start and end apart: 6 -> 6, of which waited for: 4 -> 3; matrix products, arithmetic and copies ran while one was open for 28% -> 19% of each run, Pallas kernels for 0% -> 2%
where the time goes in v2:
time: 68.9 us; the launch traced here: 68.3 us
  waiting for transfers between devices  20.1 us (29%)
  starting transfers between devices  15.2 us (22%)
  local copies, waits for them, and re-layouts  12.7 us (18%)
  Pallas kernels  11.4 us (17%)
  matrix products  5.66 us (8%)
  other arithmetic  2.22 us (3%)
  between operations  0.97 us (1%)
    all_to_all x1, waiting for transfers between devices, per_device(): lax.all_to_all(handed, 'seq', split_axis=0, concat_axis=0, tiled=True, ax...  9.87 us
    pallas_call x1, Pallas kernels, attend(): pl.pallas_call(attend_kernel, out_shape=(jax.ShapeDtypeStruct((rows, widt...  8.8 us
    all_to_all x1, starting transfers between devices, per_device(): lax.all_to_all(small_call(functools.partial(code_kernel, depth, rows), (d...  7.41 us
    all_to_all x1, waiting for transfers between devices, per_device(): lax.all_to_all(user_part.reshape(devices, slot_count, width), 'seq', spli...  7.26 us
    unnamed x23, local copies, waits for them, and re-layouts  5.62 us
    all_to_all x1, starting transfers between devices, per_device(): lax.all_to_all(user_part.reshape(devices, slot_count, width), 'seq', spli...  3.84 us
    squeeze x3, local copies, waits for them, and re-layouts, of_user(): return lax.dynamic_index_in_dim(array, user, axis, keepdims=False)  3.5 us
    all_to_all x1, starting transfers between devices, per_device(): lax.all_to_all(handed, 'seq', split_axis=0, concat_axis=0, tiled=True, ax...  3.49 us
  transfers between devices with their start and end apart: 6, of which 3 were waited for; matrix products, arithmetic and copies ran while one was open for 19% of the time, Pallas kernels for 2%

profile of v2, /device:TPU:0, one launch (start us, length us, event | category | flops | bytes accessed | tf_op | source)
XLA Modules:
  0.0 68.3 jit_solution(6704566674476723677)
XLA Ops:
  0.7 0.8 %copy-done.5 = s32[16,2,1]{0,2,1:T(1,128)S(1)} copy-done((s32[16,2,1]{0,2,1:T(1,128)S(1)}, s32[16,2,1]{0,2,1:T(1,128)}, u32[]{:S(2)}) %copy-start.5) | copy-done | bytes 152
  1.5 0.7 copy-done.6
  2.2 0.2 codes.1
  2.4 0.7 %reshape.102 = s32[16,1,128]{2,1,0:T(1,128)} reshape(s32[16,4,32]{2,1,0:T(4,128)S(1)} %codes.1) | data formatting | bytes 16384
  3.0 7.4 %all-to-all-start = ((s32[16,1,128]{2,1,0:T(1,128)}), s32[16,1,128]{2,1,0:T(1,128)S(1)}, u32[]{:S(2)}, u32[]{:S(2)}) async-start(s32[16,1,128]{2,1,0:T(1,128)} %reshape.102), calls=%async_computation | async-start | bytes 16384 | tf_op jit(solution)/shard_map/all_to_all | solution.py:183
  10.5 3.3 %convolution_convert_fusion.embed_ref = bf16[128,512]{1,0:T(8,128)(2,1)S(1)} fusion(bf16[2048,512]{1,0:T(8,128)(2,1)S(1)} %copy-done, bf16[128,1024]{1,0:T(8,128)(2,1)} %param.11, bf16[1024,2048]{1,0:T(8,128)(2,1)} %param.12), kind=kOutput, calls=%fused_computation | convolution fusion | flops 806682624 | bytes 6684672 | tf_op jit(solution)/shard_map/dot_general | solution.py:196
  13.8 3.0 %all-to-all-done = s32[16,1,128]{2,1,0:T(1,128)S(1)} async-done(((s32[16,1,128]{2,1,0:T(1,128)}), s32[16,1,128]{2,1,0:T(1,128)S(1)}, u32[]{:S(2)}, u32[]{:S(2)}) %all-to-all-start) | async-done | bytes 8224 | tf_op jit(solution)/shard_map/all_to_all | solution.py:183
  16.8 0.5 broadcast.133
  17.3 0.7 reduce.12
  18.1 1.0 %asked.1 = bf16[8,64,512]{2,1,0:T(8,128)(2,1)} custom-call(s32[64,32]{1,0:T(8,128)S(1)} %bitcast.29, bf16[128,512]{1,0:T(8,128)(2,1)S(1)} %convolution_convert_fusion.embed_ref), custom_call_target="tpu_custom_call" | custom-call | tf_op jit(solution)/shard_map/asked/pallas_call | solution.py:198
  19.2 3.5 %all-to-all-start.1 = ((bf16[8,64,512]{2,1,0:T(8,128)(2,1)}), bf16[8,64,512]{2,1,0:T(8,128)(2,1)S(1)}, u32[]{:S(2)}, u32[]{:S(2)}) async-start(bf16[8,64,512]{2,1,0:T(8,128)(2,1)} %asked.1), calls=%async_computation.1 | async-start | bytes 1048576 | tf_op jit(solution)/shard_map/all_to_all | solution.py:201
  22.7 2.4 %dynamic-slice_bitcast_fusion.1 = bf16[1024,512]{1,0:T(8,128)(2,1)} fusion(bf16[2,1024,512]{2,1,0:T(8,128)(2,1)} %keys_a.1, s32[]{:T(128)S(6)} %select_n.86), kind=kLoop, calls=%fused_computation.4 | loop fusion | bytes 2097156 | tf_op jit(solution)/shard_map/jit(dynamic_index_in_dim)/squeeze | solution.py:206
  25.1 1.0 %dynamic-slice_bitcast_fusion = bf16[1024,512]{1,0:T(8,128)(2,1)} fusion(bf16[2,1024,512]{2,1,0:T(8,128)(2,1)S(1)} %copy-done.2, s32[]{:T(128)S(6)} %select_n.86), kind=kLoop, calls=%fused_computation.3 | loop fusion | bytes 2097156 | tf_op jit(solution)/shard_map/jit(dynamic_index_in_dim)/squeeze | solution.py:206
  26.2 0.5 collective-permute-start.2
  26.8 0.2 compare_select_fusion
  27.4 9.9 %all-to-all-done.1 = bf16[8,64,512]{2,1,0:T(8,128)(2,1)S(1)} async-done(((bf16[8,64,512]{2,1,0:T(8,128)(2,1)}), bf16[8,64,512]{2,1,0:T(8,128)(2,1)S(1)}, u32[]{:S(2)}, u32[]{:S(2)}) %all-to-all-start.1) | async-done | bytes 524320 | tf_op jit(solution)/shard_map/all_to_all | solution.py:201
  37.3 1.0 %pick.3 = bf16[272,512]{1,0:T(8,128)(2,1)} custom-call(bf16[272,512]{1,0:T(8,128)(2,1)S(1)} %fusion.1.left_ref, bf16[512,512]{1,0:T(8,128)(2,1)S(1)} %bitcast.27), custom_call_target="tpu_custom_call" | custom-call | tf_op jit(solution)/shard_map/pick/pallas_call | solution.py:231
  38.4 0.1 copy.22
  38.5 0.6 dynamic_slice.36
  39.1 1.1 %slice.25.weight_ref = bf16[512,512]{1,0:T(8,128)(2,1)S(1)} slice(bf16[512,2048]{1,0:T(8,128)(2,1)} %param.14), slice={[0:512], [1024:1536]} | slice | bytes 1048576 | tf_op jit(solution)/shard_map/slice | solution.py:240
  40.2 0.7 subtract_subtract_fusion.seen_ref
  40.9 0.3 pick.2.kept_ref
  41.2 1.6 %copy-done.1 = bf16[2,1024,512]{2,1,0:T(8,128)(2,1)S(1)} copy-done((bf16[2,1024,512]{2,1,0:T(8,128)(2,1)S(1)}, bf16[2,1024,512]{2,1,0:T(8,128)(2,1)}, u32[]{:S(2)}) %copy-start.1) | copy-done | bytes 2097176
  42.8 1.6 %copy-done.3 = bf16[2,1024,512]{2,1,0:T(8,128)(2,1)S(1)} copy-done((bf16[2,1024,512]{2,1,0:T(8,128)(2,1)S(1)}, bf16[2,1024,512]{2,1,0:T(8,128)(2,1)}, u32[]{:S(2)}) %copy-start.3) | copy-done | bytes 2097176
  44.4 8.8 %attend.1 = (bf16[256,512]{1,0:T(8,128)(2,1)}, bf16[272,512]{1,0:T(8,128)(2,1)S(1)}) custom-call(bf16[272,512]{1,0:T(8,128)(2,1)S(1)} %pick.2.kept_ref, bf16[272,512]{1,0:T(8,128)(2,1)} %collective-permute-done.came_ref, bf16[512,512]{1,0:T(8,128)(2,1)S(1)} %slice.25.weight_ref, s32[256,1]{1,0:T(8,128)S(1)} %subtract_subtract_fusion.seen_ref, ...), custom_call_target="tpu_custom_call" | custom-call | tf_op jit(solution)/shard_map/attend/pallas_call | solution.py:137
  53.2 3.8 %all-to-all-start.2 = ((bf16[16,16,512]{2,1,0:T(8,128)(2,1)}), bf16[16,16,512]{2,1,0:T(8,128)(2,1)S(1)}, u32[]{:S(2)}, u32[]{:S(2)}) async-start(bf16[16,16,512]{2,1,0:T(8,128)(2,1)} %bitcast.9), calls=%async_computation.2 | async-start | bytes 524288 | tf_op jit(solution)/shard_map/all_to_all | solution.py:247
  57.1 2.1 %fusion.15 = (bf16[32,2048]{1,0:T(8,128)(2,1)S(1)}, f32[32,2048]{1,0:T(8,128)S(1)}) fusion(bf16[512,2048]{1,0:T(8,128)(2,1)} %param.14, bf16[16,512]{1,0:T(8,128)(2,1)S(1)} %get-tuple-element.19, bf16[16,512]{1,0:T(8,128)(2,1)S(1)} %get-tuple-element.18, pred[]{:T(512)S(6)} %eq.41), kind=kOutput, calls=%fused_computation.58 | convolution fusion | flops 67584000 | bytes 2523137 | tf_op jit(solution)/shard_map/dot_general | solution.py:258
  59.8 7.3 %all-to-all-done.2 = bf16[16,16,512]{2,1,0:T(8,128)(2,1)S(1)} async-done(((bf16[16,16,512]{2,1,0:T(8,128)(2,1)}), bf16[16,16,512]{2,1,0:T(8,128)(2,1)S(1)}, u32[]{:S(2)}, u32[]{:S(2)}) %all-to-all-start.2) | async-done | bytes 262176 | tf_op jit(solution)/shard_map/all_to_all | solution.py:247
  67.1 0.1 fusion.14
  67.2 0.2 multiply_reduce_fusion
  67.4 0.2 fusion
  67.7 0.7 copy.24
  (45 shorter events, 1.3 us)
Async XLA Ops:
  0.6 9.8 %copy-start = (bf16[2048,512]{1,0:T(8,128)(2,1)S(1)}, bf16[2048,512]{1,0:T(8,128)(2,1)}, u32[]{:S(2)}) copy-start(bf16[2048,512]{1,0:T(8,128)(2,1)} %param.13) | copy-start | bytes 6291460
  0.6 0.8 %copy-start.5 = (s32[16,2,1]{0,2,1:T(1,128)S(1)}, s32[16,2,1]{0,2,1:T(1,128)}, u32[]{:S(2)}) copy-start(s32[16,2,1]{0,2,1:T(1,128)} %param.18) | copy-start | bytes 388
  1.5 0.7 copy-start.6
  3.0 13.8 %all-to-all-start = ((s32[16,1,128]{2,1,0:T(1,128)}), s32[16,1,128]{2,1,0:T(1,128)S(1)}, u32[]{:S(2)}, u32[]{:S(2)}) async-start(s32[16,1,128]{2,1,0:T(1,128)} %reshape.102), calls=%async_computation | async-start | bytes 16384 | tf_op jit(solution)/shard_map/all_to_all | solution.py:183
  13.8 12.4 %copy-start.4 = (bf16[128,512]{1,0:T(8,128)(2,1)}, bf16[128,512]{1,0:T(8,128)(2,1)S(1)}, u32[]{:S(2)}) copy-start(bf16[128,512]{1,0:T(8,128)(2,1)S(1)} %convolution_convert_fusion.embed_ref) | copy-start | bytes 393220
  19.2 18.1 %all-to-all-start.1 = ((bf16[8,64,512]{2,1,0:T(8,128)(2,1)}), bf16[8,64,512]{2,1,0:T(8,128)(2,1)S(1)}, u32[]{:S(2)}, u32[]{:S(2)}) async-start(bf16[8,64,512]{2,1,0:T(8,128)(2,1)} %asked.1), calls=%async_computation.1 | async-start | bytes 1048576 | tf_op jit(solution)/shard_map/all_to_all | solution.py:201
  22.7 2.5 %copy-start.2 = (bf16[2,1024,512]{2,1,0:T(8,128)(2,1)S(1)}, bf16[2,1024,512]{2,1,0:T(8,128)(2,1)}, u32[]{:S(2)}) copy-start(bf16[2,1024,512]{2,1,0:T(8,128)(2,1)} %values_a.1) | copy-start | bytes 6291460
  25.1 13.2 %copy-start.8 = (s32[256,2]{0,1:T(2,128)S(1)}, s32[256,2]{0,1:T(2,128)}, u32[]{:S(2)}) copy-start(s32[256,2]{0,1:T(2,128)} %param.21) | copy-start | bytes 6148
  25.1 13.4 %copy-start.9 = (s32[2]{0:T(128)S(1)}, s32[2]{0:T(128)}, u32[]{:S(2)}) copy-start(s32[2]{0:T(128)} %param.20) | copy-start | bytes 28
  25.1 16.0 %collective-permute-start.1 = (bf16[1024,512]{1,0:T(8,128)(2,1)}, bf16[1024,512]{1,0:T(8,128)(2,1)}, u32[]{:S(2)}, u32[]{:S(2)}) collective-permute-start(bf16[1024,512]{1,0:T(8,128)(2,1)} %dynamic-slice_bitcast_fusion.1), channel_id=1, source_target_pairs={{0,1},{1,0},{2,3},{3,2},{4,5},{5,4},{6,7},{7,6},{8,9},{9,8},{10,11... | collective-permute-start | bytes 3145736 | tf_op jit(solution)/shard_map/ppermute | solution.py:209
  26.2 15.0 %collective-permute-start.2 = (bf16[1024,512]{1,0:T(8,128)(2,1)}, bf16[1024,512]{1,0:T(8,128)(2,1)}, u32[]{:S(2)}, u32[]{:S(2)}) collective-permute-start(bf16[1024,512]{1,0:T(8,128)(2,1)} %dynamic-slice_bitcast_fusion), channel_id=1, source_target_pairs={{0,1},{1,0},{2,3},{3,2},{4,5},{5,4},{6,7},{7,6},{8,9},{9,8},{10,11... | collective-permute-start | bytes 3145736 | tf_op jit(solution)/shard_map/ppermute | solution.py:210
  38.4 2.8 %collective-permute-start = (bf16[272,512]{1,0:T(8,128)(2,1)}, bf16[272,512]{1,0:T(8,128)(2,1)}, u32[]{:S(2)}, u32[]{:S(2)}) collective-permute-start(bf16[272,512]{1,0:T(8,128)(2,1)} %pick.3), channel_id=1, source_target_pairs={{0,1},{1,0},{2,3},{3,2},{4,5},{5,4},{6,7},{7,6},{8,9},{9,8},{10,11... | collective-permute-start | bytes 835592 | tf_op jit(solution)/shard_map/ppermute | solution.py:233
  41.2 1.6 %copy-start.1 = (bf16[2,1024,512]{2,1,0:T(8,128)(2,1)S(1)}, bf16[2,1024,512]{2,1,0:T(8,128)(2,1)}, u32[]{:S(2)}) copy-start(bf16[2,1024,512]{2,1,0:T(8,128)(2,1)} %keys_a.1) | copy-start | bytes 6291460
  42.8 1.6 %copy-start.3 = (bf16[2,1024,512]{2,1,0:T(8,128)(2,1)S(1)}, bf16[2,1024,512]{2,1,0:T(8,128)(2,1)}, u32[]{:S(2)}) copy-start(bf16[2,1024,512]{2,1,0:T(8,128)(2,1)} %values_a.1) | copy-start | bytes 6291460
  53.2 13.9 %all-to-all-start.2 = ((bf16[16,16,512]{2,1,0:T(8,128)(2,1)}), bf16[16,16,512]{2,1,0:T(8,128)(2,1)S(1)}, u32[]{:S(2)}, u32[]{:S(2)}) async-start(bf16[16,16,512]{2,1,0:T(8,128)(2,1)} %bitcast.9), calls=%async_computation.2 | async-start | bytes 524288 | tf_op jit(solution)/shard_map/all_to_all | solution.py:247
  57.0 10.4 %copy-start.7 = (bf16[512,512]{1,0:T(8,128)(2,1)S(1)}, bf16[512,512]{1,0:T(8,128)(2,1)}, u32[]{:S(2)}) copy-start(bf16[512,512]{1,0:T(8,128)(2,1)} %param.15) | copy-start | bytes 1572868

commit v3 on v2

v3 whole, which is shorter than its diff:
```python
import functools

import jax
import jax.numpy as jnp
from jax import lax
from jax.experimental import pallas as pl
from jax.experimental.pallas import tpu as pltpu
from jax.sharding import PartitionSpec as P

HEADS = 8
LANES = 128


def layer_norm(values):
    centre = values - jnp.mean(values, axis=-1, keepdims=True)
    return centre * lax.rsqrt(jnp.mean(centre * centre, axis=-1, keepdims=True) + 1e-05)


def self_term(query, key, value):
    rows, width = query.shape
    size = width // HEADS
    q_heads = query.astype(jnp.float32).reshape(rows, HEADS, size)
    k_heads = key.astype(jnp.float32).reshape(rows, HEADS, size)
    v_heads = value.astype(jnp.float32).reshape(rows, HEADS, size)
    score = jnp.sum(q_heads * k_heads, axis=-1) * size ** (-0.5)
    return (jax.nn.silu(score)[:, :, None] * v_heads).reshape(rows, width)


def code_kernel(depth, rows, owner_hbm, row_hbm, out_ref, owner_ref, row_ref, sems):
    copies = (
        pltpu.make_async_copy(owner_hbm, owner_ref, sems.at[0]),
        pltpu.make_async_copy(row_hbm, row_ref, sems.at[1]),
    )
    for copy in copies:
        copy.start()
    for copy in copies:
        copy.wait()
    users = owner_ref.shape[0]
    owners = jnp.concatenate([owner_ref[user] for user in range(users)], axis=1)
    wanted = jnp.concatenate([row_ref[user : user + 1, :] for user in range(users)], axis=1)
    slot = lax.broadcasted_iota(jnp.int32, owners.shape, 1)
    ranks = jnp.zeros_like(owners)
    for other in range(owners.shape[1] - 1):
        same = (owners == owners[:, other : other + 1]) & (slot > other)
        ranks = ranks + same.astype(jnp.int32)
    code = (owners * depth + ranks) * rows + wanted
    out_ref[...] = jnp.broadcast_to(code[None], out_ref.shape)


def asked_kernel(depth, codes_ref, embed_ref, out_ref, chosen_ref):
    devices, _, slots = codes_ref.shape
    rows = embed_ref.shape[0]
    want = lax.axis_index("seq") * depth + lax.broadcasted_iota(jnp.int32, (depth, slots), 0)
    lane = lax.broadcasted_iota(jnp.int32, (depth, rows), 1)
    for asker in range(devices):
        codes = jnp.broadcast_to(codes_ref[asker], (depth, slots))
        hit = lax.div(codes, rows) == want
        asked = jnp.sum(jnp.where(hit, lax.rem(codes, rows), 0), axis=1, keepdims=True)
        chosen_ref[asker * depth : (asker + 1) * depth, :] = (lane == asked).astype(jnp.float32)
    picked = jnp.dot(
        chosen_ref[...].astype(jnp.bfloat16), embed_ref[...], preferred_element_type=jnp.float32
    ).astype(jnp.bfloat16)
    for receiver in range(out_ref.shape[0]):
        out_ref[receiver] = picked


def column(row, height):
    down = lax.broadcasted_iota(jnp.int32, (height, row.shape[1]), 0)
    along = lax.broadcasted_iota(jnp.int32, (height, row.shape[1]), 1)
    return jnp.sum(jnp.where(down == along, row, 0), axis=1, keepdims=True)


def ready_kernel(
    depth,
    rows,
    block,
    lengths_ref,
    codes_ref,
    offsets_ref,
    sent_ref,
    kept_ref,
    seen_ref,
):
    devices, _, slots = codes_ref.shape
    users = offsets_ref.shape[0]
    slot_count = slots // users
    room = devices * depth
    me = lax.axis_index("seq")
    core = lax.rem(me, users)
    asker = lax.broadcasted_iota(jnp.int32, codes_ref.shape, 0)
    places = lax.div(codes_ref[...], rows)
    owner = lax.div(places, depth)
    spots = jnp.where(
        lax.rem(owner, users) == core,
        lax.div(owner, users) * room + asker * depth + lax.rem(places, depth),
        -1,
    )
    first = spots[:, :, :slot_count]
    second = spots[:, :, slot_count:]
    mine = jnp.where(core == 0, first, second)
    other = jnp.where(core == 0, second, first)

    def one(array, index):
        return jnp.sum(jnp.where(asker[:, :, :slot_count] == index, array, 0), axis=0)

    cands = devices * slot_count
    blank = jnp.zeros((1, LANES - slot_count), jnp.int32)
    for chosen_ref, all_of, extra in (
        (sent_ref, other, one(mine, me + 1 - 2 * core)),
        (kept_ref, mine, one(other, me)),
    ):
        row = jnp.concatenate([all_of[r] for r in range(devices)] + [extra, blank], axis=1)
        spot = column(row, cands + slot_count)
        place = lax.broadcasted_iota(jnp.int32, chosen_ref.shape, 1)
        chosen_ref[...] = (place == spot).astype(jnp.float32).astype(jnp.bfloat16)

    offsets = jnp.where(core == 0, offsets_ref[0:1, :], offsets_ref[1:2, :])
    seen_ref[...] = column(lengths_ref[core] - (me - core) * block - offsets, cands)


def pick_kernel(chosen_ref, gathered_ref, out_ref):
    out_ref[...] = jnp.dot(
        chosen_ref[...], gathered_ref[...], preferred_element_type=jnp.float32
    ).astype(out_ref.dtype)


def keep_kernel(
    chosen_ref,
    gathered_ref,
    keys_near,
    values_near,
    keys_far,
    values_far,
    proj_hbm,
    out_ref,
    weight_ref,
    keys_ref,
    values_ref,
    sems,
):
    users, block, width = keys_near.shape
    core = lax.rem(lax.axis_index("seq"), users)
    here = pl.ds(pl.multiple_of(core * block, block), block)
    there = pl.ds(pl.multiple_of((1 - core) * block, block), block)
    copies = (
        pltpu.make_async_copy(keys_near.at[core], keys_ref.at[here], sems.at[0]),
        pltpu.make_async_copy(values_near.at[core], values_ref.at[here], sems.at[1]),
        pltpu.make_async_copy(keys_far.at[core], keys_ref.at[there], sems.at[2]),
        pltpu.make_async_copy(values_far.at[core], values_ref.at[there], sems.at[3]),
        pltpu.make_async_copy(proj_hbm.at[:, pl.ds(2 * width, width)], weight_ref, sems.at[4]),
    )
    for copy in copies:
        copy.start()
    pick_kernel(chosen_ref, gathered_ref, out_ref)
    for copy in copies:
        copy.wait()


def attend_kernel(kept_ref, came_ref, weight_ref, seen_ref, keys, values, out_ref, routed_ref):
    rows, width = out_ref.shape
    size = width // HEADS
    routed = kept_ref[...] + came_ref[...]
    routed_ref[...] = routed
    query = jax.nn.silu(
        jnp.dot(routed[:rows], weight_ref[...], preferred_element_type=jnp.float32)
    ).astype(jnp.bfloat16)
    query = query * jnp.bfloat16(0.5 * size ** (-0.5))
    lane = lax.broadcasted_iota(jnp.int32, (rows, LANES), 1)
    per_tile = LANES // size
    for tile in range(width // LANES):
        span = slice(tile * LANES, (tile + 1) * LANES)
        whole = query[:, span]
        joined = None
        for head in range(per_tile):
            mine = (lane >= head * size) & (lane < (head + 1) * size)
            part = jnp.where(mine, whole, jnp.zeros_like(whole))
            half = lax.dot_general(
                part, keys[:, span], (((1,), (1,)), ((), ())), preferred_element_type=jnp.float32
            ).astype(jnp.bfloat16)
            weight = half + half * jnp.tanh(half)
            event = lax.broadcasted_iota(jnp.int32, weight.shape, 1)
            weight = jnp.where(event < seen_ref[...], weight, jnp.zeros_like(weight))
            total = jnp.dot(weight, values[:, span], preferred_element_type=jnp.float32)
            joined = total if joined is None else jnp.where(mine, total, joined)
        out_ref[:, span] = joined.astype(out_ref.dtype)


IN_VMEM = pl.BlockSpec(memory_space=pltpu.VMEM)
IN_SMEM = pl.BlockSpec(memory_space=pltpu.SMEM)
IN_HBM = pl.BlockSpec(memory_space=pltpu.HBM)


def stay(array):
    return pltpu.with_memory_space_constraint(array, pltpu.HBM)


def call(kernel, name, outs, specs, scratch=(), vmem=24):
    many = isinstance(outs, tuple)
    return pl.pallas_call(
        kernel,
        out_shape=outs,
        in_specs=specs,
        out_specs=(IN_VMEM,) * len(outs) if many else IN_VMEM,
        scratch_shapes=scratch,
        compiler_params=pltpu.CompilerParams(vmem_limit_bytes=vmem * 2**20),
        name=name,
    )


def shaped(shape, dtype=jnp.bfloat16):
    return jax.ShapeDtypeStruct(shape, dtype)


def per_device(
    item_features,
    tower_in,
    tower_out,
    proj_weight,
    out_weight,
    hist_keys,
    hist_values,
    owner_of,
    row_in,
    hist_lengths,
    causal_offsets,
):
    width = tower_out.shape[1]
    devices = lax.axis_size("seq")
    me = lax.axis_index("seq")
    slot_count, users = row_in.shape
    assert users == 2 and devices % users == 0
    slots = slot_count * users
    rows = item_features.shape[0]
    hist_dev = hist_keys.shape[1]
    depth = max(2, 2 * slots // devices)
    room = devices * depth
    core = me % users
    swap = [(i, i ^ 1) for i in range(devices)]
    alike = [[b + users * k for k in range(devices // users)] for b in range(users)]

    half = devices // users
    cands = devices * slot_count

    codes = lax.all_to_all(
        call(
            functools.partial(code_kernel, depth, rows),
            "codes",
            shaped((devices, 1, slots), jnp.int32),
            [IN_HBM] * 2,
            [
                pltpu.VMEM((users, 1, slot_count), jnp.int32),
                pltpu.VMEM((users, slot_count), jnp.int32),
                pltpu.SemaphoreType.DMA((2,)),
            ],
        )(stay(owner_of.transpose(1, 2, 0)), stay(row_in.T)),
        "seq",
        split_axis=0,
        concat_axis=0,
        tiled=True,
    )

    keys_far = lax.ppermute(hist_keys, "seq", swap)
    values_far = lax.ppermute(hist_values, "seq", swap)

    hidden = jax.nn.silu(
        jnp.dot(item_features, tower_in, preferred_element_type=jnp.float32)
    ).astype(jnp.bfloat16)
    item_embed = jnp.dot(hidden, tower_out, preferred_element_type=jnp.float32).astype(jnp.bfloat16)

    handed = call(
        functools.partial(asked_kernel, depth),
        "asked",
        shaped((half, room, width)),
        [IN_VMEM] * 2,
        [pltpu.VMEM((room, rows), jnp.float32)],
    )(codes, item_embed)
    gathered = lax.all_to_all(
        handed, "seq", split_axis=0, concat_axis=0, tiled=True, axis_index_groups=alike
    ).reshape(half * room, width)

    chosen = shaped((cands + slot_count, half * room))
    events = users * hist_dev
    choose_sent, choose_kept, seen = call(
        functools.partial(ready_kernel, depth, rows, hist_dev),
        "ready",
        (chosen, chosen, shaped((cands, 1), jnp.int32)),
        [IN_SMEM] + [IN_VMEM] * 2,
    )(hist_lengths, codes, causal_offsets.T)

    taken = shaped((cands + slot_count, width))
    sent = call(pick_kernel, "pick", taken, [IN_VMEM] * 2)(choose_sent, gathered)
    came = lax.ppermute(sent, "seq", swap)
    kept, weight, keys, values = call(
        keep_kernel,
        "keep",
        (taken, shaped((width, width)), shaped((events, width)), shaped((events, width))),
        [IN_VMEM] * 2 + [IN_HBM] * 5,
        [pltpu.SemaphoreType.DMA((5,))],
    )(
        choose_kept,
        gathered,
        stay(hist_keys),
        stay(hist_values),
        stay(keys_far),
        stay(values_far),
        stay(proj_weight),
    )

    user_part, routed = call(
        attend_kernel,
        "attend",
        (shaped((cands, width)), shaped((cands + slot_count, width))),
        [IN_VMEM] * 6,
        vmem=48,
    )(kept, came, weight, seen, keys, values)
    backs = lax.all_to_all(
        user_part.reshape(devices, slot_count, width), "seq", split_axis=0, concat_axis=0, tiled=True
    )

    own_mine = lax.dynamic_slice_in_dim(routed, me * slot_count, slot_count, 0)
    own_other = routed[cands:]
    routed_own = jnp.where(
        core == 0,
        jnp.concatenate([own_mine, own_other]),
        jnp.concatenate([own_other, own_mine]),
    )
    proj = jax.nn.silu(jnp.dot(routed_own, proj_weight, preferred_element_type=jnp.float32))
    gate = proj[:, :width]
    value = proj[:, width : 2 * width].astype(jnp.bfloat16)
    query = proj[:, 2 * width : 3 * width].astype(jnp.bfloat16)
    key = proj[:, 3 * width :].astype(jnp.bfloat16)
    own = self_term(query, key, value)

    attended = jnp.sum(
        backs.astype(jnp.float32).reshape(devices // users, slots, width), axis=0
    )
    mixed = (layer_norm(attended + own) * gate).astype(jnp.bfloat16)
    result = routed_own.astype(jnp.float32) + jnp.dot(
        mixed, out_weight, preferred_element_type=jnp.float32
    )
    cand_out = result.astype(jnp.bfloat16).reshape(users, slot_count, width).transpose(1, 0, 2)
    return (item_embed, cand_out)


def solution(mesh):
    return jax.shard_map(
        per_device,
        mesh=mesh,
        in_specs=(
            P(("grp", "seq"), None),
            P(),
            P(),
            P(),
            P(),
            P("grp", "seq", None),
            P("grp", "seq", None),
            P(("grp", "seq"), None, None),
            P(("grp", "seq"), None),
            P("grp"),
            P("grp", None),
        ),
        out_specs=(P(("grp", "seq"), None), P(("grp", "seq"), None, None)),
        check_vma=False,
    )
```

time: 68.9 us -> 60.4 us (0.88)
  local copies, waits for them, and re-layouts: 12.7 us -> 1.78 us
  waiting for transfers between devices: 20.1 us -> 23.2 us
  other arithmetic: 2.22 us -> 0.48 us
  Pallas kernels: 11.4 us -> 12.6 us
    unnamed x23 -> x14, local copies, waits for them, and re-layouts: 5.62 us -> 0.68 us
    squeeze x4 -> x0, local copies, waits for them, and re-layouts: 3.58 us -> none  [the longest x3 3.5 us: of_user(): return lax.dynamic_index_in_dim(array, user, axis, keepdims=False)]
    all_to_all x1, waiting for transfers between devices: 9.87 us -> 12.9 us  [per_device(): lax.all_to_all(handed, 'seq', split_axis=0, concat_axis=0, tiled=True, ax...]
    pallas_call x5 -> x6, Pallas kernels: 11.4 us -> 12.6 us  [the longest x1 6.19 us: per_device(): call(attend_kernel, 'attend', (shaped((cands, width)), shaped((cands + sl...]
    slice x2 -> x0, local copies, waits for them, and re-layouts: 1.1 us -> none  [the longest x1 1.08 us: per_device(): proj_weight[:, 2 * width:3 * width]]
  transfers between devices with their start and end apart: 6 -> 6, of which waited for: 3 -> 3; matrix products, arithmetic and copies ran while one was open for 19% -> 10% of each run, Pallas kernels for 2% -> 11%
where the time goes in v3:
time: 60.4 us; the launch traced here: 60 us
  waiting for transfers between devices  23.2 us (38%)
  starting transfers between devices  15.4 us (25%)
  Pallas kernels  12.6 us (21%)
  matrix products  5.67 us (9%)
  local copies, waits for them, and re-layouts  1.78 us (3%)
  between operations  0.89 us (1%)
    all_to_all x1, waiting for transfers between devices, per_device(): lax.all_to_all(handed, 'seq', split_axis=0, concat_axis=0, tiled=True, ax...  12.9 us
    all_to_all x1, starting transfers between devices, per_device(): lax.all_to_all(call(functools.partial(code_kernel, depth, rows), 'codes',...  7.41 us
    all_to_all x1, waiting for transfers between devices, per_device(): lax.all_to_all(user_part.reshape(devices, slot_count, width), 'seq', spli...  7.26 us
    pallas_call x1, Pallas kernels, per_device(): call(attend_kernel, 'attend', (shaped((cands, width)), shaped((cands + sl...  6.19 us
    all_to_all x1, starting transfers between devices, per_device(): lax.all_to_all(user_part.reshape(devices, slot_count, width), 'seq', spli...  3.8 us
    all_to_all x1, starting transfers between devices, per_device(): lax.all_to_all(handed, 'seq', split_axis=0, concat_axis=0, tiled=True, ax...  3.49 us
    dot_general x1, matrix products, per_device(): jnp.dot(hidden, tower_out, preferred_element_type=jnp.float32)  3.3 us
    all_to_all x1, waiting for transfers between devices, per_device(): lax.all_to_all(call(functools.partial(code_kernel, depth, rows), 'codes',...  3.01 us
  transfers between devices with their start and end apart: 6, of which 3 were waited for; matrix products, arithmetic and copies ran while one was open for 10% of the time, Pallas kernels for 11%

profile of v3, /device:TPU:0, one launch (start us, length us, event | category | flops | bytes accessed | tf_op | source)
XLA Modules:
  0.0 60.0 jit_solution(11827775393751236133)
XLA Ops:
  0.6 0.0 copy-start
  0.6 0.6 collective-permute-start
  1.2 0.1 collective-permute-start.1
  1.3 1.5 %codes.1 = s32[16,1,32]{2,1,0:T(1,128)} custom-call(s32[2,1,16]{2,1,0:T(1,128)} %bitcast.24, s32[2,16]{1,0:T(2,128)} %bitcast.25), custom_call_target="tpu_custom_call" | custom-call | tf_op jit(solution)/shard_map/codes/pallas_call | solution.py:245
  2.8 7.4 %all-to-all-start = ((s32[16,1,32]{2,1,0:T(1,128)}), s32[16,1,32]{2,1,0:T(1,128)S(1)}, u32[]{:S(2)}, u32[]{:S(2)}) async-start(s32[16,1,32]{2,1,0:T(1,128)} %codes.1), calls=%async_computation | async-start | bytes 16384 | tf_op jit(solution)/shard_map/all_to_all | solution.py:244
  10.2 0.0 copy-start.4
  10.2 3.3 %convolution_convert_fusion.embed_ref = bf16[128,512]{1,0:T(8,128)(2,1)S(1)} fusion(bf16[2048,512]{1,0:T(8,128)(2,1)S(1)} %copy-done, bf16[128,1024]{1,0:T(8,128)(2,1)} %param.11, bf16[1024,2048]{1,0:T(8,128)(2,1)} %param.12), kind=kOutput, calls=%fused_computation | convolution fusion | flops 806682624 | bytes 6684672 | tf_op jit(solution)/shard_map/dot_general | solution.py:268
  13.6 0.0 copy-start.1
  13.6 3.0 %all-to-all-done.codes_ref = s32[16,1,32]{2,1,0:T(1,128)S(1)} async-done(((s32[16,1,32]{2,1,0:T(1,128)}), s32[16,1,32]{2,1,0:T(1,128)S(1)}, u32[]{:S(2)}, u32[]{:S(2)}) %all-to-all-start) | async-done | bytes 2080 | tf_op jit(solution)/shard_map/all_to_all | solution.py:244
  16.6 1.1 %asked.1 = bf16[8,64,512]{2,1,0:T(8,128)(2,1)} custom-call(s32[16,1,32]{2,1,0:T(1,128)S(1)} %all-to-all-done.codes_ref, bf16[128,512]{1,0:T(8,128)(2,1)S(1)} %convolution_convert_fusion.embed_ref), custom_call_target="tpu_custom_call" | custom-call | tf_op jit(solution)/shard_map/asked/pallas_call | solution.py:270
  17.6 3.5 %all-to-all-start.1 = ((bf16[8,64,512]{2,1,0:T(8,128)(2,1)}), bf16[8,64,512]{2,1,0:T(8,128)(2,1)S(1)}, u32[]{:S(2)}, u32[]{:S(2)}) async-start(bf16[8,64,512]{2,1,0:T(8,128)(2,1)} %asked.1), calls=%async_computation.1 | async-start | bytes 1048576 | tf_op jit(solution)/shard_map/all_to_all | solution.py:277
  21.2 1.1 %ready.1 = (bf16[272,512]{1,0:T(8,128)(2,1)S(1)}, bf16[272,512]{1,0:T(8,128)(2,1)S(1)}, s32[256,1]{1,0:T(8,128)S(1)}) custom-call(s32[2]{0:T(128)S(1)} %copy-done.5, s32[16,1,32]{2,1,0:T(1,128)S(1)} %all-to-all-done.codes_ref, s32[2,256]{1,0:T(2,128)S(1)} %bitcast.20), custom_call_target="tpu_custom_call" | custom-call | tf_op jit(solution)/shard_map/ready/pallas_call | solution.py:283
  22.3 0.6 %copy-done.2 = s32[256,1]{1,0:T(8,128)} copy-done((s32[256,1]{1,0:T(8,128)}, s32[256,1]{1,0:T(8,128)S(1)}, u32[]{:S(2)}) %copy-start.2) | copy-done | bytes 1048
  22.9 12.9 %all-to-all-done.1 = bf16[8,64,512]{2,1,0:T(8,128)(2,1)S(1)} async-done(((bf16[8,64,512]{2,1,0:T(8,128)(2,1)}), bf16[8,64,512]{2,1,0:T(8,128)(2,1)S(1)}, u32[]{:S(2)}, u32[]{:S(2)}) %all-to-all-start.1) | async-done | bytes 524320 | tf_op jit(solution)/shard_map/all_to_all | solution.py:277
  35.8 0.3 pick.1
  36.1 0.1 collective-permute-start.2
  36.2 2.4 %keep.1 = (bf16[272,512]{1,0:T(8,128)(2,1)S(1)}, bf16[512,512]{1,0:T(8,128)(2,1)S(1)}, bf16[2048,512]{1,0:T(8,128)(2,1)S(1)}, bf16[2048,512]{1,0:T(8,128)(2,1)S(1)}) custom-call(bf16[272,512]{1,0:T(8,128)(2,1)S(1)} %get-tuple-element.11.chosen_ref, bf16[512,512]{1,0:T(8,128)(2,1)S(1)} %bitcast.19, bf16[2,1024,512]{2,1,0:T(8,128)(2,1)} %keys_near.1, ...), custom_call_target="tpu_custom_call" | custom-call | tf_op jit(solution)/shard_map/keep/pallas_call | solution.py:293
  38.7 6.2 %attend.1 = (bf16[256,512]{1,0:T(8,128)(2,1)}, bf16[272,512]{1,0:T(8,128)(2,1)S(1)}) custom-call(bf16[272,512]{1,0:T(8,128)(2,1)S(1)} %get-tuple-element.12.kept_ref, bf16[272,512]{1,0:T(8,128)(2,1)S(1)} %collective-permute-done.2.came_ref, bf16[512,512]{1,0:T(8,128)(2,1)S(1)} %get-tuple-element.14.weight_ref, s32[256,1]{1,0:T(8,128)S(1)} %copy-done.3, ...), custom_call_target="tpu_custom_call" | custom-call | tf_op jit(solution)/shard_map/attend/pallas_call | solution.py:309
  44.9 3.8 %all-to-all-start.2 = ((bf16[16,16,512]{2,1,0:T(8,128)(2,1)}), bf16[16,16,512]{2,1,0:T(8,128)(2,1)S(1)}, u32[]{:S(2)}, u32[]{:S(2)}) async-start(bf16[16,16,512]{2,1,0:T(8,128)(2,1)} %bitcast.4), calls=%async_computation.2 | async-start | bytes 524288 | tf_op jit(solution)/shard_map/all_to_all | solution.py:316
  48.7 0.0 copy-start.6
  48.7 2.1 %fusion.10 = (bf16[32,2048]{1,0:T(8,128)(2,1)S(1)}, f32[32,2048]{1,0:T(8,128)S(1)}) fusion(bf16[512,2048]{1,0:T(8,128)(2,1)} %proj_hbm.1, bf16[16,512]{1,0:T(8,128)(2,1)S(1)} %get-tuple-element.23, bf16[16,512]{1,0:T(8,128)(2,1)S(1)} %get-tuple-element.22, pred[]{:T(512)S(6)} %eq.5), kind=kOutput, calls=%fused_computation.24 | convolution fusion | flops 67584000 | bytes 2523137 | tf_op jit(solution)/shard_map/dot_general | solution.py:327
  50.9 0.1 mul.64
  51.0 0.1 reduce_sum.37
  51.1 0.1 copy.16
  51.1 0.1 copy.17
  51.2 0.1 mul.68
  51.3 0.1 mul.69
  51.4 7.3 %all-to-all-done.2 = bf16[16,16,512]{2,1,0:T(8,128)(2,1)S(1)} async-done(((bf16[16,16,512]{2,1,0:T(8,128)(2,1)}), bf16[16,16,512]{2,1,0:T(8,128)(2,1)S(1)}, u32[]{:S(2)}, u32[]{:S(2)}) %all-to-all-start.2) | async-done | bytes 262176 | tf_op jit(solution)/shard_map/all_to_all | solution.py:316
  58.7 0.1 fusion.9
  58.9 0.2 multiply_reduce_fusion
  59.1 0.2 fusion
  59.3 0.7 %copy.20 = bf16[2,16,512]{2,0,1:T(2,128)(2,1)} copy(bf16[2,16,512]{2,1,0:T(8,128)(2,1)S(1)} %bitcast.22) | data formatting | bytes 65536 | tf_op jit(solution)/shard_map/reshape | solution.py:341
  (18 shorter events, 0.1 us)
Async XLA Ops:
  0.6 9.6 %copy-start = (bf16[2048,512]{1,0:T(8,128)(2,1)S(1)}, bf16[2048,512]{1,0:T(8,128)(2,1)}, u32[]{:S(2)}) copy-start(bf16[2048,512]{1,0:T(8,128)(2,1)} %param.13) | copy-start | bytes 6291460
  0.6 35.5 %collective-permute-start = (bf16[2,1024,512]{2,1,0:T(8,128)(2,1)}, bf16[2,1024,512]{2,1,0:T(8,128)(2,1)}, u32[]{:S(2)}, u32[]{:S(2)}) collective-permute-start(bf16[2,1024,512]{2,1,0:T(8,128)(2,1)} %keys_near.1), channel_id=1, source_target_pairs={{0,1},{1,0},{2,3},{3,2},{4,5},{5,4},{6,7},{7,6},{8,9},{9,8},{10,11... | collective-permute-start | bytes 6291464 | tf_op jit(solution)/shard_map/ppermute | solution.py:262
  1.2 35.0 %collective-permute-start.1 = (bf16[2,1024,512]{2,1,0:T(8,128)(2,1)}, bf16[2,1024,512]{2,1,0:T(8,128)(2,1)}, u32[]{:S(2)}, u32[]{:S(2)}) collective-permute-start(bf16[2,1024,512]{2,1,0:T(8,128)(2,1)} %values_near.1), channel_id=1, source_target_pairs={{0,1},{1,0},{2,3},{3,2},{4,5},{5,4},{6,7},{7,6},{8,9},{9,8},{10,11... | collective-permute-start | bytes 6291464 | tf_op jit(solution)/shard_map/ppermute | solution.py:263
  2.8 13.8 %all-to-all-start = ((s32[16,1,32]{2,1,0:T(1,128)}), s32[16,1,32]{2,1,0:T(1,128)S(1)}, u32[]{:S(2)}, u32[]{:S(2)}) async-start(s32[16,1,32]{2,1,0:T(1,128)} %codes.1), calls=%async_computation | async-start | bytes 16384 | tf_op jit(solution)/shard_map/all_to_all | solution.py:244
  10.2 10.9 %copy-start.4 = (s32[256,2]{0,1:T(2,128)S(1)}, s32[256,2]{0,1:T(2,128)}, u32[]{:S(2)}) copy-start(s32[256,2]{0,1:T(2,128)} %param.21) | copy-start | bytes 6148
  10.2 10.9 %copy-start.5 = (s32[2]{0:T(128)S(1)}, s32[2]{0:T(128)}, u32[]{:S(2)}) copy-start(s32[2]{0:T(128)} %lengths_ref.1) | copy-start | bytes 28
  13.6 4.1 %copy-start.1 = (bf16[128,512]{1,0:T(8,128)(2,1)}, bf16[128,512]{1,0:T(8,128)(2,1)S(1)}, u32[]{:S(2)}) copy-start(bf16[128,512]{1,0:T(8,128)(2,1)S(1)} %convolution_convert_fusion.embed_ref) | copy-start | bytes 393220
  17.6 18.1 %all-to-all-start.1 = ((bf16[8,64,512]{2,1,0:T(8,128)(2,1)}), bf16[8,64,512]{2,1,0:T(8,128)(2,1)S(1)}, u32[]{:S(2)}, u32[]{:S(2)}) async-start(bf16[8,64,512]{2,1,0:T(8,128)(2,1)} %asked.1), calls=%async_computation.1 | async-start | bytes 1048576 | tf_op jit(solution)/shard_map/all_to_all | solution.py:277
  22.2 0.7 %copy-start.2 = (s32[256,1]{1,0:T(8,128)}, s32[256,1]{1,0:T(8,128)S(1)}, u32[]{:S(2)}) copy-start(s32[256,1]{1,0:T(8,128)S(1)} %get-tuple-element.15.seen_ref) | copy-start | bytes 3076
  36.1 2.6 %collective-permute-start.2 = (bf16[272,512]{1,0:T(8,128)(2,1)S(1)}, bf16[272,512]{1,0:T(8,128)(2,1)S(1)}, u32[]{:S(2)}, u32[]{:S(2)}) collective-permute-start(bf16[272,512]{1,0:T(8,128)(2,1)S(1)} %pick.1), channel_id=1, source_target_pairs={{0,1},{1,0},{2,3},{3,2},{4,5},{5,4},{6,7},{7,6},{8,9},{9,8},{10,11... | collective-permute-start | bytes 835592 | tf_op jit(solution)/shard_map/ppermute | solution.py:292
  36.2 2.5 %copy-start.3 = (s32[256,1]{1,0:T(8,128)S(1)}, s32[256,1]{1,0:T(8,128)}, u32[]{:S(2)}) copy-start(s32[256,1]{1,0:T(8,128)} %copy-done.2) | copy-start | bytes 3076
  44.9 13.8 %all-to-all-start.2 = ((bf16[16,16,512]{2,1,0:T(8,128)(2,1)}), bf16[16,16,512]{2,1,0:T(8,128)(2,1)S(1)}, u32[]{:S(2)}, u32[]{:S(2)}) async-start(bf16[16,16,512]{2,1,0:T(8,128)(2,1)} %bitcast.4), calls=%async_computation.2 | async-start | bytes 524288 | tf_op jit(solution)/shard_map/all_to_all | solution.py:316
  48.7 10.4 %copy-start.6 = (bf16[512,512]{1,0:T(8,128)(2,1)S(1)}, bf16[512,512]{1,0:T(8,128)(2,1)}, u32[]{:S(2)}) copy-start(bf16[512,512]{1,0:T(8,128)(2,1)} %param.15) | copy-start | bytes 1572868

commit v4 on v3

--- a/solution.py
+++ b/solution.py
@@ -6,6 +6,7 @@
 from jax.experimental import pallas as pl
 from jax.experimental.pallas import tpu as pltpu
 from jax.sharding import PartitionSpec as P
+
 
 HEADS = 8
 LANES = 128
@@ -24,6 +25,23 @@
     v_heads = value.astype(jnp.float32).reshape(rows, HEADS, size)
     score = jnp.sum(q_heads * k_heads, axis=-1) * size ** (-0.5)
     return (jax.nn.silu(score)[:, :, None] * v_heads).reshape(rows, width)
+
+
+def ring_order(chips):
+    ring = list(range(0, chips, 2)) + list(range(1, chips, 2))[::-1]
+    start = ring.index(min(chips - 1, (chips // 2) | 1))
+    return ring[start:] + ring[:start]
+
+
+def middle_order(chips):
+    return sorted(range(chips), key=lambda chip: abs(2 * (chip - chips // 2) + 0.5))
+
+
+def place_in(order, chip):
+    place = jnp.zeros_like(chip)
+    for number, other in enumerate(order):
+        place = jnp.where(chip == other, number, place)
+    return place
 
 
 def code_kernel(depth, rows, owner_hbm, row_hbm, out_ref, owner_ref, row_ref, sems):
@@ -47,7 +65,7 @@
     out_ref[...] = jnp.broadcast_to(code[None], out_ref.shape)
 
 
-def asked_kernel(depth, codes_ref, embed_ref, out_ref, chosen_ref):
+def asked_kernel(depth, codes_ref, embed_ref, out_hbm, chosen_ref, picked_ref, sems):
     devices, _, slots = codes_ref.shape
     rows = embed_ref.shape[0]
     want = lax.axis_index("seq") * depth + lax.broadcasted_iota(jnp.int32, (depth, slots), 0)
@@ -57,11 +75,17 @@
         hit = lax.div(codes, rows) == want
         asked = jnp.sum(jnp.where(hit, lax.rem(codes, rows), 0), axis=1, keepdims=True)
         chosen_ref[asker * depth : (asker + 1) * depth, :] = (lane == asked).astype(jnp.float32)
-    picked = jnp.dot(
+    picked_ref[...] = jnp.dot(
         chosen_ref[...].astype(jnp.bfloat16), embed_ref[...], preferred_element_type=jnp.float32
     ).astype(jnp.bfloat16)
-    for receiver in range(out_ref.shape[0]):
-        out_ref[receiver] = picked
+    copies = [
+        pltpu.make_async_copy(picked_ref, out_hbm.at[receiver], sems.at[receiver])
+        for receiver in range(out_hbm.shape[0])
+    ]
+    for copy in copies:
+        copy.start()
+    for copy in copies:
+        copy.wait()
 
 
 def column(row, height):
@@ -74,6 +98,8 @@
     depth,
     rows,
     block,
+    order,
+    handing,
     lengths_ref,
     codes_ref,
     offsets_ref,
@@ -87,12 +113,13 @@
     room = devices * depth
     me = lax.axis_index("seq")
     core = lax.rem(me, users)
+    mine_at = place_in(order, lax.div(me, users)) * users + core
     asker = lax.broadcasted_iota(jnp.int32, codes_ref.shape, 0)
     places = lax.div(codes_ref[...], rows)
     owner = lax.div(places, depth)
     spots = jnp.where(
         lax.rem(owner, users) == core,
-        lax.div(owner, users) * room + asker * depth + lax.rem(places, depth),
+        place_in(handing, lax.div(owner, users)) * room + asker * depth + lax.rem(places, depth),
         -1,
     )
     first = spots[:, :, :slot_count]
@@ -106,8 +133,8 @@
     cands = devices * slot_count
     blank = jnp.zeros((1, LANES - slot_count), jnp.int32)
     for chosen_ref, all_of, extra in (
-        (sent_ref, other, one(mine, me + 1 - 2 * core)),
-        (kept_ref, mine, one(other, me)),
+        (sent_ref, other, one(mine, mine_at + 1 - 2 * core)),
+        (kept_ref, mine, one(other, mine_at)),
     ):
         row = jnp.concatenate([all_of[r] for r in range(devices)] + [extra, blank], axis=1)
         spot = column(row, cands + slot_count)
@@ -115,6 +142,13 @@
         chosen_ref[...] = (place == spot).astype(jnp.float32).astype(jnp.bfloat16)
 
     offsets = jnp.where(core == 0, offsets_ref[0:1, :], offsets_ref[1:2, :])
+    offsets = jnp.concatenate(
+        [
+            offsets[:, slot_count * device : slot_count * (device + 1)]
+            for device in (users * chip + other for chip in order for other in range(users))
+        ],
+        axis=1,
+    )
     seen_ref[...] = column(lengths_ref[core] - (me - core) * block - offsets, cands)
 
 
@@ -165,6 +199,8 @@
         jnp.dot(routed[:rows], weight_ref[...], preferred_element_type=jnp.float32)
     ).astype(jnp.bfloat16)
     query = query * jnp.bfloat16(0.5 * size ** (-0.5))
+    event = lax.broadcasted_iota(jnp.int32, (rows, keys.shape[0]), 1)
+    shown = (event < seen_ref[...]).astype(jnp.float32).astype(jnp.bfloat16)
     lane = lax.broadcasted_iota(jnp.int32, (rows, LANES), 1)
     per_tile = LANES // size
     for tile in range(width // LANES):
@@ -178,8 +214,7 @@
                 part, keys[:, span], (((1,), (1,)), ((), ())), preferred_element_type=jnp.float32
             ).astype(jnp.bfloat16)
             weight = half + half * jnp.tanh(half)
-            event = lax.broadcasted_iota(jnp.int32, weight.shape, 1)
-            weight = jnp.where(event < seen_ref[...], weight, jnp.zeros_like(weight))
+            weight = weight * shown
             total = jnp.dot(weight, values[:, span], preferred_element_type=jnp.float32)
             joined = total if joined is None else jnp.where(mine, total, joined)
         out_ref[:, span] = joined.astype(out_ref.dtype)
@@ -194,16 +229,15 @@
     return pltpu.with_memory_space_constraint(array, pltpu.HBM)
 
 
-def call(kernel, name, outs, specs, scratch=(), vmem=24):
+def call(kernel, outs, specs, scratch=(), vmem=24, out_space=IN_VMEM):
     many = isinstance(outs, tuple)
     return pl.pallas_call(
         kernel,
         out_shape=outs,
         in_specs=specs,
-        out_specs=(IN_VMEM,) * len(outs) if many else IN_VMEM,
+        out_specs=(out_space,) * len(outs) if many else out_space,
         scratch_shapes=scratch,
         compiler_params=pltpu.CompilerParams(vmem_limit_bytes=vmem * 2**20),
-        name=name,
     )
 
 
@@ -236,15 +270,17 @@
     room = devices * depth
     core = me % users
     swap = [(i, i ^ 1) for i in range(devices)]
-    alike = [[b + users * k for k in range(devices // users)] for b in range(users)]
-
     half = devices // users
+    order = ring_order(half)
+    handing = middle_order(half)
+    everyone = [[users * chip + other for chip in order for other in range(users)]]
+    alike = [[users * chip + other for chip in handing] for other in range(users)]
+    mine_at = place_in(order, me // users) * users + core
     cands = devices * slot_count
 
     codes = lax.all_to_all(
         call(
             functools.partial(code_kernel, depth, rows),
-            "codes",
             shaped((devices, 1, slots), jnp.int32),
             [IN_HBM] * 2,
             [
@@ -257,6 +293,7 @@
         split_axis=0,
         concat_axis=0,
         tiled=True,
+        axis_index_groups=everyone,
     )
 
     keys_far = lax.ppermute(hist_keys, "seq", swap)
@@ -269,30 +306,33 @@
 
     handed = call(
         functools.partial(asked_kernel, depth),
-        "asked",
         shaped((half, room, width)),
         [IN_VMEM] * 2,
-        [pltpu.VMEM((room, rows), jnp.float32)],
+        [
+            pltpu.VMEM((room, rows), jnp.float32),
+            pltpu.VMEM((room, width), jnp.bfloat16),
+            pltpu.SemaphoreType.DMA((half,)),
+        ],
+        out_space=IN_HBM,
     )(codes, item_embed)
     gathered = lax.all_to_all(
         handed, "seq", split_axis=0, concat_axis=0, tiled=True, axis_index_groups=alike
-    ).reshape(half * room, width)
+    )
+    gathered = gathered.reshape(half * room, width)
 
     chosen = shaped((cands + slot_count, half * room))
     events = users * hist_dev
     choose_sent, choose_kept, seen = call(
-        functools.partial(ready_kernel, depth, rows, hist_dev),
-        "ready",
+        functools.partial(ready_kernel, depth, rows, hist_dev, order, handing),
         (chosen, chosen, shaped((cands, 1), jnp.int32)),
         [IN_SMEM] + [IN_VMEM] * 2,
     )(hist_lengths, codes, causal_offsets.T)
 
     taken = shaped((cands + slot_count, width))
-    sent = call(pick_kernel, "pick", taken, [IN_VMEM] * 2)(choose_sent, gathered)
+    sent = call(pick_kernel, taken, [IN_VMEM] * 2)(choose_sent, gathered)
     came = lax.ppermute(sent, "seq", swap)
     kept, weight, keys, values = call(
         keep_kernel,
-        "keep",
         (taken, shaped((width, width)), shaped((events, width)), shaped((events, width))),
         [IN_VMEM] * 2 + [IN_HBM] * 5,
         [pltpu.SemaphoreType.DMA((5,))],
@@ -308,16 +348,20 @@
 
     user_part, routed = call(
         attend_kernel,
-        "attend",
         (shaped((cands, width)), shaped((cands + slot_count, width))),
         [IN_VMEM] * 6,
         vmem=48,
     )(kept, came, weight, seen, keys, values)
     backs = lax.all_to_all(
-        user_part.reshape(devices, slot_count, width), "seq", split_axis=0, concat_axis=0, tiled=True
-    )
-
-    own_mine = lax.dynamic_slice_in_dim(routed, me * slot_count, slot_count, 0)
+        user_part.reshape(devices, slot_count, width),
+        "seq",
+        split_axis=0,
+        concat_axis=0,
+        tiled=True,
+        axis_index_groups=everyone,
+    )
+
+    own_mine = lax.dynamic_slice_in_dim(routed, mine_at * slot_count, slot_count, 0)
     own_other = routed[cands:]
     routed_own = jnp.where(
         core == 0,

time: 60.4 us -> 55.2 us (0.914)
  the two profiles are of different devices: /device:TPU:0 before, /device:TPU:1 now
where the time goes in v4:
time: 55.2 us; the launch traced here: 54.8 us
  starting transfers between devices  20.2 us (37%)
  waiting for transfers between devices  13.6 us (25%)
  Pallas kernels  12.2 us (22%)
  matrix products  5.66 us (10%)
  local copies, waits for them, and re-layouts  1.78 us (3%)
  between operations  0.83 us (2%)
    all_to_all x1, waiting for transfers between devices, per_device(): lax.all_to_all(handed, 'seq', split_axis=0, concat_axis=0, tiled=True, ax...  9.46 us
    all_to_all x1, starting transfers between devices, per_device(): lax.all_to_all(call(functools.partial(code_kernel, depth, rows), shaped((...  7.96 us
    pallas_call x1, Pallas kernels, per_device(): call(attend_kernel, (shaped((cands, width)), shaped((cands + slot_count,...  5.58 us
    all_to_all x1, starting transfers between devices, per_device(): lax.all_to_all(user_part.reshape(devices, slot_count, width), 'seq', spli...  5.22 us
    all_to_all x1, waiting for transfers between devices, per_device(): lax.all_to_all(user_part.reshape(devices, slot_count, width), 'seq', spli...  4.15 us
    all_to_all x1, starting transfers between devices, per_device(): lax.all_to_all(handed, 'seq', split_axis=0, concat_axis=0, tiled=True, ax...  4.14 us
    dot_general x1, matrix products, per_device(): jnp.dot(hidden, tower_out, preferred_element_type=jnp.float32)  3.29 us
    pallas_call x1, Pallas kernels, per_device(): call(keep_kernel, (taken, shaped((width, width)), shaped((events, width))...  2.42 us
  transfers between devices with their start and end apart: 6, of which 2 were waited for; matrix products, arithmetic and copies ran while one was open for 11% of the time, Pallas kernels for 12%

profile of v4, /device:TPU:1, one launch (start us, length us, event | category | flops | bytes accessed | tf_op | source)
XLA Modules:
  0.0 54.8 jit_solution(5761495501484553941)
XLA Ops:
  0.6 0.0 copy-start
  0.6 0.1 collective-permute-start
  0.7 0.5 collective-permute-start.1
  1.2 1.6 %shard_map.122 = s32[16,1,32]{2,1,0:T(1,128)} custom-call(s32[2,1,16]{2,1,0:T(1,128)} %bitcast.24, s32[2,16]{1,0:T(2,128)} %bitcast.25), custom_call_target="tpu_custom_call" | custom-call | tf_op jit(solution)/shard_map/pallas_call | solution.py:282
  2.8 8.0 %all-to-all-start = ((s32[16,1,32]{2,1,0:T(1,128)}), s32[16,1,32]{2,1,0:T(1,128)S(1)}, u32[]{:S(2)}, u32[]{:S(2)}) async-start(s32[16,1,32]{2,1,0:T(1,128)} %shard_map.122), calls=%async_computation | async-start | bytes 16384 | tf_op jit(solution)/shard_map/all_to_all | solution.py:281
  10.7 0.0 copy-start.4
  10.8 0.0 copy-start.5
  10.8 3.3 %convolution_convert_fusion.embed_ref = bf16[128,512]{1,0:T(8,128)(2,1)S(1)} fusion(bf16[2048,512]{1,0:T(8,128)(2,1)S(1)} %copy-done, bf16[128,1024]{1,0:T(8,128)(2,1)} %param.11, bf16[1024,2048]{1,0:T(8,128)(2,1)} %param.12), kind=kOutput, calls=%fused_computation | convolution fusion | flops 806682624 | bytes 6684672 | tf_op jit(solution)/shard_map/dot_general | solution.py:305
  14.1 0.0 copy-start.1
  14.1 0.0 all-to-all-done.codes_ref
  14.1 1.1 %shard_map.124 = bf16[8,64,512]{2,1,0:T(8,128)(2,1)} custom-call(s32[16,1,32]{2,1,0:T(1,128)S(1)} %all-to-all-done.codes_ref, bf16[128,512]{1,0:T(8,128)(2,1)S(1)} %convolution_convert_fusion.embed_ref), custom_call_target="tpu_custom_call" | custom-call | tf_op jit(solution)/shard_map/pallas_call | solution.py:307
  15.2 4.1 %all-to-all-start.1 = ((bf16[8,64,512]{2,1,0:T(8,128)(2,1)}), bf16[8,64,512]{2,1,0:T(8,128)(2,1)S(1)}, u32[]{:S(2)}, u32[]{:S(2)}) async-start(bf16[8,64,512]{2,1,0:T(8,128)(2,1)} %shard_map.124), calls=%async_computation.1 | async-start | bytes 1048576 | tf_op jit(solution)/shard_map/all_to_all | solution.py:318
  19.4 1.2 %shard_map.123 = (bf16[272,512]{1,0:T(8,128)(2,1)S(1)}, bf16[272,512]{1,0:T(8,128)(2,1)S(1)}, s32[256,1]{1,0:T(8,128)S(1)}) custom-call(s32[2]{0:T(128)S(1)} %copy-done.5, s32[16,1,32]{2,1,0:T(1,128)S(1)} %all-to-all-done.codes_ref, s32[2,256]{1,0:T(2,128)S(1)} %bitcast.20), custom_call_target="tpu_custom_call" | custom-call | tf_op jit(solution)/shard_map/pallas_call | solution.py:325
  20.6 0.6 %copy-done.2 = s32[256,1]{1,0:T(8,128)} copy-done((s32[256,1]{1,0:T(8,128)}, s32[256,1]{1,0:T(8,128)S(1)}, u32[]{:S(2)}) %copy-start.2) | copy-done | bytes 1048
  21.2 9.5 %all-to-all-done.1 = bf16[8,64,512]{2,1,0:T(8,128)(2,1)S(1)} async-done(((bf16[8,64,512]{2,1,0:T(8,128)(2,1)}), bf16[8,64,512]{2,1,0:T(8,128)(2,1)S(1)}, u32[]{:S(2)}, u32[]{:S(2)}) %all-to-all-start.1) | async-done | bytes 524320 | tf_op jit(solution)/shard_map/all_to_all | solution.py:318
  30.7 0.3 shard_map.126
  31.0 2.3 %collective-permute-start.2 = (bf16[272,512]{1,0:T(8,128)(2,1)S(1)}, bf16[272,512]{1,0:T(8,128)(2,1)S(1)}, u32[]{:S(2)}, u32[]{:S(2)}) collective-permute-start(bf16[272,512]{1,0:T(8,128)(2,1)S(1)} %shard_map.126), channel_id=1, source_target_pairs={{0,1},{1,0},{2,3},{3,2},{4,5},{5,4},{6,7},{7,6},{8,9},{9,8},{10,11... | collective-permute-start | bytes 835592 | tf_op jit(solution)/shard_map/ppermute | solution.py:333
  33.3 2.4 %shard_map.125 = (bf16[272,512]{1,0:T(8,128)(2,1)S(1)}, bf16[512,512]{1,0:T(8,128)(2,1)S(1)}, bf16[2048,512]{1,0:T(8,128)(2,1)S(1)}, bf16[2048,512]{1,0:T(8,128)(2,1)S(1)}) custom-call(bf16[272,512]{1,0:T(8,128)(2,1)S(1)} %get-tuple-element.11.chosen_ref, bf16[512,512]{1,0:T(8,128)(2,1)S(1)} %bitcast.19, bf16[2,1024,512]{2,1,0:T(8,128)(2,1)} %keys_near.1, ...), custom_call_target="tpu_custom_call" | custom-call | tf_op jit(solution)/shard_map/pallas_call | solution.py:334
  35.8 5.6 %shard_map.127 = (bf16[256,512]{1,0:T(8,128)(2,1)}, bf16[272,512]{1,0:T(8,128)(2,1)S(1)}) custom-call(bf16[272,512]{1,0:T(8,128)(2,1)S(1)} %get-tuple-element.12.kept_ref, bf16[272,512]{1,0:T(8,128)(2,1)S(1)} %collective-permute-done.2.came_ref, bf16[512,512]{1,0:T(8,128)(2,1)S(1)} %get-tuple-element.14.weight_ref, s32[256,1]{1,0:T(8,128)S(1)} %copy-done.3, ...), custom_call_target="tpu_custom_call" | custom-call | tf_op jit(solution)/shard_map/pallas_call | solution.py:349
  41.4 5.2 %all-to-all-start.2 = ((bf16[16,16,512]{2,1,0:T(8,128)(2,1)}), bf16[16,16,512]{2,1,0:T(8,128)(2,1)S(1)}, u32[]{:S(2)}, u32[]{:S(2)}) async-start(bf16[16,16,512]{2,1,0:T(8,128)(2,1)} %bitcast.4), calls=%async_computation.2 | async-start | bytes 524288 | tf_op jit(solution)/shard_map/all_to_all | solution.py:355
  46.6 2.1 %fusion.10 = (bf16[32,2048]{1,0:T(8,128)(2,1)S(1)}, f32[32,2048]{1,0:T(8,128)S(1)}) fusion(bf16[512,2048]{1,0:T(8,128)(2,1)} %proj_hbm.1, bf16[16,512]{1,0:T(8,128)(2,1)S(1)} %get-tuple-element.23, bf16[16,512]{1,0:T(8,128)(2,1)S(1)} %get-tuple-element.22, pred[]{:T(512)S(6)} %eq.27), kind=kOutput, calls=%fused_computation.24 | convolution fusion | flops 67584000 | bytes 2523137 | tf_op jit(solution)/shard_map/dot_general | solution.py:371
  48.8 0.1 mul.68
  48.9 0.1 reduce_sum.37
  49.0 0.1 copy.16
  49.1 0.1 copy.17
  49.1 0.1 mul.72
  49.3 0.1 mul.73
  49.3 4.2 %all-to-all-done.2 = bf16[16,16,512]{2,1,0:T(8,128)(2,1)S(1)} async-done(((bf16[16,16,512]{2,1,0:T(8,128)(2,1)}), bf16[16,16,512]{2,1,0:T(8,128)(2,1)S(1)}, u32[]{:S(2)}, u32[]{:S(2)}) %all-to-all-start.2) | async-done | bytes 262176 | tf_op jit(solution)/shard_map/all_to_all | solution.py:355
  53.5 0.1 fusion.9
  53.7 0.2 multiply_reduce_fusion
  53.9 0.2 fusion
  54.1 0.7 %copy.20 = bf16[2,16,512]{2,0,1:T(2,128)(2,1)} copy(bf16[2,16,512]{2,1,0:T(8,128)(2,1)S(1)} %bitcast.22) | data formatting | bytes 65536 | tf_op jit(solution)/shard_map/reshape | solution.py:385
  (18 shorter events, 0.1 us)
Async XLA Ops:
  0.6 10.1 %copy-start = (bf16[2048,512]{1,0:T(8,128)(2,1)S(1)}, bf16[2048,512]{1,0:T(8,128)(2,1)}, u32[]{:S(2)}) copy-start(bf16[2048,512]{1,0:T(8,128)(2,1)} %param.13) | copy-start | bytes 6291460
  0.6 32.7 %collective-permute-start = (bf16[2,1024,512]{2,1,0:T(8,128)(2,1)}, bf16[2,1024,512]{2,1,0:T(8,128)(2,1)}, u32[]{:S(2)}, u32[]{:S(2)}) collective-permute-start(bf16[2,1024,512]{2,1,0:T(8,128)(2,1)} %keys_near.1), channel_id=1, source_target_pairs={{0,1},{1,0},{2,3},{3,2},{4,5},{5,4},{6,7},{7,6},{8,9},{9,8},{10,11... | collective-permute-start | bytes 6291464 | tf_op jit(solution)/shard_map/ppermute | solution.py:299
  0.7 32.6 %collective-permute-start.1 = (bf16[2,1024,512]{2,1,0:T(8,128)(2,1)}, bf16[2,1024,512]{2,1,0:T(8,128)(2,1)}, u32[]{:S(2)}, u32[]{:S(2)}) collective-permute-start(bf16[2,1024,512]{2,1,0:T(8,128)(2,1)} %values_near.1), channel_id=1, source_target_pairs={{0,1},{1,0},{2,3},{3,2},{4,5},{5,4},{6,7},{7,6},{8,9},{9,8},{10,11... | collective-permute-start | bytes 6291464 | tf_op jit(solution)/shard_map/ppermute | solution.py:300
  2.8 11.3 %all-to-all-start = ((s32[16,1,32]{2,1,0:T(1,128)}), s32[16,1,32]{2,1,0:T(1,128)S(1)}, u32[]{:S(2)}, u32[]{:S(2)}) async-start(s32[16,1,32]{2,1,0:T(1,128)} %shard_map.122), calls=%async_computation | async-start | bytes 16384 | tf_op jit(solution)/shard_map/all_to_all | solution.py:281
  10.7 8.6 %copy-start.4 = (s32[256,2]{0,1:T(2,128)S(1)}, s32[256,2]{0,1:T(2,128)}, u32[]{:S(2)}) copy-start(s32[256,2]{0,1:T(2,128)} %param.21) | copy-start | bytes 6148
  10.8 8.6 %copy-start.5 = (s32[2]{0:T(128)S(1)}, s32[2]{0:T(128)}, u32[]{:S(2)}) copy-start(s32[2]{0:T(128)} %lengths_ref.1) | copy-start | bytes 28
  14.1 1.2 %copy-start.1 = (bf16[128,512]{1,0:T(8,128)(2,1)}, bf16[128,512]{1,0:T(8,128)(2,1)S(1)}, u32[]{:S(2)}) copy-start(bf16[128,512]{1,0:T(8,128)(2,1)S(1)} %convolution_convert_fusion.embed_ref) | copy-start | bytes 393220
  15.2 15.4 %all-to-all-start.1 = ((bf16[8,64,512]{2,1,0:T(8,128)(2,1)}), bf16[8,64,512]{2,1,0:T(8,128)(2,1)S(1)}, u32[]{:S(2)}, u32[]{:S(2)}) async-start(bf16[8,64,512]{2,1,0:T(8,128)(2,1)} %shard_map.124), calls=%async_computation.1 | async-start | bytes 1048576 | tf_op jit(solution)/shard_map/all_to_all | solution.py:318
  20.6 0.7 %copy-start.2 = (s32[256,1]{1,0:T(8,128)}, s32[256,1]{1,0:T(8,128)S(1)}, u32[]{:S(2)}) copy-start(s32[256,1]{1,0:T(8,128)S(1)} %get-tuple-element.15.seen_ref) | copy-start | bytes 3076
  31.0 4.8 %collective-permute-start.2 = (bf16[272,512]{1,0:T(8,128)(2,1)S(1)}, bf16[272,512]{1,0:T(8,128)(2,1)S(1)}, u32[]{:S(2)}, u32[]{:S(2)}) collective-permute-start(bf16[272,512]{1,0:T(8,128)(2,1)S(1)} %shard_map.126), channel_id=1, source_target_pairs={{0,1},{1,0},{2,3},{3,2},{4,5},{5,4},{6,7},{7,6},{8,9},{9,8},{10,11... | collective-permute-start | bytes 835592 | tf_op jit(solution)/shard_map/ppermute | solution.py:333
  33.3 2.5 %copy-start.3 = (s32[256,1]{1,0:T(8,128)S(1)}, s32[256,1]{1,0:T(8,128)}, u32[]{:S(2)}) copy-start(s32[256,1]{1,0:T(8,128)} %copy-done.2) | copy-start | bytes 3076
  41.4 12.1 %all-to-all-start.2 = ((bf16[16,16,512]{2,1,0:T(8,128)(2,1)}), bf16[16,16,512]{2,1,0:T(8,128)(2,1)S(1)}, u32[]{:S(2)}, u32[]{:S(2)}) async-start(bf16[16,16,512]{2,1,0:T(8,128)(2,1)} %bitcast.4), calls=%async_computation.2 | async-start | bytes 524288 | tf_op jit(solution)/shard_map/all_to_all | solution.py:355
  46.6 7.3 %copy-start.6 = (bf16[512,512]{1,0:T(8,128)(2,1)S(1)}, bf16[512,512]{1,0:T(8,128)(2,1)}, u32[]{:S(2)}) copy-start(bf16[512,512]{1,0:T(8,128)(2,1)} %param.15) | copy-start | bytes 1572868

commit v5 on v4

--- a/solution.py
+++ b/solution.py
@@ -28,13 +28,13 @@
 
 
 def ring_order(chips):
-    ring = list(range(0, chips, 2)) + list(range(1, chips, 2))[::-1]
+    ring = list(range(1, chips, 2)) + list(range(0, chips, 2))[::-1]
     start = ring.index(min(chips - 1, (chips // 2) | 1))
     return ring[start:] + ring[:start]
 
 
 def middle_order(chips):
-    return sorted(range(chips), key=lambda chip: abs(2 * (chip - chips // 2) + 0.5))
+    return [(chips // 2 + step) % chips for step in range(chips)]
 
 
 def place_in(order, chip):
@@ -218,6 +218,25 @@
             total = jnp.dot(weight, values[:, span], preferred_element_type=jnp.float32)
             joined = total if joined is None else jnp.where(mine, total, joined)
         out_ref[:, span] = joined.astype(out_ref.dtype)
+
+
+def finish_kernel(backs_ref, own_ref, gate_ref, routed_ref, weight_ref, out_ref):
+    slot_count, users, _ = out_ref.shape
+    chips = backs_ref.shape[0] // users
+    attended = []
+    for user in range(users):
+        parts = [backs_ref[chip * users + user].astype(jnp.float32) for chip in range(chips)]
+        while len(parts) > 1:
+            parts = [sum(parts[k : k + 2][1:], parts[k]) for k in range(0, len(parts), 2)]
+        attended.append(parts[0])
+    total = jnp.concatenate(attended, axis=0) + own_ref[...]
+    mixed = (layer_norm(total) * gate_ref[...]).astype(jnp.bfloat16)
+    result = routed_ref[...].astype(jnp.float32) + jnp.dot(
+        mixed, weight_ref[...], preferred_element_type=jnp.float32
+    )
+    for cand in range(slot_count):
+        rows = [result[user * slot_count + cand : user * slot_count + cand + 1] for user in range(users)]
+        out_ref[cand] = jnp.concatenate(rows, axis=0).astype(out_ref.dtype)
 
 
 IN_VMEM = pl.BlockSpec(memory_space=pltpu.VMEM)
@@ -375,14 +394,9 @@
     key = proj[:, 3 * width :].astype(jnp.bfloat16)
     own = self_term(query, key, value)
 
-    attended = jnp.sum(
-        backs.astype(jnp.float32).reshape(devices // users, slots, width), axis=0
-    )
-    mixed = (layer_norm(attended + own) * gate).astype(jnp.bfloat16)
-    result = routed_own.astype(jnp.float32) + jnp.dot(
-        mixed, out_weight, preferred_element_type=jnp.float32
-    )
-    cand_out = result.astype(jnp.bfloat16).reshape(users, slot_count, width).transpose(1, 0, 2)
+    cand_out = call(
+        finish_kernel, shaped((slot_count, users, width)), [IN_VMEM] * 5
+    )(backs, own, gate, routed_own, out_weight)
     return (item_embed, cand_out)
 
 

time: 55.2 us -> 54.1 us (0.980)
  the two profiles are of different devices: /device:TPU:1 before, /device:TPU:0 now
where the time goes in v5:
time: 54.1 us; the launch traced here: 53.4 us
  starting transfers between devices  19.5 us (36%)
  waiting for transfers between devices  13.2 us (24%)
  Pallas kernels  13.1 us (24%)
  matrix products  5.38 us (10%)
  local copies, waits for them, and re-layouts  1.12 us (2%)
  between operations  0.91 us (2%)
    all_to_all x1, waiting for transfers between devices, per_device(): lax.all_to_all(handed, 'seq', split_axis=0, concat_axis=0, tiled=True, ax...  10.1 us
    all_to_all x1, starting transfers between devices, per_device(): lax.all_to_all(call(functools.partial(code_kernel, depth, rows), shaped((...  8.33 us
    pallas_call x1, Pallas kernels, per_device(): call(attend_kernel, (shaped((cands, width)), shaped((cands + slot_count,...  5.58 us
    all_to_all x1, starting transfers between devices, per_device(): lax.all_to_all(user_part.reshape(devices, slot_count, width), 'seq', spli...  5.55 us
    all_to_all x1, starting transfers between devices, per_device(): lax.all_to_all(handed, 'seq', split_axis=0, concat_axis=0, tiled=True, ax...  4.9 us
    dot_general x1, matrix products, per_device(): jnp.dot(hidden, tower_out, preferred_element_type=jnp.float32)  3.3 us
    all_to_all x1, waiting for transfers between devices, per_device(): lax.all_to_all(user_part.reshape(devices, slot_count, width), 'seq', spli...  3.06 us
    pallas_call x1, Pallas kernels, per_device(): call(keep_kernel, (taken, shaped((width, width)), shaped((events, width))...  2.42 us
  transfers between devices with their start and end apart: 6, of which 2 were waited for; matrix products, arithmetic and copies ran while one was open for 11% of the time, Pallas kernels for 12%

profile of v5, /device:TPU:0, one launch (start us, length us, event | category | flops | bytes accessed | tf_op | source)
XLA Modules:
  0.0 53.4 jit_solution(16304450362877743053)
XLA Ops:
  0.6 0.0 copy-start
  0.6 0.6 %collective-permute-start = (bf16[2,1024,512]{2,1,0:T(8,128)(2,1)}, bf16[2,1024,512]{2,1,0:T(8,128)(2,1)}, u32[]{:S(2)}, u32[]{:S(2)}) collective-permute-start(bf16[2,1024,512]{2,1,0:T(8,128)(2,1)} %keys_near.1), channel_id=1, source_target_pairs={{0,1},{1,0},{2,3},{3,2},{4,5},{5,4},{6,7},{7,6},{8,9},{9,8},{10,11... | collective-permute-start | bytes 6291464 | tf_op jit(solution)/shard_map/ppermute | solution.py:318
  1.2 0.1 collective-permute-start.1
  1.3 1.5 %shard_map.122 = s32[16,1,32]{2,1,0:T(1,128)} custom-call(s32[2,1,16]{2,1,0:T(1,128)} %bitcast.13, s32[2,16]{1,0:T(2,128)} %bitcast.14), custom_call_target="tpu_custom_call" | custom-call | tf_op jit(solution)/shard_map/pallas_call | solution.py:301
  2.8 8.3 %all-to-all-start = ((s32[16,1,32]{2,1,0:T(1,128)}), s32[16,1,32]{2,1,0:T(1,128)S(1)}, u32[]{:S(2)}, u32[]{:S(2)}) async-start(s32[16,1,32]{2,1,0:T(1,128)} %shard_map.122), calls=%async_computation | async-start | bytes 16384 | tf_op jit(solution)/shard_map/all_to_all | solution.py:300
  11.1 0.0 copy-start.5
  11.2 0.0 copy-start.6
  11.2 3.3 %convolution_convert_fusion.embed_ref = bf16[128,512]{1,0:T(8,128)(2,1)S(1)} fusion(bf16[2048,512]{1,0:T(8,128)(2,1)S(1)} %copy-done, bf16[128,1024]{1,0:T(8,128)(2,1)} %param.11, bf16[1024,2048]{1,0:T(8,128)(2,1)} %param.12), kind=kOutput, calls=%fused_computation | convolution fusion | flops 806682624 | bytes 6684672 | tf_op jit(solution)/shard_map/dot_general | solution.py:324
  14.5 0.0 copy-start.2
  14.5 0.0 all-to-all-done.codes_ref
  14.5 1.1 %shard_map.124 = bf16[8,64,512]{2,1,0:T(8,128)(2,1)} custom-call(s32[16,1,32]{2,1,0:T(1,128)S(1)} %all-to-all-done.codes_ref, bf16[128,512]{1,0:T(8,128)(2,1)S(1)} %convolution_convert_fusion.embed_ref), custom_call_target="tpu_custom_call" | custom-call | tf_op jit(solution)/shard_map/pallas_call | solution.py:326
  15.6 4.9 %all-to-all-start.1 = ((bf16[8,64,512]{2,1,0:T(8,128)(2,1)}), bf16[8,64,512]{2,1,0:T(8,128)(2,1)S(1)}, u32[]{:S(2)}, u32[]{:S(2)}) async-start(bf16[8,64,512]{2,1,0:T(8,128)(2,1)} %shard_map.124), calls=%async_computation.1 | async-start | bytes 1048576 | tf_op jit(solution)/shard_map/all_to_all | solution.py:337
  20.5 1.2 %shard_map.123 = (bf16[272,512]{1,0:T(8,128)(2,1)S(1)}, bf16[272,512]{1,0:T(8,128)(2,1)S(1)}, s32[256,1]{1,0:T(8,128)S(1)}) custom-call(s32[2]{0:T(128)S(1)} %copy-done.6, s32[16,1,32]{2,1,0:T(1,128)S(1)} %all-to-all-done.codes_ref, s32[2,256]{1,0:T(2,128)S(1)} %bitcast.12), custom_call_target="tpu_custom_call" | custom-call | tf_op jit(solution)/shard_map/pallas_call | solution.py:344
  21.7 0.6 %copy-done.3 = s32[256,1]{1,0:T(8,128)} copy-done((s32[256,1]{1,0:T(8,128)}, s32[256,1]{1,0:T(8,128)S(1)}, u32[]{:S(2)}) %copy-start.3) | copy-done | bytes 1048
  22.4 10.1 %all-to-all-done.1 = bf16[8,64,512]{2,1,0:T(8,128)(2,1)S(1)} async-done(((bf16[8,64,512]{2,1,0:T(8,128)(2,1)}), bf16[8,64,512]{2,1,0:T(8,128)(2,1)S(1)}, u32[]{:S(2)}, u32[]{:S(2)}) %all-to-all-start.1) | async-done | bytes 524320 | tf_op jit(solution)/shard_map/all_to_all | solution.py:337
  32.5 0.3 shard_map.126
  32.8 0.1 collective-permute-start.2
  33.0 0.0 collective-permute-done.keys_far
  33.0 0.0 collective-permute-done.1.values_far
  33.0 2.4 %shard_map.125 = (bf16[272,512]{1,0:T(8,128)(2,1)S(1)}, bf16[512,512]{1,0:T(8,128)(2,1)S(1)}, bf16[2048,512]{1,0:T(8,128)(2,1)S(1)}, bf16[2048,512]{1,0:T(8,128)(2,1)S(1)}) custom-call(bf16[272,512]{1,0:T(8,128)(2,1)S(1)} %get-tuple-element.11.chosen_ref, bf16[512,512]{1,0:T(8,128)(2,1)S(1)} %bitcast.11, bf16[2,1024,512]{2,1,0:T(8,128)(2,1)} %keys_near.1, ...), custom_call_target="tpu_custom_call" | custom-call | tf_op jit(solution)/shard_map/pallas_call | solution.py:353
  35.4 0.0 collective-permute-done.2.came_ref
  35.4 5.6 %shard_map.127 = (bf16[256,512]{1,0:T(8,128)(2,1)}, bf16[272,512]{1,0:T(8,128)(2,1)S(1)}) custom-call(bf16[272,512]{1,0:T(8,128)(2,1)S(1)} %get-tuple-element.12.kept_ref, bf16[272,512]{1,0:T(8,128)(2,1)S(1)} %collective-permute-done.2.came_ref, bf16[512,512]{1,0:T(8,128)(2,1)S(1)} %get-tuple-element.14.weight_ref, s32[256,1]{1,0:T(8,128)S(1)} %copy-done.4, ...), custom_call_target="tpu_custom_call" | custom-call | tf_op jit(solution)/shard_map/pallas_call | solution.py:368
  41.0 5.5 %all-to-all-start.2 = ((bf16[16,16,512]{2,1,0:T(8,128)(2,1)}), bf16[16,16,512]{2,1,0:T(8,128)(2,1)S(1)}, u32[]{:S(2)}, u32[]{:S(2)}) async-start(bf16[16,16,512]{2,1,0:T(8,128)(2,1)} %bitcast.4), calls=%async_computation.2 | async-start | bytes 524288 | tf_op jit(solution)/shard_map/all_to_all | solution.py:374
  46.6 2.1 %fusion.2 = (bf16[32,2048]{1,0:T(8,128)(2,1)S(1)}, f32[32,2048]{1,0:T(8,128)S(1)}) fusion(bf16[32,512]{1,0:T(8,128)(2,1)S(1)} %maximum_select_fusion.routed_ref, bf16[512,2048]{1,0:T(8,128)(2,1)} %proj_hbm.1), kind=kOutput, calls=%fused_computation.10 | convolution fusion | flops 67436544 | bytes 2523136 | tf_op jit(solution)/shard_map/dot_general | solution.py:390
  48.7 0.1 mul.54
  48.8 0.1 reduce_sum.9
  48.9 0.1 copy.14
  49.0 0.1 copy.15
  49.1 0.1 mul.58
  49.2 0.1 mul.59
  49.3 3.1 %all-to-all-done.2.backs_ref = bf16[16,16,512]{2,1,0:T(8,128)(2,1)S(1)} async-done(((bf16[16,16,512]{2,1,0:T(8,128)(2,1)}), bf16[16,16,512]{2,1,0:T(8,128)(2,1)S(1)}, u32[]{:S(2)}, u32[]{:S(2)}) %all-to-all-start.2) | async-done | bytes 262176 | tf_op jit(solution)/shard_map/all_to_all | solution.py:374
  52.4 1.0 %shard_map.128 = bf16[16,2,512]{2,1,0:T(2,128)(2,1)} custom-call(bf16[16,16,512]{2,1,0:T(8,128)(2,1)S(1)} %all-to-all-done.2.backs_ref, f32[32,512]{1,0:T(8,128)S(1)} %convert_multiply_fusion.own_ref, f32[32,512]{1,0:T(8,128)S(1)} %slice.26.gate_ref, bf16[32,512]{1,0:T(8,128)(2,1)S(1)} %maximum_select_fusion.routed_ref, bf16[512,512]{1,0:T(8,128)(2,1)S(1)} %copy-done.1), custom_call_target="tpu_custom_call" | custom-call | tf_op jit(solution)/shard_map/pallas_call | solution.py:397
  (15 shorter events, 0.1 us)
Async XLA Ops:
  0.6 10.5 %copy-start = (bf16[2048,512]{1,0:T(8,128)(2,1)S(1)}, bf16[2048,512]{1,0:T(8,128)(2,1)}, u32[]{:S(2)}) copy-start(bf16[2048,512]{1,0:T(8,128)(2,1)} %param.13) | copy-start | bytes 6291460
  0.6 32.3 %collective-permute-start = (bf16[2,1024,512]{2,1,0:T(8,128)(2,1)}, bf16[2,1024,512]{2,1,0:T(8,128)(2,1)}, u32[]{:S(2)}, u32[]{:S(2)}) collective-permute-start(bf16[2,1024,512]{2,1,0:T(8,128)(2,1)} %keys_near.1), channel_id=1, source_target_pairs={{0,1},{1,0},{2,3},{3,2},{4,5},{5,4},{6,7},{7,6},{8,9},{9,8},{10,11... | collective-permute-start | bytes 6291464 | tf_op jit(solution)/shard_map/ppermute | solution.py:318
  1.2 31.8 %collective-permute-start.1 = (bf16[2,1024,512]{2,1,0:T(8,128)(2,1)}, bf16[2,1024,512]{2,1,0:T(8,128)(2,1)}, u32[]{:S(2)}, u32[]{:S(2)}) collective-permute-start(bf16[2,1024,512]{2,1,0:T(8,128)(2,1)} %values_near.1), channel_id=1, source_target_pairs={{0,1},{1,0},{2,3},{3,2},{4,5},{5,4},{6,7},{7,6},{8,9},{9,8},{10,11... | collective-permute-start | bytes 6291464 | tf_op jit(solution)/shard_map/ppermute | solution.py:319
  2.8 11.7 %all-to-all-start = ((s32[16,1,32]{2,1,0:T(1,128)}), s32[16,1,32]{2,1,0:T(1,128)S(1)}, u32[]{:S(2)}, u32[]{:S(2)}) async-start(s32[16,1,32]{2,1,0:T(1,128)} %shard_map.122), calls=%async_computation | async-start | bytes 16384 | tf_op jit(solution)/shard_map/all_to_all | solution.py:300
  11.1 9.4 %copy-start.5 = (s32[256,2]{0,1:T(2,128)S(1)}, s32[256,2]{0,1:T(2,128)}, u32[]{:S(2)}) copy-start(s32[256,2]{0,1:T(2,128)} %param.21) | copy-start | bytes 6148
  11.2 9.4 %copy-start.6 = (s32[2]{0:T(128)S(1)}, s32[2]{0:T(128)}, u32[]{:S(2)}) copy-start(s32[2]{0:T(128)} %lengths_ref.1) | copy-start | bytes 28
  14.5 1.2 %copy-start.2 = (bf16[128,512]{1,0:T(8,128)(2,1)}, bf16[128,512]{1,0:T(8,128)(2,1)S(1)}, u32[]{:S(2)}) copy-start(bf16[128,512]{1,0:T(8,128)(2,1)S(1)} %convolution_convert_fusion.embed_ref) | copy-start | bytes 393220
  15.6 16.9 %all-to-all-start.1 = ((bf16[8,64,512]{2,1,0:T(8,128)(2,1)}), bf16[8,64,512]{2,1,0:T(8,128)(2,1)S(1)}, u32[]{:S(2)}, u32[]{:S(2)}) async-start(bf16[8,64,512]{2,1,0:T(8,128)(2,1)} %shard_map.124), calls=%async_computation.1 | async-start | bytes 1048576 | tf_op jit(solution)/shard_map/all_to_all | solution.py:337
  21.7 0.7 %copy-start.3 = (s32[256,1]{1,0:T(8,128)}, s32[256,1]{1,0:T(8,128)S(1)}, u32[]{:S(2)}) copy-start(s32[256,1]{1,0:T(8,128)S(1)} %get-tuple-element.15.seen_ref) | copy-start | bytes 3076
  32.8 2.6 %collective-permute-start.2 = (bf16[272,512]{1,0:T(8,128)(2,1)S(1)}, bf16[272,512]{1,0:T(8,128)(2,1)S(1)}, u32[]{:S(2)}, u32[]{:S(2)}) collective-permute-start(bf16[272,512]{1,0:T(8,128)(2,1)S(1)} %shard_map.126), channel_id=1, source_target_pairs={{0,1},{1,0},{2,3},{3,2},{4,5},{5,4},{6,7},{7,6},{8,9},{9,8},{10,11... | collective-permute-start | bytes 835592 | tf_op jit(solution)/shard_map/ppermute | solution.py:352
  33.0 2.5 %copy-start.4 = (s32[256,1]{1,0:T(8,128)S(1)}, s32[256,1]{1,0:T(8,128)}, u32[]{:S(2)}) copy-start(s32[256,1]{1,0:T(8,128)} %copy-done.3) | copy-start | bytes 3076
  41.0 11.3 %copy-start.1 = (bf16[512,512]{1,0:T(8,128)(2,1)S(1)}, bf16[512,512]{1,0:T(8,128)(2,1)}, u32[]{:S(2)}) copy-start(bf16[512,512]{1,0:T(8,128)(2,1)} %weight_ref.1) | copy-start | bytes 1572868
  41.0 11.3 %all-to-all-start.2 = ((bf16[16,16,512]{2,1,0:T(8,128)(2,1)}), bf16[16,16,512]{2,1,0:T(8,128)(2,1)S(1)}, u32[]{:S(2)}, u32[]{:S(2)}) async-start(bf16[16,16,512]{2,1,0:T(8,128)(2,1)} %bitcast.4), calls=%async_computation.2 | async-start | bytes 524288 | tf_op jit(solution)/shard_map/all_to_all | solution.py:374

commit v6 on v5

--- a/solution.py
+++ b/solution.py
@@ -56,11 +56,12 @@
     users = owner_ref.shape[0]
     owners = jnp.concatenate([owner_ref[user] for user in range(users)], axis=1)
     wanted = jnp.concatenate([row_ref[user : user + 1, :] for user in range(users)], axis=1)
-    slot = lax.broadcasted_iota(jnp.int32, owners.shape, 1)
-    ranks = jnp.zeros_like(owners)
-    for other in range(owners.shape[1] - 1):
-        same = (owners == owners[:, other : other + 1]) & (slot > other)
-        ranks = ranks + same.astype(jnp.int32)
+    slots = owners.shape[1]
+    before = lax.broadcasted_iota(jnp.int32, (slots, slots), 0) < lax.broadcasted_iota(
+        jnp.int32, (slots, slots), 1
+    )
+    same = (column(owners, slots) == owners) & before
+    ranks = jnp.sum(same.astype(jnp.int32), axis=0, keepdims=True)
     code = (owners * depth + ranks) * rows + wanted
     out_ref[...] = jnp.broadcast_to(code[None], out_ref.shape)
 
@@ -70,20 +71,26 @@
     rows = embed_ref.shape[0]
     want = lax.axis_index("seq") * depth + lax.broadcasted_iota(jnp.int32, (depth, slots), 0)
     lane = lax.broadcasted_iota(jnp.int32, (depth, rows), 1)
-    for asker in range(devices):
-        codes = jnp.broadcast_to(codes_ref[asker], (depth, slots))
-        hit = lax.div(codes, rows) == want
-        asked = jnp.sum(jnp.where(hit, lax.rem(codes, rows), 0), axis=1, keepdims=True)
-        chosen_ref[asker * depth : (asker + 1) * depth, :] = (lane == asked).astype(jnp.float32)
-    picked_ref[...] = jnp.dot(
-        chosen_ref[...].astype(jnp.bfloat16), embed_ref[...], preferred_element_type=jnp.float32
-    ).astype(jnp.bfloat16)
-    copies = [
-        pltpu.make_async_copy(picked_ref, out_hbm.at[receiver], sems.at[receiver])
-        for receiver in range(out_hbm.shape[0])
-    ]
-    for copy in copies:
-        copy.start()
+    copies = []
+    parts = sems.shape[1]
+    for part in range(parts):
+        askers = range(devices * part // parts, devices * (part + 1) // parts)
+        for asker in askers:
+            codes = jnp.broadcast_to(codes_ref[asker], (depth, slots))
+            hit = lax.div(codes, rows) == want
+            asked = jnp.sum(jnp.where(hit, lax.rem(codes, rows), 0), axis=1, keepdims=True)
+            chosen_ref[asker * depth : (asker + 1) * depth, :] = (lane == asked).astype(jnp.float32)
+        span = slice(askers[0] * depth, (askers[-1] + 1) * depth)
+        lines = pl.ds(askers[0] * depth, len(askers) * depth)
+        picked_ref[span, :] = jnp.dot(
+            chosen_ref[span, :].astype(jnp.bfloat16), embed_ref[...], preferred_element_type=jnp.float32
+        ).astype(jnp.bfloat16)
+        for receiver in range(out_hbm.shape[0]):
+            copy = pltpu.make_async_copy(
+                picked_ref.at[lines], out_hbm.at[receiver, lines], sems.at[receiver, part]
+            )
+            copy.start()
+            copies.append(copy)
     for copy in copies:
         copy.wait()
 
@@ -190,7 +197,9 @@
         copy.wait()
 
 
-def attend_kernel(kept_ref, came_ref, weight_ref, seen_ref, keys, values, out_ref, routed_ref):
+def attend_kernel(
+    kept_ref, came_ref, weight_ref, seen_ref, keys, values, out_hbm, routed_ref, out_ref, sems
+):
     rows, width = out_ref.shape
     size = width // HEADS
     routed = kept_ref[...] + came_ref[...]
@@ -203,6 +212,7 @@
     shown = (event < seen_ref[...]).astype(jnp.float32).astype(jnp.bfloat16)
     lane = lax.broadcasted_iota(jnp.int32, (rows, LANES), 1)
     per_tile = LANES // size
+    copies = []
     for tile in range(width // LANES):
         span = slice(tile * LANES, (tile + 1) * LANES)
         whole = query[:, span]
@@ -218,6 +228,13 @@
             total = jnp.dot(weight, values[:, span], preferred_element_type=jnp.float32)
             joined = total if joined is None else jnp.where(mine, total, joined)
         out_ref[:, span] = joined.astype(out_ref.dtype)
+        copy = pltpu.make_async_copy(
+            out_ref.at[:, pl.ds(tile * LANES, LANES)], out_hbm.at[:, pl.ds(tile * LANES, LANES)], sems.at[tile]
+        )
+        copy.start()
+        copies.append(copy)
+    for copy in copies:
+        copy.wait()
 
 
 def finish_kernel(backs_ref, own_ref, gate_ref, routed_ref, weight_ref, out_ref):
@@ -254,7 +271,7 @@
         kernel,
         out_shape=outs,
         in_specs=specs,
-        out_specs=(out_space,) * len(outs) if many else out_space,
+        out_specs=(out_space,) * len(outs) if many and not isinstance(out_space, tuple) else out_space,
         scratch_shapes=scratch,
         compiler_params=pltpu.CompilerParams(vmem_limit_bytes=vmem * 2**20),
     )
@@ -330,7 +347,7 @@
         [
             pltpu.VMEM((room, rows), jnp.float32),
             pltpu.VMEM((room, width), jnp.bfloat16),
-            pltpu.SemaphoreType.DMA((half,)),
+            pltpu.SemaphoreType.DMA((half, 1)),
         ],
         out_space=IN_HBM,
     )(codes, item_embed)
@@ -369,7 +386,9 @@
         attend_kernel,
         (shaped((cands, width)), shaped((cands + slot_count, width))),
         [IN_VMEM] * 6,
+        [pltpu.VMEM((cands, width), jnp.bfloat16), pltpu.SemaphoreType.DMA((width // LANES,))],
         vmem=48,
+        out_space=(IN_HBM, IN_VMEM),
     )(kept, came, weight, seen, keys, values)
     backs = lax.all_to_all(
         user_part.reshape(devices, slot_count, width),

time: 54.1 us -> 54.1 us (level)
  no operation moved by 1% of the time
where the time goes in v6:
time: 54.1 us; the launch traced here: 53.3 us
  starting transfers between devices  19.5 us (36%)
  waiting for transfers between devices  13.2 us (24%)
  Pallas kernels  13.1 us (24%)
  matrix products  5.38 us (10%)
  local copies, waits for them, and re-layouts  1.13 us (2%)
  between operations  0.93 us (2%)
    all_to_all x1, waiting for transfers between devices, per_device(): lax.all_to_all(handed, 'seq', split_axis=0, concat_axis=0, tiled=True, ax...  10.1 us
    all_to_all x1, starting transfers between devices, per_device(): lax.all_to_all(call(functools.partial(code_kernel, depth, rows), shaped((...  8.33 us
    all_to_all x1, starting transfers between devices, per_device(): lax.all_to_all(user_part.reshape(devices, slot_count, width), 'seq', spli...  5.56 us
    pallas_call x1, Pallas kernels, per_device(): call(attend_kernel, (shaped((cands, width)), shaped((cands + slot_count,...  5.54 us
    all_to_all x1, starting transfers between devices, per_device(): lax.all_to_all(handed, 'seq', split_axis=0, concat_axis=0, tiled=True, ax...  4.9 us
    dot_general x1, matrix products, per_device(): jnp.dot(hidden, tower_out, preferred_element_type=jnp.float32)  3.29 us
    all_to_all x1, waiting for transfers between devices, per_device(): lax.all_to_all(user_part.reshape(devices, slot_count, width), 'seq', spli...  3.06 us
    pallas_call x1, Pallas kernels, per_device(): call(keep_kernel, (taken, shaped((width, width)), shaped((events, width))...  2.42 us
  transfers between devices with their start and end apart: 6, of which 2 were waited for; matrix products, arithmetic and copies ran while one was open for 11% of the time, Pallas kernels for 12%

profile of v6, /device:TPU:0, one launch (start us, length us, event | category | flops | bytes accessed | tf_op | source)
XLA Modules:
  0.0 53.3 jit_solution(6309431480500162807)
XLA Ops:
  0.6 0.0 copy-start
  0.6 0.6 %collective-permute-start = (bf16[2,1024,512]{2,1,0:T(8,128)(2,1)}, bf16[2,1024,512]{2,1,0:T(8,128)(2,1)}, u32[]{:S(2)}, u32[]{:S(2)}) collective-permute-start(bf16[2,1024,512]{2,1,0:T(8,128)(2,1)} %keys_near.1), channel_id=1, source_target_pairs={{0,1},{1,0},{2,3},{3,2},{4,5},{5,4},{6,7},{7,6},{8,9},{9,8},{10,11... | collective-permute-start | bytes 6291464 | tf_op jit(solution)/shard_map/ppermute | solution.py:335
  1.2 0.1 collective-permute-start.1
  1.3 1.5 %shard_map.122 = s32[16,1,32]{2,1,0:T(1,128)} custom-call(s32[2,1,16]{2,1,0:T(1,128)} %bitcast.13, s32[2,16]{1,0:T(2,128)} %bitcast.14), custom_call_target="tpu_custom_call" | custom-call | tf_op jit(solution)/shard_map/pallas_call | solution.py:318
  2.8 8.3 %all-to-all-start = ((s32[16,1,32]{2,1,0:T(1,128)}), s32[16,1,32]{2,1,0:T(1,128)S(1)}, u32[]{:S(2)}, u32[]{:S(2)}) async-start(s32[16,1,32]{2,1,0:T(1,128)} %shard_map.122), calls=%async_computation | async-start | bytes 16384 | tf_op jit(solution)/shard_map/all_to_all | solution.py:317
  11.1 0.0 copy-start.5
  11.1 0.0 copy-start.6
  11.1 3.3 %convolution_convert_fusion.embed_ref = bf16[128,512]{1,0:T(8,128)(2,1)S(1)} fusion(bf16[2048,512]{1,0:T(8,128)(2,1)S(1)} %copy-done, bf16[128,1024]{1,0:T(8,128)(2,1)} %param.11, bf16[1024,2048]{1,0:T(8,128)(2,1)} %param.12), kind=kOutput, calls=%fused_computation | convolution fusion | flops 806682624 | bytes 6684672 | tf_op jit(solution)/shard_map/dot_general | solution.py:341
  14.4 0.0 copy-start.2
  14.5 0.0 all-to-all-done.codes_ref
  14.5 1.1 %shard_map.124 = bf16[8,64,512]{2,1,0:T(8,128)(2,1)} custom-call(s32[16,1,32]{2,1,0:T(1,128)S(1)} %all-to-all-done.codes_ref, bf16[128,512]{1,0:T(8,128)(2,1)S(1)} %convolution_convert_fusion.embed_ref), custom_call_target="tpu_custom_call" | custom-call | tf_op jit(solution)/shard_map/pallas_call | solution.py:343
  15.6 4.9 %all-to-all-start.1 = ((bf16[8,64,512]{2,1,0:T(8,128)(2,1)}), bf16[8,64,512]{2,1,0:T(8,128)(2,1)S(1)}, u32[]{:S(2)}, u32[]{:S(2)}) async-start(bf16[8,64,512]{2,1,0:T(8,128)(2,1)} %shard_map.124), calls=%async_computation.1 | async-start | bytes 1048576 | tf_op jit(solution)/shard_map/all_to_all | solution.py:354
  20.5 1.2 %shard_map.123 = (bf16[272,512]{1,0:T(8,128)(2,1)S(1)}, bf16[272,512]{1,0:T(8,128)(2,1)S(1)}, s32[256,1]{1,0:T(8,128)S(1)}) custom-call(s32[2]{0:T(128)S(1)} %copy-done.6, s32[16,1,32]{2,1,0:T(1,128)S(1)} %all-to-all-done.codes_ref, s32[2,256]{1,0:T(2,128)S(1)} %bitcast.12), custom_call_target="tpu_custom_call" | custom-call | tf_op jit(solution)/shard_map/pallas_call | solution.py:361
  21.7 0.6 %copy-done.3 = s32[256,1]{1,0:T(8,128)} copy-done((s32[256,1]{1,0:T(8,128)}, s32[256,1]{1,0:T(8,128)S(1)}, u32[]{:S(2)}) %copy-start.3) | copy-done | bytes 1048
  22.4 10.1 %all-to-all-done.1 = bf16[8,64,512]{2,1,0:T(8,128)(2,1)S(1)} async-done(((bf16[8,64,512]{2,1,0:T(8,128)(2,1)}), bf16[8,64,512]{2,1,0:T(8,128)(2,1)S(1)}, u32[]{:S(2)}, u32[]{:S(2)}) %all-to-all-start.1) | async-done | bytes 524320 | tf_op jit(solution)/shard_map/all_to_all | solution.py:354
  32.5 0.3 shard_map.126
  32.8 0.1 collective-permute-start.2
  32.9 0.0 collective-permute-done.keys_far
  32.9 0.0 collective-permute-done.1.values_far
  33.0 2.4 %shard_map.125 = (bf16[272,512]{1,0:T(8,128)(2,1)S(1)}, bf16[512,512]{1,0:T(8,128)(2,1)S(1)}, bf16[2048,512]{1,0:T(8,128)(2,1)S(1)}, bf16[2048,512]{1,0:T(8,128)(2,1)S(1)}) custom-call(bf16[272,512]{1,0:T(8,128)(2,1)S(1)} %get-tuple-element.11.chosen_ref, bf16[512,512]{1,0:T(8,128)(2,1)S(1)} %bitcast.11, bf16[2,1024,512]{2,1,0:T(8,128)(2,1)} %keys_near.1, ...), custom_call_target="tpu_custom_call" | custom-call | tf_op jit(solution)/shard_map/pallas_call | solution.py:370
  35.4 5.5 %shard_map.127 = (bf16[256,512]{1,0:T(8,128)(2,1)}, bf16[272,512]{1,0:T(8,128)(2,1)S(1)}) custom-call(bf16[272,512]{1,0:T(8,128)(2,1)S(1)} %get-tuple-element.12.kept_ref, bf16[272,512]{1,0:T(8,128)(2,1)S(1)} %collective-permute-done.2.came_ref, bf16[512,512]{1,0:T(8,128)(2,1)S(1)} %get-tuple-element.14.weight_ref, s32[256,1]{1,0:T(8,128)S(1)} %copy-done.4, ...), custom_call_target="tpu_custom_call" | custom-call | tf_op jit(solution)/shard_map/pallas_call | solution.py:385
  41.0 0.0 copy-start.1
  41.0 5.6 %all-to-all-start.2 = ((bf16[16,16,512]{2,1,0:T(8,128)(2,1)}), bf16[16,16,512]{2,1,0:T(8,128)(2,1)S(1)}, u32[]{:S(2)}, u32[]{:S(2)}) async-start(bf16[16,16,512]{2,1,0:T(8,128)(2,1)} %bitcast.4), calls=%async_computation.2 | async-start | bytes 524288 | tf_op jit(solution)/shard_map/all_to_all | solution.py:393
  46.6 2.1 %fusion.2 = (bf16[32,2048]{1,0:T(8,128)(2,1)S(1)}, f32[32,2048]{1,0:T(8,128)S(1)}) fusion(bf16[32,512]{1,0:T(8,128)(2,1)S(1)} %maximum_select_fusion.routed_ref, bf16[512,2048]{1,0:T(8,128)(2,1)} %proj_hbm.1), kind=kOutput, calls=%fused_computation.10 | convolution fusion | flops 67436544 | bytes 2523136 | tf_op jit(solution)/shard_map/dot_general | solution.py:409
  48.7 0.1 mul.54
  48.8 0.1 reduce_sum.9
  48.9 0.1 copy.14
  49.0 0.1 copy.15
  49.0 0.1 mul.58
  49.1 0.1 mul.59
  49.3 3.1 %all-to-all-done.2.backs_ref = bf16[16,16,512]{2,1,0:T(8,128)(2,1)S(1)} async-done(((bf16[16,16,512]{2,1,0:T(8,128)(2,1)}), bf16[16,16,512]{2,1,0:T(8,128)(2,1)S(1)}, u32[]{:S(2)}, u32[]{:S(2)}) %all-to-all-start.2) | async-done | bytes 262176 | tf_op jit(solution)/shard_map/all_to_all | solution.py:393
  52.3 1.0 %shard_map.128 = bf16[16,2,512]{2,1,0:T(2,128)(2,1)} custom-call(bf16[16,16,512]{2,1,0:T(8,128)(2,1)S(1)} %all-to-all-done.2.backs_ref, f32[32,512]{1,0:T(8,128)S(1)} %convert_multiply_fusion.own_ref, f32[32,512]{1,0:T(8,128)S(1)} %slice.26.gate_ref, bf16[32,512]{1,0:T(8,128)(2,1)S(1)} %maximum_select_fusion.routed_ref, bf16[512,512]{1,0:T(8,128)(2,1)S(1)} %copy-done.1), custom_call_target="tpu_custom_call" | custom-call | tf_op jit(solution)/shard_map/pallas_call | solution.py:416
  (15 shorter events, 0.1 us)
Async XLA Ops:
  0.6 10.5 %copy-start = (bf16[2048,512]{1,0:T(8,128)(2,1)S(1)}, bf16[2048,512]{1,0:T(8,128)(2,1)}, u32[]{:S(2)}) copy-start(bf16[2048,512]{1,0:T(8,128)(2,1)} %param.13) | copy-start | bytes 6291460
  0.6 32.3 %collective-permute-start = (bf16[2,1024,512]{2,1,0:T(8,128)(2,1)}, bf16[2,1024,512]{2,1,0:T(8,128)(2,1)}, u32[]{:S(2)}, u32[]{:S(2)}) collective-permute-start(bf16[2,1024,512]{2,1,0:T(8,128)(2,1)} %keys_near.1), channel_id=1, source_target_pairs={{0,1},{1,0},{2,3},{3,2},{4,5},{5,4},{6,7},{7,6},{8,9},{9,8},{10,11... | collective-permute-start | bytes 6291464 | tf_op jit(solution)/shard_map/ppermute | solution.py:335
  1.2 31.7 %collective-permute-start.1 = (bf16[2,1024,512]{2,1,0:T(8,128)(2,1)}, bf16[2,1024,512]{2,1,0:T(8,128)(2,1)}, u32[]{:S(2)}, u32[]{:S(2)}) collective-permute-start(bf16[2,1024,512]{2,1,0:T(8,128)(2,1)} %values_near.1), channel_id=1, source_target_pairs={{0,1},{1,0},{2,3},{3,2},{4,5},{5,4},{6,7},{7,6},{8,9},{9,8},{10,11... | collective-permute-start | bytes 6291464 | tf_op jit(solution)/shard_map/ppermute | solution.py:336
  2.8 11.7 %all-to-all-start = ((s32[16,1,32]{2,1,0:T(1,128)}), s32[16,1,32]{2,1,0:T(1,128)S(1)}, u32[]{:S(2)}, u32[]{:S(2)}) async-start(s32[16,1,32]{2,1,0:T(1,128)} %shard_map.122), calls=%async_computation | async-start | bytes 16384 | tf_op jit(solution)/shard_map/all_to_all | solution.py:317
  11.1 9.4 %copy-start.5 = (s32[256,2]{0,1:T(2,128)S(1)}, s32[256,2]{0,1:T(2,128)}, u32[]{:S(2)}) copy-start(s32[256,2]{0,1:T(2,128)} %param.21) | copy-start | bytes 6148
  11.1 9.4 %copy-start.6 = (s32[2]{0:T(128)S(1)}, s32[2]{0:T(128)}, u32[]{:S(2)}) copy-start(s32[2]{0:T(128)} %lengths_ref.1) | copy-start | bytes 28
  14.4 1.2 %copy-start.2 = (bf16[128,512]{1,0:T(8,128)(2,1)}, bf16[128,512]{1,0:T(8,128)(2,1)S(1)}, u32[]{:S(2)}) copy-start(bf16[128,512]{1,0:T(8,128)(2,1)S(1)} %convolution_convert_fusion.embed_ref) | copy-start | bytes 393220
  15.6 16.9 %all-to-all-start.1 = ((bf16[8,64,512]{2,1,0:T(8,128)(2,1)}), bf16[8,64,512]{2,1,0:T(8,128)(2,1)S(1)}, u32[]{:S(2)}, u32[]{:S(2)}) async-start(bf16[8,64,512]{2,1,0:T(8,128)(2,1)} %shard_map.124), calls=%async_computation.1 | async-start | bytes 1048576 | tf_op jit(solution)/shard_map/all_to_all | solution.py:354
  21.7 0.7 %copy-start.3 = (s32[256,1]{1,0:T(8,128)}, s32[256,1]{1,0:T(8,128)S(1)}, u32[]{:S(2)}) copy-start(s32[256,1]{1,0:T(8,128)S(1)} %get-tuple-element.15.seen_ref) | copy-start | bytes 3076
  32.8 2.6 %collective-permute-start.2 = (bf16[272,512]{1,0:T(8,128)(2,1)S(1)}, bf16[272,512]{1,0:T(8,128)(2,1)S(1)}, u32[]{:S(2)}, u32[]{:S(2)}) collective-permute-start(bf16[272,512]{1,0:T(8,128)(2,1)S(1)} %shard_map.126), channel_id=1, source_target_pairs={{0,1},{1,0},{2,3},{3,2},{4,5},{5,4},{6,7},{7,6},{8,9},{9,8},{10,11... | collective-permute-start | bytes 835592 | tf_op jit(solution)/shard_map/ppermute | solution.py:369
  33.0 2.5 %copy-start.4 = (s32[256,1]{1,0:T(8,128)S(1)}, s32[256,1]{1,0:T(8,128)}, u32[]{:S(2)}) copy-start(s32[256,1]{1,0:T(8,128)} %copy-done.3) | copy-start | bytes 3076
  41.0 11.4 %copy-start.1 = (bf16[512,512]{1,0:T(8,128)(2,1)S(1)}, bf16[512,512]{1,0:T(8,128)(2,1)}, u32[]{:S(2)}) copy-start(bf16[512,512]{1,0:T(8,128)(2,1)} %weight_ref.1) | copy-start | bytes 1572868
  41.0 11.4 %all-to-all-start.2 = ((bf16[16,16,512]{2,1,0:T(8,128)(2,1)}), bf16[16,16,512]{2,1,0:T(8,128)(2,1)S(1)}, u32[]{:S(2)}, u32[]{:S(2)}) async-start(bf16[16,16,512]{2,1,0:T(8,128)(2,1)} %bitcast.4), calls=%async_computation.2 | async-start | bytes 524288 | tf_op jit(solution)/shard_map/all_to_all | solution.py:393

commit v7 on v6

--- a/solution.py
+++ b/solution.py
@@ -77,8 +77,10 @@
         askers = range(devices * part // parts, devices * (part + 1) // parts)
         for asker in askers:
             codes = jnp.broadcast_to(codes_ref[asker], (depth, slots))
-            hit = lax.div(codes, rows) == want
-            asked = jnp.sum(jnp.where(hit, lax.rem(codes, rows), 0), axis=1, keepdims=True)
+            inside = codes - want * rows
+            asked = jnp.sum(
+                jnp.where((inside >= 0) & (inside < rows), inside, 0), axis=1, keepdims=True
+            )
             chosen_ref[asker * depth : (asker + 1) * depth, :] = (lane == asked).astype(jnp.float32)
         span = slice(askers[0] * depth, (askers[-1] + 1) * depth)
         lines = pl.ds(askers[0] * depth, len(askers) * depth)

time: 54.1 us -> 54.1 us (level)
  no operation moved by 1% of the time
where the time goes in v7:
time: 54.1 us; the launch traced here: 53.3 us
  starting transfers between devices  19.5 us (36%)
  waiting for transfers between devices  13.2 us (24%)
  Pallas kernels  13.1 us (24%)
  matrix products  5.37 us (10%)
  local copies, waits for them, and re-layouts  1.13 us (2%)
  between operations  0.93 us (2%)
    all_to_all x1, waiting for transfers between devices, per_device(): lax.all_to_all(handed, 'seq', split_axis=0, concat_axis=0, tiled=True, ax...  10.1 us
    all_to_all x1, starting transfers between devices, per_device(): lax.all_to_all(call(functools.partial(code_kernel, depth, rows), shaped((...  8.33 us
    all_to_all x1, starting transfers between devices, per_device(): lax.all_to_all(user_part.reshape(devices, slot_count, width), 'seq', spli...  5.56 us
    pallas_call x1, Pallas kernels, per_device(): call(attend_kernel, (shaped((cands, width)), shaped((cands + slot_count,...  5.54 us
    all_to_all x1, starting transfers between devices, per_device(): lax.all_to_all(handed, 'seq', split_axis=0, concat_axis=0, tiled=True, ax...  4.89 us
    dot_general x1, matrix products, per_device(): jnp.dot(hidden, tower_out, preferred_element_type=jnp.float32)  3.29 us
    all_to_all x1, waiting for transfers between devices, per_device(): lax.all_to_all(user_part.reshape(devices, slot_count, width), 'seq', spli...  3.06 us
    pallas_call x1, Pallas kernels, per_device(): call(keep_kernel, (taken, shaped((width, width)), shaped((events, width))...  2.42 us
  transfers between devices with their start and end apart: 6, of which 2 were waited for; matrix products, arithmetic and copies ran while one was open for 11% of the time, Pallas kernels for 12%

profile of v7, /device:TPU:0, one launch (start us, length us, event | category | flops | bytes accessed | tf_op | source)
XLA Modules:
  0.0 53.3 jit_solution(7091196763458823983)
XLA Ops:
  0.6 0.0 copy-start
  0.6 0.6 %collective-permute-start = (bf16[2,1024,512]{2,1,0:T(8,128)(2,1)}, bf16[2,1024,512]{2,1,0:T(8,128)(2,1)}, u32[]{:S(2)}, u32[]{:S(2)}) collective-permute-start(bf16[2,1024,512]{2,1,0:T(8,128)(2,1)} %keys_near.1), channel_id=1, source_target_pairs={{0,1},{1,0},{2,3},{3,2},{4,5},{5,4},{6,7},{7,6},{8,9},{9,8},{10,11... | collective-permute-start | bytes 6291464 | tf_op jit(solution)/shard_map/ppermute | solution.py:337
  1.2 0.1 collective-permute-start.1
  1.3 1.5 %shard_map.122 = s32[16,1,32]{2,1,0:T(1,128)} custom-call(s32[2,1,16]{2,1,0:T(1,128)} %bitcast.13, s32[2,16]{1,0:T(2,128)} %bitcast.14), custom_call_target="tpu_custom_call" | custom-call | tf_op jit(solution)/shard_map/pallas_call | solution.py:320
  2.8 8.3 %all-to-all-start = ((s32[16,1,32]{2,1,0:T(1,128)}), s32[16,1,32]{2,1,0:T(1,128)S(1)}, u32[]{:S(2)}, u32[]{:S(2)}) async-start(s32[16,1,32]{2,1,0:T(1,128)} %shard_map.122), calls=%async_computation | async-start | bytes 16384 | tf_op jit(solution)/shard_map/all_to_all | solution.py:319
  11.1 0.0 copy-start.5
  11.1 0.0 copy-start.6
  11.1 3.3 %convolution_convert_fusion.embed_ref = bf16[128,512]{1,0:T(8,128)(2,1)S(1)} fusion(bf16[2048,512]{1,0:T(8,128)(2,1)S(1)} %copy-done, bf16[128,1024]{1,0:T(8,128)(2,1)} %param.11, bf16[1024,2048]{1,0:T(8,128)(2,1)} %param.12), kind=kOutput, calls=%fused_computation | convolution fusion | flops 806682624 | bytes 6684672 | tf_op jit(solution)/shard_map/dot_general | solution.py:343
  14.4 0.0 copy-start.2
  14.5 0.0 all-to-all-done.codes_ref
  14.5 1.1 %shard_map.124 = bf16[8,64,512]{2,1,0:T(8,128)(2,1)} custom-call(s32[16,1,32]{2,1,0:T(1,128)S(1)} %all-to-all-done.codes_ref, bf16[128,512]{1,0:T(8,128)(2,1)S(1)} %convolution_convert_fusion.embed_ref), custom_call_target="tpu_custom_call" | custom-call | tf_op jit(solution)/shard_map/pallas_call | solution.py:345
  15.6 4.9 %all-to-all-start.1 = ((bf16[8,64,512]{2,1,0:T(8,128)(2,1)}), bf16[8,64,512]{2,1,0:T(8,128)(2,1)S(1)}, u32[]{:S(2)}, u32[]{:S(2)}) async-start(bf16[8,64,512]{2,1,0:T(8,128)(2,1)} %shard_map.124), calls=%async_computation.1 | async-start | bytes 1048576 | tf_op jit(solution)/shard_map/all_to_all | solution.py:356
  20.5 1.2 %shard_map.123 = (bf16[272,512]{1,0:T(8,128)(2,1)S(1)}, bf16[272,512]{1,0:T(8,128)(2,1)S(1)}, s32[256,1]{1,0:T(8,128)S(1)}) custom-call(s32[2]{0:T(128)S(1)} %copy-done.6, s32[16,1,32]{2,1,0:T(1,128)S(1)} %all-to-all-done.codes_ref, s32[2,256]{1,0:T(2,128)S(1)} %bitcast.12), custom_call_target="tpu_custom_call" | custom-call | tf_op jit(solution)/shard_map/pallas_call | solution.py:363
  21.7 0.6 %copy-done.3 = s32[256,1]{1,0:T(8,128)} copy-done((s32[256,1]{1,0:T(8,128)}, s32[256,1]{1,0:T(8,128)S(1)}, u32[]{:S(2)}) %copy-start.3) | copy-done | bytes 1048
  22.4 10.1 %all-to-all-done.1 = bf16[8,64,512]{2,1,0:T(8,128)(2,1)S(1)} async-done(((bf16[8,64,512]{2,1,0:T(8,128)(2,1)}), bf16[8,64,512]{2,1,0:T(8,128)(2,1)S(1)}, u32[]{:S(2)}, u32[]{:S(2)}) %all-to-all-start.1) | async-done | bytes 524320 | tf_op jit(solution)/shard_map/all_to_all | solution.py:356
  32.5 0.3 shard_map.126
  32.8 0.1 collective-permute-start.2
  32.9 0.0 collective-permute-done.keys_far
  32.9 0.0 collective-permute-done.1.values_far
  33.0 2.4 %shard_map.125 = (bf16[272,512]{1,0:T(8,128)(2,1)S(1)}, bf16[512,512]{1,0:T(8,128)(2,1)S(1)}, bf16[2048,512]{1,0:T(8,128)(2,1)S(1)}, bf16[2048,512]{1,0:T(8,128)(2,1)S(1)}) custom-call(bf16[272,512]{1,0:T(8,128)(2,1)S(1)} %get-tuple-element.11.chosen_ref, bf16[512,512]{1,0:T(8,128)(2,1)S(1)} %bitcast.11, bf16[2,1024,512]{2,1,0:T(8,128)(2,1)} %keys_near.1, ...), custom_call_target="tpu_custom_call" | custom-call | tf_op jit(solution)/shard_map/pallas_call | solution.py:372
  35.4 5.5 %shard_map.127 = (bf16[256,512]{1,0:T(8,128)(2,1)}, bf16[272,512]{1,0:T(8,128)(2,1)S(1)}) custom-call(bf16[272,512]{1,0:T(8,128)(2,1)S(1)} %get-tuple-element.12.kept_ref, bf16[272,512]{1,0:T(8,128)(2,1)S(1)} %collective-permute-done.2.came_ref, bf16[512,512]{1,0:T(8,128)(2,1)S(1)} %get-tuple-element.14.weight_ref, s32[256,1]{1,0:T(8,128)S(1)} %copy-done.4, ...), custom_call_target="tpu_custom_call" | custom-call | tf_op jit(solution)/shard_map/pallas_call | solution.py:387
  41.0 0.0 copy-start.1
  41.0 5.6 %all-to-all-start.2 = ((bf16[16,16,512]{2,1,0:T(8,128)(2,1)}), bf16[16,16,512]{2,1,0:T(8,128)(2,1)S(1)}, u32[]{:S(2)}, u32[]{:S(2)}) async-start(bf16[16,16,512]{2,1,0:T(8,128)(2,1)} %bitcast.4), calls=%async_computation.2 | async-start | bytes 524288 | tf_op jit(solution)/shard_map/all_to_all | solution.py:395
  46.6 2.1 %fusion.2 = (bf16[32,2048]{1,0:T(8,128)(2,1)S(1)}, f32[32,2048]{1,0:T(8,128)S(1)}) fusion(bf16[32,512]{1,0:T(8,128)(2,1)S(1)} %maximum_select_fusion.routed_ref, bf16[512,2048]{1,0:T(8,128)(2,1)} %proj_hbm.1), kind=kOutput, calls=%fused_computation.10 | convolution fusion | flops 67436544 | bytes 2523136 | tf_op jit(solution)/shard_map/dot_general | solution.py:411
  48.7 0.1 mul.54
  48.8 0.1 reduce_sum.9
  48.9 0.1 copy.14
  49.0 0.1 copy.15
  49.0 0.1 mul.58
  49.1 0.1 mul.59
  49.3 3.1 %all-to-all-done.2.backs_ref = bf16[16,16,512]{2,1,0:T(8,128)(2,1)S(1)} async-done(((bf16[16,16,512]{2,1,0:T(8,128)(2,1)}), bf16[16,16,512]{2,1,0:T(8,128)(2,1)S(1)}, u32[]{:S(2)}, u32[]{:S(2)}) %all-to-all-start.2) | async-done | bytes 262176 | tf_op jit(solution)/shard_map/all_to_all | solution.py:395
  52.3 1.0 %shard_map.128 = bf16[16,2,512]{2,1,0:T(2,128)(2,1)} custom-call(bf16[16,16,512]{2,1,0:T(8,128)(2,1)S(1)} %all-to-all-done.2.backs_ref, f32[32,512]{1,0:T(8,128)S(1)} %convert_multiply_fusion.own_ref, f32[32,512]{1,0:T(8,128)S(1)} %slice.26.gate_ref, bf16[32,512]{1,0:T(8,128)(2,1)S(1)} %maximum_select_fusion.routed_ref, bf16[512,512]{1,0:T(8,128)(2,1)S(1)} %copy-done.1), custom_call_target="tpu_custom_call" | custom-call | tf_op jit(solution)/shard_map/pallas_call | solution.py:418
  (15 shorter events, 0.1 us)
Async XLA Ops:
  0.6 10.5 %copy-start = (bf16[2048,512]{1,0:T(8,128)(2,1)S(1)}, bf16[2048,512]{1,0:T(8,128)(2,1)}, u32[]{:S(2)}) copy-start(bf16[2048,512]{1,0:T(8,128)(2,1)} %param.13) | copy-start | bytes 6291460
  0.6 32.3 %collective-permute-start = (bf16[2,1024,512]{2,1,0:T(8,128)(2,1)}, bf16[2,1024,512]{2,1,0:T(8,128)(2,1)}, u32[]{:S(2)}, u32[]{:S(2)}) collective-permute-start(bf16[2,1024,512]{2,1,0:T(8,128)(2,1)} %keys_near.1), channel_id=1, source_target_pairs={{0,1},{1,0},{2,3},{3,2},{4,5},{5,4},{6,7},{7,6},{8,9},{9,8},{10,11... | collective-permute-start | bytes 6291464 | tf_op jit(solution)/shard_map/ppermute | solution.py:337
  1.2 31.7 %collective-permute-start.1 = (bf16[2,1024,512]{2,1,0:T(8,128)(2,1)}, bf16[2,1024,512]{2,1,0:T(8,128)(2,1)}, u32[]{:S(2)}, u32[]{:S(2)}) collective-permute-start(bf16[2,1024,512]{2,1,0:T(8,128)(2,1)} %values_near.1), channel_id=1, source_target_pairs={{0,1},{1,0},{2,3},{3,2},{4,5},{5,4},{6,7},{7,6},{8,9},{9,8},{10,11... | collective-permute-start | bytes 6291464 | tf_op jit(solution)/shard_map/ppermute | solution.py:338
  2.8 11.7 %all-to-all-start = ((s32[16,1,32]{2,1,0:T(1,128)}), s32[16,1,32]{2,1,0:T(1,128)S(1)}, u32[]{:S(2)}, u32[]{:S(2)}) async-start(s32[16,1,32]{2,1,0:T(1,128)} %shard_map.122), calls=%async_computation | async-start | bytes 16384 | tf_op jit(solution)/shard_map/all_to_all | solution.py:319
  11.1 9.4 %copy-start.5 = (s32[256,2]{0,1:T(2,128)S(1)}, s32[256,2]{0,1:T(2,128)}, u32[]{:S(2)}) copy-start(s32[256,2]{0,1:T(2,128)} %param.21) | copy-start | bytes 6148
  11.1 9.4 %copy-start.6 = (s32[2]{0:T(128)S(1)}, s32[2]{0:T(128)}, u32[]{:S(2)}) copy-start(s32[2]{0:T(128)} %lengths_ref.1) | copy-start | bytes 28
  14.4 1.2 %copy-start.2 = (bf16[128,512]{1,0:T(8,128)(2,1)}, bf16[128,512]{1,0:T(8,128)(2,1)S(1)}, u32[]{:S(2)}) copy-start(bf16[128,512]{1,0:T(8,128)(2,1)S(1)} %convolution_convert_fusion.embed_ref) | copy-start | bytes 393220
  15.6 16.9 %all-to-all-start.1 = ((bf16[8,64,512]{2,1,0:T(8,128)(2,1)}), bf16[8,64,512]{2,1,0:T(8,128)(2,1)S(1)}, u32[]{:S(2)}, u32[]{:S(2)}) async-start(bf16[8,64,512]{2,1,0:T(8,128)(2,1)} %shard_map.124), calls=%async_computation.1 | async-start | bytes 1048576 | tf_op jit(solution)/shard_map/all_to_all | solution.py:356
  21.7 0.7 %copy-start.3 = (s32[256,1]{1,0:T(8,128)}, s32[256,1]{1,0:T(8,128)S(1)}, u32[]{:S(2)}) copy-start(s32[256,1]{1,0:T(8,128)S(1)} %get-tuple-element.15.seen_ref) | copy-start | bytes 3076
  32.8 2.6 %collective-permute-start.2 = (bf16[272,512]{1,0:T(8,128)(2,1)S(1)}, bf16[272,512]{1,0:T(8,128)(2,1)S(1)}, u32[]{:S(2)}, u32[]{:S(2)}) collective-permute-start(bf16[272,512]{1,0:T(8,128)(2,1)S(1)} %shard_map.126), channel_id=1, source_target_pairs={{0,1},{1,0},{2,3},{3,2},{4,5},{5,4},{6,7},{7,6},{8,9},{9,8},{10,11... | collective-permute-start | bytes 835592 | tf_op jit(solution)/shard_map/ppermute | solution.py:371
  33.0 2.5 %copy-start.4 = (s32[256,1]{1,0:T(8,128)S(1)}, s32[256,1]{1,0:T(8,128)}, u32[]{:S(2)}) copy-start(s32[256,1]{1,0:T(8,128)} %copy-done.3) | copy-start | bytes 3076
  41.0 11.4 %copy-start.1 = (bf16[512,512]{1,0:T(8,128)(2,1)S(1)}, bf16[512,512]{1,0:T(8,128)(2,1)}, u32[]{:S(2)}) copy-start(bf16[512,512]{1,0:T(8,128)(2,1)} %weight_ref.1) | copy-start | bytes 1572868
  41.0 11.4 %all-to-all-start.2 = ((bf16[16,16,512]{2,1,0:T(8,128)(2,1)}), bf16[16,16,512]{2,1,0:T(8,128)(2,1)S(1)}, u32[]{:S(2)}, u32[]{:S(2)}) async-start(bf16[16,16,512]{2,1,0:T(8,128)(2,1)} %bitcast.4), calls=%async_computation.2 | async-start | bytes 524288 | tf_op jit(solution)/shard_map/all_to_all | solution.py:395

commit v8 on v6

--- a/solution.py
+++ b/solution.py
@@ -28,9 +28,9 @@
 
 
 def ring_order(chips):
-    ring = list(range(1, chips, 2)) + list(range(0, chips, 2))[::-1]
-    start = ring.index(min(chips - 1, (chips // 2) | 1))
-    return ring[start:] + ring[:start]
+    half = chips // 2
+    ring = list(range(1, half, 2)) + list(range(0, half, 2))[::-1]
+    return [half + chip for chip in ring] + ring[:1] + ring[:0:-1] + list(range(2 * half, chips))
 
 
 def middle_order(chips):

time: 54.1 us -> 54.1 us (level)
  no operation moved by 1% of the time
where the time goes in v8:
time: 54.1 us; the launch traced here: 53.3 us
  starting transfers between devices  19.5 us (36%)
  waiting for transfers between devices  13.2 us (24%)
  Pallas kernels  13.1 us (24%)
  matrix products  5.38 us (10%)
  local copies, waits for them, and re-layouts  1.13 us (2%)
  between operations  0.93 us (2%)
    all_to_all x1, waiting for transfers between devices, per_device(): lax.all_to_all(handed, 'seq', split_axis=0, concat_axis=0, tiled=True, ax...  10.1 us
    all_to_all x1, starting transfers between devices, per_device(): lax.all_to_all(call(functools.partial(code_kernel, depth, rows), shaped((...  8.33 us
    all_to_all x1, starting transfers between devices, per_device(): lax.all_to_all(user_part.reshape(devices, slot_count, width), 'seq', spli...  5.56 us
    pallas_call x1, Pallas kernels, per_device(): call(attend_kernel, (shaped((cands, width)), shaped((cands + slot_count,...  5.54 us
    all_to_all x1, starting transfers between devices, per_device(): lax.all_to_all(handed, 'seq', split_axis=0, concat_axis=0, tiled=True, ax...  4.9 us
    dot_general x1, matrix products, per_device(): jnp.dot(hidden, tower_out, preferred_element_type=jnp.float32)  3.29 us
    all_to_all x1, waiting for transfers between devices, per_device(): lax.all_to_all(user_part.reshape(devices, slot_count, width), 'seq', spli...  3.06 us
    pallas_call x1, Pallas kernels, per_device(): call(keep_kernel, (taken, shaped((width, width)), shaped((events, width))...  2.42 us
  transfers between devices with their start and end apart: 6, of which 2 were waited for; matrix products, arithmetic and copies ran while one was open for 11% of the time, Pallas kernels for 12%

profile of v8, /device:TPU:0, one launch (start us, length us, event | category | flops | bytes accessed | tf_op | source)
XLA Modules:
  0.0 53.3 jit_solution(8296466268749227411)
XLA Ops:
  0.6 0.0 copy-start
  0.6 0.6 %collective-permute-start = (bf16[2,1024,512]{2,1,0:T(8,128)(2,1)}, bf16[2,1024,512]{2,1,0:T(8,128)(2,1)}, u32[]{:S(2)}, u32[]{:S(2)}) collective-permute-start(bf16[2,1024,512]{2,1,0:T(8,128)(2,1)} %keys_near.1), channel_id=1, source_target_pairs={{0,1},{1,0},{2,3},{3,2},{4,5},{5,4},{6,7},{7,6},{8,9},{9,8},{10,11... | collective-permute-start | bytes 6291464 | tf_op jit(solution)/shard_map/ppermute | solution.py:335
  1.2 0.1 collective-permute-start.1
  1.3 1.5 %shard_map.122 = s32[16,1,32]{2,1,0:T(1,128)} custom-call(s32[2,1,16]{2,1,0:T(1,128)} %bitcast.13, s32[2,16]{1,0:T(2,128)} %bitcast.14), custom_call_target="tpu_custom_call" | custom-call | tf_op jit(solution)/shard_map/pallas_call | solution.py:318
  2.8 8.3 %all-to-all-start = ((s32[16,1,32]{2,1,0:T(1,128)}), s32[16,1,32]{2,1,0:T(1,128)S(1)}, u32[]{:S(2)}, u32[]{:S(2)}) async-start(s32[16,1,32]{2,1,0:T(1,128)} %shard_map.122), calls=%async_computation | async-start | bytes 16384 | tf_op jit(solution)/shard_map/all_to_all | solution.py:317
  11.1 0.0 copy-start.5
  11.1 0.0 copy-start.6
  11.1 3.3 %convolution_convert_fusion.embed_ref = bf16[128,512]{1,0:T(8,128)(2,1)S(1)} fusion(bf16[2048,512]{1,0:T(8,128)(2,1)S(1)} %copy-done, bf16[128,1024]{1,0:T(8,128)(2,1)} %param.11, bf16[1024,2048]{1,0:T(8,128)(2,1)} %param.12), kind=kOutput, calls=%fused_computation | convolution fusion | flops 806682624 | bytes 6684672 | tf_op jit(solution)/shard_map/dot_general | solution.py:341
  14.4 0.0 copy-start.2
  14.5 0.0 all-to-all-done.codes_ref
  14.5 1.1 %shard_map.124 = bf16[8,64,512]{2,1,0:T(8,128)(2,1)} custom-call(s32[16,1,32]{2,1,0:T(1,128)S(1)} %all-to-all-done.codes_ref, bf16[128,512]{1,0:T(8,128)(2,1)S(1)} %convolution_convert_fusion.embed_ref), custom_call_target="tpu_custom_call" | custom-call | tf_op jit(solution)/shard_map/pallas_call | solution.py:343
  15.6 4.9 %all-to-all-start.1 = ((bf16[8,64,512]{2,1,0:T(8,128)(2,1)}), bf16[8,64,512]{2,1,0:T(8,128)(2,1)S(1)}, u32[]{:S(2)}, u32[]{:S(2)}) async-start(bf16[8,64,512]{2,1,0:T(8,128)(2,1)} %shard_map.124), calls=%async_computation.1 | async-start | bytes 1048576 | tf_op jit(solution)/shard_map/all_to_all | solution.py:354
  20.5 1.2 %shard_map.123 = (bf16[272,512]{1,0:T(8,128)(2,1)S(1)}, bf16[272,512]{1,0:T(8,128)(2,1)S(1)}, s32[256,1]{1,0:T(8,128)S(1)}) custom-call(s32[2]{0:T(128)S(1)} %copy-done.6, s32[16,1,32]{2,1,0:T(1,128)S(1)} %all-to-all-done.codes_ref, s32[2,256]{1,0:T(2,128)S(1)} %bitcast.12), custom_call_target="tpu_custom_call" | custom-call | tf_op jit(solution)/shard_map/pallas_call | solution.py:361
  21.7 0.6 %copy-done.3 = s32[256,1]{1,0:T(8,128)} copy-done((s32[256,1]{1,0:T(8,128)}, s32[256,1]{1,0:T(8,128)S(1)}, u32[]{:S(2)}) %copy-start.3) | copy-done | bytes 1048
  22.4 10.1 %all-to-all-done.1 = bf16[8,64,512]{2,1,0:T(8,128)(2,1)S(1)} async-done(((bf16[8,64,512]{2,1,0:T(8,128)(2,1)}), bf16[8,64,512]{2,1,0:T(8,128)(2,1)S(1)}, u32[]{:S(2)}, u32[]{:S(2)}) %all-to-all-start.1) | async-done | bytes 524320 | tf_op jit(solution)/shard_map/all_to_all | solution.py:354
  32.5 0.3 shard_map.126
  32.8 0.1 collective-permute-start.2
  32.9 0.0 collective-permute-done.keys_far
  32.9 0.0 collective-permute-done.1.values_far
  33.0 2.4 %shard_map.125 = (bf16[272,512]{1,0:T(8,128)(2,1)S(1)}, bf16[512,512]{1,0:T(8,128)(2,1)S(1)}, bf16[2048,512]{1,0:T(8,128)(2,1)S(1)}, bf16[2048,512]{1,0:T(8,128)(2,1)S(1)}) custom-call(bf16[272,512]{1,0:T(8,128)(2,1)S(1)} %get-tuple-element.11.chosen_ref, bf16[512,512]{1,0:T(8,128)(2,1)S(1)} %bitcast.11, bf16[2,1024,512]{2,1,0:T(8,128)(2,1)} %keys_near.1, ...), custom_call_target="tpu_custom_call" | custom-call | tf_op jit(solution)/shard_map/pallas_call | solution.py:370
  35.4 5.5 %shard_map.127 = (bf16[256,512]{1,0:T(8,128)(2,1)}, bf16[272,512]{1,0:T(8,128)(2,1)S(1)}) custom-call(bf16[272,512]{1,0:T(8,128)(2,1)S(1)} %get-tuple-element.12.kept_ref, bf16[272,512]{1,0:T(8,128)(2,1)S(1)} %collective-permute-done.2.came_ref, bf16[512,512]{1,0:T(8,128)(2,1)S(1)} %get-tuple-element.14.weight_ref, s32[256,1]{1,0:T(8,128)S(1)} %copy-done.4, ...), custom_call_target="tpu_custom_call" | custom-call | tf_op jit(solution)/shard_map/pallas_call | solution.py:385
  41.0 0.0 copy-start.1
  41.0 5.6 %all-to-all-start.2 = ((bf16[16,16,512]{2,1,0:T(8,128)(2,1)}), bf16[16,16,512]{2,1,0:T(8,128)(2,1)S(1)}, u32[]{:S(2)}, u32[]{:S(2)}) async-start(bf16[16,16,512]{2,1,0:T(8,128)(2,1)} %bitcast.4), calls=%async_computation.2 | async-start | bytes 524288 | tf_op jit(solution)/shard_map/all_to_all | solution.py:393
  46.6 2.1 %fusion.2 = (bf16[32,2048]{1,0:T(8,128)(2,1)S(1)}, f32[32,2048]{1,0:T(8,128)S(1)}) fusion(bf16[32,512]{1,0:T(8,128)(2,1)S(1)} %maximum_select_fusion.routed_ref, bf16[512,2048]{1,0:T(8,128)(2,1)} %proj_hbm.1), kind=kOutput, calls=%fused_computation.10 | convolution fusion | flops 67436544 | bytes 2523136 | tf_op jit(solution)/shard_map/dot_general | solution.py:409
  48.7 0.1 mul.54
  48.8 0.1 reduce_sum.9
  48.9 0.1 copy.14
  48.9 0.1 copy.15
  49.0 0.1 mul.58
  49.1 0.1 mul.59
  49.3 3.1 %all-to-all-done.2.backs_ref = bf16[16,16,512]{2,1,0:T(8,128)(2,1)S(1)} async-done(((bf16[16,16,512]{2,1,0:T(8,128)(2,1)}), bf16[16,16,512]{2,1,0:T(8,128)(2,1)S(1)}, u32[]{:S(2)}, u32[]{:S(2)}) %all-to-all-start.2) | async-done | bytes 262176 | tf_op jit(solution)/shard_map/all_to_all | solution.py:393
  52.3 1.0 %shard_map.128 = bf16[16,2,512]{2,1,0:T(2,128)(2,1)} custom-call(bf16[16,16,512]{2,1,0:T(8,128)(2,1)S(1)} %all-to-all-done.2.backs_ref, f32[32,512]{1,0:T(8,128)S(1)} %convert_multiply_fusion.own_ref, f32[32,512]{1,0:T(8,128)S(1)} %slice.26.gate_ref, bf16[32,512]{1,0:T(8,128)(2,1)S(1)} %maximum_select_fusion.routed_ref, bf16[512,512]{1,0:T(8,128)(2,1)S(1)} %copy-done.1), custom_call_target="tpu_custom_call" | custom-call | tf_op jit(solution)/shard_map/pallas_call | solution.py:416
  (15 shorter events, 0.1 us)
Async XLA Ops:
  0.6 10.5 %copy-start = (bf16[2048,512]{1,0:T(8,128)(2,1)S(1)}, bf16[2048,512]{1,0:T(8,128)(2,1)}, u32[]{:S(2)}) copy-start(bf16[2048,512]{1,0:T(8,128)(2,1)} %param.13) | copy-start | bytes 6291460
  0.6 32.3 %collective-permute-start = (bf16[2,1024,512]{2,1,0:T(8,128)(2,1)}, bf16[2,1024,512]{2,1,0:T(8,128)(2,1)}, u32[]{:S(2)}, u32[]{:S(2)}) collective-permute-start(bf16[2,1024,512]{2,1,0:T(8,128)(2,1)} %keys_near.1), channel_id=1, source_target_pairs={{0,1},{1,0},{2,3},{3,2},{4,5},{5,4},{6,7},{7,6},{8,9},{9,8},{10,11... | collective-permute-start | bytes 6291464 | tf_op jit(solution)/shard_map/ppermute | solution.py:335
  1.2 31.7 %collective-permute-start.1 = (bf16[2,1024,512]{2,1,0:T(8,128)(2,1)}, bf16[2,1024,512]{2,1,0:T(8,128)(2,1)}, u32[]{:S(2)}, u32[]{:S(2)}) collective-permute-start(bf16[2,1024,512]{2,1,0:T(8,128)(2,1)} %values_near.1), channel_id=1, source_target_pairs={{0,1},{1,0},{2,3},{3,2},{4,5},{5,4},{6,7},{7,6},{8,9},{9,8},{10,11... | collective-permute-start | bytes 6291464 | tf_op jit(solution)/shard_map/ppermute | solution.py:336
  2.8 11.7 %all-to-all-start = ((s32[16,1,32]{2,1,0:T(1,128)}), s32[16,1,32]{2,1,0:T(1,128)S(1)}, u32[]{:S(2)}, u32[]{:S(2)}) async-start(s32[16,1,32]{2,1,0:T(1,128)} %shard_map.122), calls=%async_computation | async-start | bytes 16384 | tf_op jit(solution)/shard_map/all_to_all | solution.py:317
  11.1 9.4 %copy-start.5 = (s32[256,2]{0,1:T(2,128)S(1)}, s32[256,2]{0,1:T(2,128)}, u32[]{:S(2)}) copy-start(s32[256,2]{0,1:T(2,128)} %param.21) | copy-start | bytes 6148
  11.1 9.4 %copy-start.6 = (s32[2]{0:T(128)S(1)}, s32[2]{0:T(128)}, u32[]{:S(2)}) copy-start(s32[2]{0:T(128)} %lengths_ref.1) | copy-start | bytes 28
  14.4 1.2 %copy-start.2 = (bf16[128,512]{1,0:T(8,128)(2,1)}, bf16[128,512]{1,0:T(8,128)(2,1)S(1)}, u32[]{:S(2)}) copy-start(bf16[128,512]{1,0:T(8,128)(2,1)S(1)} %convolution_convert_fusion.embed_ref) | copy-start | bytes 393220
  15.6 16.9 %all-to-all-start.1 = ((bf16[8,64,512]{2,1,0:T(8,128)(2,1)}), bf16[8,64,512]{2,1,0:T(8,128)(2,1)S(1)}, u32[]{:S(2)}, u32[]{:S(2)}) async-start(bf16[8,64,512]{2,1,0:T(8,128)(2,1)} %shard_map.124), calls=%async_computation.1 | async-start | bytes 1048576 | tf_op jit(solution)/shard_map/all_to_all | solution.py:354
  21.7 0.7 %copy-start.3 = (s32[256,1]{1,0:T(8,128)}, s32[256,1]{1,0:T(8,128)S(1)}, u32[]{:S(2)}) copy-start(s32[256,1]{1,0:T(8,128)S(1)} %get-tuple-element.15.seen_ref) | copy-start | bytes 3076
  32.8 2.6 %collective-permute-start.2 = (bf16[272,512]{1,0:T(8,128)(2,1)S(1)}, bf16[272,512]{1,0:T(8,128)(2,1)S(1)}, u32[]{:S(2)}, u32[]{:S(2)}) collective-permute-start(bf16[272,512]{1,0:T(8,128)(2,1)S(1)} %shard_map.126), channel_id=1, source_target_pairs={{0,1},{1,0},{2,3},{3,2},{4,5},{5,4},{6,7},{7,6},{8,9},{9,8},{10,11... | collective-permute-start | bytes 835592 | tf_op jit(solution)/shard_map/ppermute | solution.py:369
  32.9 2.5 %copy-start.4 = (s32[256,1]{1,0:T(8,128)S(1)}, s32[256,1]{1,0:T(8,128)}, u32[]{:S(2)}) copy-start(s32[256,1]{1,0:T(8,128)} %copy-done.3) | copy-start | bytes 3076
  41.0 11.4 %copy-start.1 = (bf16[512,512]{1,0:T(8,128)(2,1)S(1)}, bf16[512,512]{1,0:T(8,128)(2,1)}, u32[]{:S(2)}) copy-start(bf16[512,512]{1,0:T(8,128)(2,1)} %weight_ref.1) | copy-start | bytes 1572868
  41.0 11.4 %all-to-all-start.2 = ((bf16[16,16,512]{2,1,0:T(8,128)(2,1)}), bf16[16,16,512]{2,1,0:T(8,128)(2,1)S(1)}, u32[]{:S(2)}, u32[]{:S(2)}) async-start(bf16[16,16,512]{2,1,0:T(8,128)(2,1)} %bitcast.4), calls=%async_computation.2 | async-start | bytes 524288 | tf_op jit(solution)/shard_map/all_to_all | solution.py:393
